TPU v7x, 512 devices: a whole 4x4x16 slice. The times are simulated.
512 devices in a mesh: seq: 64 (over y, z), tp: 8 (over x, core).
Axes of the slice: x: 4, y: 4, z: 16, core: 2. Of those that a mesh axis runs over, the one named last changes fastest.
Arguments:
- crop_features: bfloat16 [192, 21, 21, 1536], P('seq'), may hold values from -45 to 45
- crop_counts: int32 [64], replicated, may hold values from 1 to 3, as said below
- first_crop: int32 [64], replicated, may hold values from 0 to 127, as said below
- tile_embed: bfloat16 [3, 1536], replicated, may hold values from -3 to 3
- dw_weight: bfloat16 [49, 1536], replicated, may hold values from -0.875 to 0.875
- conv_bias: bfloat16 [1536], replicated, may hold values from -3 to 3
- ln_gain: bfloat16 [1536], replicated, may hold values from 0.099609375 to 1.8984375
- ln_bias: bfloat16 [1536], replicated, may hold values from -2 to 2
- w_up: bfloat16 [1536, 6144], P('seq', 'tp'), may hold values from -0.15625 to 0.15625
- b_up: bfloat16 [6144], P('tp'), may hold values from -3 to 3
- w_down: bfloat16 [6144, 1536], P('tp', 'seq'), may hold values from -0.078125 to 0.078125
- b_down: bfloat16 [1536], P('tp'), may hold values from -2 to 2
- gamma: float32 [1536], P('tp'), may hold values from 0.5 to 2
Outputs:
- visual_rows: bfloat16 [128, 21, 21, 1536], P('seq', None, None, 'tp')
Inputs may be any that keep to these rules, and one draw needn't show every extreme that they name: `crop_counts`: the counts sum to 128; 3 is reached in every draw. first_crop[0] is 0 and the entries never fall; device d holds first_crop[d+1] - first_crop[d] crops (the last device 128 - first_crop[last]), at most 3, and some device holds exactly 3; |first_crop[d] - d * 2| <= 1.
All inputs are finite; a program needn't handle non-finite values.
Results may differ from a plain program's by a relative error of at most 0.009.
Values may be sent and summed in bfloat16 or wider, within the bound.
No kernel may reach another device: no remote copies, remote signals or barrier semaphores. Data moves between devices by JAX's collectives and lax.ppermute only.
A program may use at most 128 MiB of HBM per device.

v0:
```python
import jax
import jax.numpy as jnp
from jax import lax
from jax.sharding import PartitionSpec as P

CROPS_DEV = 2


def from_behind(block, axis, distance):
    devices = range(lax.axis_size(axis))
    route = [(i - distance, i) for i in devices if i - distance in devices]
    return lax.ppermute(block, axis, route)


def regroup(slot_data, seq_index, first_held, held_limit, per_dev):

    def outgoing(offset_dev):
        target = (seq_index + offset_dev) * per_dev + jnp.arange(per_dev, dtype=jnp.int32)
        slot_idx = jnp.clip(target - first_held, 0, slot_data.shape[0] - 1)
        is_valid = (target >= first_held) & (target < held_limit)
        picked = jnp.take(slot_data, slot_idx, axis=0)
        return jnp.where(is_valid[:, None, None, None], picked, jnp.zeros_like(picked))

    result = outgoing(0)
    for offset_dev in (1, -1):
        result = result + from_behind(outgoing(offset_dev), "seq", offset_dev)
    return result


def encode(
    block_data,
    crop_ids,
    crop_counts,
    tile_embed,
    dw_weight,
    conv_bias,
    ln_gain,
    ln_bias,
    w_up,
    b_up,
    w_down,
    b_down,
    gamma,
):
    crop_number = block_data.shape[0]
    grid_size = block_data.shape[1]
    channels = block_data.shape[3]
    kernel_side = 7
    image_start = jnp.cumsum(crop_counts) - crop_counts
    image_begin = jnp.max(
        jnp.where(image_start[None, :] <= crop_ids[:, None], image_start[None, :], 0), axis=1
    )
    place_ids = crop_ids - image_begin
    choose = (
        place_ids[:, None] == jnp.arange(tile_embed.shape[0], dtype=jnp.int32)[None, :]
    ).astype(jnp.float32)
    tile_rows = jnp.sum(choose[:, :, None] * tile_embed.astype(jnp.float32)[None, :, :], axis=1)
    block_in = block_data.astype(jnp.float32) + tile_rows[:, None, None, :]
    padded = jnp.pad(block_in, ((0, 0), (3, 3), (3, 3), (0, 0)))
    conv_sum = jnp.zeros_like(block_in)
    for row_shift in range(kernel_side):
        for col_shift in range(kernel_side):
            conv_sum = conv_sum + padded[
                :, row_shift : row_shift + grid_size, col_shift : col_shift + grid_size, :
            ] * dw_weight[row_shift * kernel_side + col_shift].astype(jnp.float32)
    cell_rows = crop_number * grid_size * grid_size
    conv_out = (conv_sum + conv_bias.astype(jnp.float32)).reshape(cell_rows, channels)
    ln_mean = jnp.mean(conv_out, axis=1, keepdims=True)
    ln_var = jnp.mean((conv_out - ln_mean) ** 2, axis=1, keepdims=True)
    normed = (
        (conv_out - ln_mean) / jnp.sqrt(ln_var + 1e-06) * ln_gain.astype(jnp.float32)
        + ln_bias.astype(jnp.float32)
    ).astype(jnp.bfloat16)
    up_whole, down_whole = (
        lax.all_gather(w_up, "seq", axis=0, tiled=True),
        lax.all_gather(w_down, "seq", axis=1, tiled=True),
    )
    pre_act = jnp.dot(normed, up_whole, preferred_element_type=jnp.float32)
    hidden = jax.nn.gelu(pre_act + b_up.astype(jnp.float32), approximate=False).astype(jnp.bfloat16)
    partial_value = jnp.dot(hidden, down_whole, preferred_element_type=jnp.float32)
    summed = lax.psum_scatter(
        partial_value.astype(jnp.bfloat16), "tp", scatter_dimension=1, tiled=True
    ).astype(jnp.float32)
    out_width = b_down.shape[0]
    offset = lax.axis_index("tp") * out_width
    residual = lax.dynamic_slice_in_dim(block_in.reshape(cell_rows, channels), offset, out_width, 1)
    result = residual + gamma * (summed + b_down.astype(jnp.float32))
    return result.astype(jnp.bfloat16).reshape(crop_number, grid_size, grid_size, out_width)


def per_device(
    crop_features,
    crop_counts,
    first_crop,
    tile_embed,
    dw_weight,
    conv_bias,
    ln_gain,
    ln_bias,
    w_up,
    b_up,
    w_down,
    b_down,
    gamma,
):
    seq_count = lax.axis_size("seq")
    seq_index = lax.axis_index("seq")
    per_dev = CROPS_DEV
    slot_count = crop_features.shape[0]
    crop_total = per_dev * seq_count
    first_held = lax.dynamic_index_in_dim(first_crop, seq_index, 0, keepdims=False)
    next_first = lax.dynamic_index_in_dim(
        first_crop, jnp.minimum(seq_index + 1, seq_count - 1), 0, keepdims=False
    )
    held_limit = jnp.where(seq_index + 1 < seq_count, next_first, crop_total)
    held_ids = first_held + jnp.arange(slot_count, dtype=jnp.int32)
    encoded = encode(
        crop_features,
        held_ids,
        crop_counts,
        tile_embed,
        dw_weight,
        conv_bias,
        ln_gain,
        ln_bias,
        w_up,
        b_up,
        w_down,
        b_down,
        gamma,
    )
    visual_rows = regroup(encoded, seq_index, first_held, held_limit, per_dev)
    return visual_rows


def solution(mesh):
    placed = (
        P("seq", None, None, None),
        P(),
        P(),
        P(),
        P(),
        P(),
        P(),
        P(),
        P("seq", "tp"),
        P("tp"),
        P("tp", "seq"),
        P("tp"),
        P("tp"),
    )
    return jax.shard_map(
        per_device,
        mesh=mesh,
        in_specs=placed,
        out_specs=P("seq", None, None, "tp"),
        check_vma=False,
    )
```

profile of v0, /device:TPU:25, one launch (start us, length us, event | category | flops | bytes accessed | tf_op | source)
XLA Modules:
  0.0 387.3 jit_solution(10020580241406690454)
XLA Ops:
  6.5 0.7 all-gather.5.cloned.1.call-update
  7.3 0.7 all-gather.3.cloned.1.call-update
  8.1 1.2 convert_reduce_fusion.46
  9.3 1.6 convert_reduce_fusion.48
  10.9 1.6 convert_reduce_fusion.47
  12.5 0.7 convert_element_type.537
  13.2 0.7 copy.20
  14.8 1.3 fusion.144
  17.5 0.7 convert_element_type.636
  18.3 7.2 %convert_add_fusion = f32[3,21,21,1536]{3,2,1,0:T(8,128)} fusion(bf16[3,21,21,1536]{3,2,1,0:T(8,128)(2,1)} %param.15, f32[3,1536]{1,0:T(4,128)S(1)} %multiply_reduce_fusion.1), kind=kLoop, calls=%fused_computation.149 | loop fusion | flops 4064256 | bytes 12211200 | tf_op jit(solution)/shard_map/add | solution.py:58
  25.5 179.8 %fusion.142 = (f32[3,21,21]{2,1,0:T(8,128)S(1)}, f32[3,21,21,1536]{3,2,1,0:T(8,128)}) fusion(f32[1536]{0:T(1024)S(1)} %convert_element_type.636, f32[1536]{0:T(1024)S(1)} %get-tuple-element.53, f32[1536]{0:T(1024)S(1)} %get-tuple-element.54, f32[1536]{0:T(1024)S(1)} %get-tuple-element.7, f32[1536]{0:T(1024)S(1)} %get-tuple-element.8, ...), kind=kLoop, calls=%fused_computation.281 | loop fusion | flops 201179344 | bytes 16569516 | tf_op jit(solution)/shard_map/reduce_sum | solution.py:68
  205.3 9.4 %reshape.478 = f32[1323,1536]{1,0:T(8,128)} reshape(f32[3,21,21,1536]{3,2,1,0:T(8,128)} %get-tuple-element.62) | data formatting | bytes 16257024 | tf_op jit(solution)/shard_map/reshape | solution.py:67
  215.0 4.8 %multiply_reduce_fusion = f32[3,21,21]{2,1,0:T(8,128)S(1)} fusion(f32[3,21,21,1536]{3,2,1,0:T(8,128)} %get-tuple-element.62, f32[3,21,21]{2,1,0:T(8,128)S(1)} %broadcast_multiply_fusion), kind=kLoop, calls=%fused_computation.148 | loop fusion | flops 6095061 | bytes 8139096 | tf_op jit(solution)/shard_map/reduce_sum | solution.py:69
  220.0 66.1 %all-gather.3.cloned.1.call-done = bf16[1536,768]{1,0:T(8,128)(2,1)} async-done(((bf16[24,768]{1,0:T(8,128)(2,1)}), bf16[1536,768]{1,0:T(8,128)(2,1)}) %all-gather.3.cloned.1.call-update) | async-done | bytes 2359312 | tf_op jit(solution)/shard_map/all_gather | solution.py:75
  286.0 21.7 %convolution_convert_fusion = bf16[1323,1536]{0,1:T(8,128)(2,1)} fusion(bf16[768,1536]{0,1:T(8,128)(2,1)} %all-gather.5.cloned.1.call-done, bf16[1536,768]{1,0:T(8,128)(2,1)} %all-gather.3.cloned.1.call-done, f32[1323,1536]{1,0:T(8,128)} %reshape.478, f32[1536]{0:T(1024)S(1)} %convert_element_type.638, f32[1536]{0:T(1024)S(1)} %convert_element_type.637, ...), kind=kOutput, calls=%fused_computation.151 | convolution fusion | flops 6321950208 | bytes 16937304 | tf_op jit(solution)/shard_map/dot_general | solution.py:80
  307.7 9.4 %reshape.477 = f32[1323,1536]{1,0:T(8,128)} reshape(f32[3,21,21,1536]{3,2,1,0:T(8,128)} %convert_add_fusion) | data formatting | bytes 16257024 | tf_op jit(solution)/shard_map/reshape | solution.py:86
  317.1 2.0 constant_dynamic-slice_fusion
  321.9 34.8 %reduce-scatter.2.cloned.1.call-done = bf16[1323,192]{0,1:T(8,128)(2,1)} async-done(((bf16[1323,1536]{0,1:T(8,128)(2,1)}), bf16[1323,192]{0,1:T(8,128)(2,1)}) %reduce-scatter.2.cloned.1.call-update) | async-done | bytes 508048 | tf_op jit(solution)/shard_map/reduce_scatter | solution.py:81
  356.7 1.4 add_convert_fusion.6
  359.4 6.0 %collective-permute-start.1 = (bf16[2,21,21,192]{3,2,1,0:T(8,128)(2,1)S(1)}, bf16[2,21,21,192]{3,2,1,0:T(8,128)(2,1)S(1)}, u32[]{:S(2)}, u32[]{:S(2)}) collective-permute-start(bf16[2,21,21,192]{3,2,1,0:T(8,128)(2,1)S(1)} %select_select_fusion), channel_id=1, source_target_pairs={{8,0},{16,8},{24,16},{32,24},{40,32},{48,40},{56,48},{64,56},{72,6... | collective-permute-start | bytes 1016072 | tf_op jit(solution)/shard_map/ppermute | solution.py:12
  366.1 1.9 collective-permute-start
  369.2 3.6 collective-permute-done.1
  372.9 6.7 %collective-permute-done = bf16[2,21,21,192]{3,2,1,0:T(8,128)(2,1)S(1)} collective-permute-done((bf16[2,21,21,192]{3,2,1,0:T(8,128)(2,1)S(1)}, bf16[2,21,21,192]{3,2,1,0:T(8,128)(2,1)S(1)}, u32[]{:S(2)}, u32[]{:S(2)}) %collective-permute-start) | collective-permute-done | bytes 338720 | tf_op jit(solution)/shard_map/ppermute | solution.py:12
  379.7 1.1 copy.23
  (47 shorter events, 8.2 us)
Async XLA Ops:
  6.5 213.4 %all-gather.5.cloned.1.call-start = ((), (), s32[]{:S(2)}) async-start(), calls=%async_computation.2 | async-start | bytes 2396160 | tf_op jit(solution)/shard_map/all_gather | solution.py:76
  7.3 278.7 %all-gather.3.cloned.1.call-start = ((), (), s32[]{:S(2)}) async-start(), calls=%async_computation.1 | async-start | bytes 2396160 | tf_op jit(solution)/shard_map/all_gather | solution.py:75
  8.0 348.7 %reduce-scatter.2.cloned.1.call-start = ((), (), s32[]{:S(2)}) async-start(), calls=%async_computation.3 | async-start | bytes 4866048 | tf_op jit(solution)/shard_map/reduce_scatter | solution.py:81
  205.3 9.5 %copy-start = (bf16[1536]{0:T(1024)(128)(2,1)S(1)}, bf16[1536]{0:T(1024)(128)(2,1)}, u32[]{:S(2)}) copy-start(bf16[1536]{0:T(1024)(128)(2,1)} %param.22) | copy-start | bytes 9220
  205.3 9.5 %copy-start.1 = (bf16[1536]{0:T(1024)(128)(2,1)S(1)}, bf16[1536]{0:T(1024)(128)(2,1)}, u32[]{:S(2)}) copy-start(bf16[1536]{0:T(1024)(128)(2,1)} %param.21) | copy-start | bytes 9220
  205.3 14.6 %copy-start.2 = (bf16[768]{0:T(1024)(128)(2,1)S(1)}, bf16[768]{0:T(1024)(128)(2,1)}, u32[]{:S(2)}) copy-start(bf16[768]{0:T(1024)(128)(2,1)} %param.24) | copy-start | bytes 4612
  307.7 11.8 %copy-start.4 = (bf16[192]{0:T(256)(128)(2,1)S(1)}, bf16[192]{0:T(256)(128)(2,1)}, u32[]{:S(2)}) copy-start(bf16[192]{0:T(256)(128)(2,1)} %param.26) | copy-start | bytes 1156
  307.7 49.0 %copy-start.3 = (f32[192]{0:T(256)S(1)}, f32[192]{0:T(256)}, u32[]{:S(2)}) copy-start(f32[192]{0:T(256)} %param.27) | copy-start | bytes 2308
  359.4 13.4 %collective-permute-start.1 = (bf16[2,21,21,192]{3,2,1,0:T(8,128)(2,1)S(1)}, bf16[2,21,21,192]{3,2,1,0:T(8,128)(2,1)S(1)}, u32[]{:S(2)}, u32[]{:S(2)}) collective-permute-start(bf16[2,21,21,192]{3,2,1,0:T(8,128)(2,1)S(1)} %select_select_fusion), channel_id=1, source_target_pairs={{8,0},{16,8},{24,16},{32,24},{40,32},{48,40},{56,48},{64,56},{72,6... | collective-permute-start | bytes 1016072 | tf_op jit(solution)/shard_map/ppermute | solution.py:12
  366.1 13.4 %collective-permute-start = (bf16[2,21,21,192]{3,2,1,0:T(8,128)(2,1)S(1)}, bf16[2,21,21,192]{3,2,1,0:T(8,128)(2,1)S(1)}, u32[]{:S(2)}, u32[]{:S(2)}) collective-permute-start(bf16[2,21,21,192]{3,2,1,0:T(8,128)(2,1)S(1)} %select_select_fusion.1), channel_id=1, source_target_pairs={{0,8},{8,16},{16,24},{24,32},{32,40},{40,48},{48,56},{56,64},{64,7... | collective-permute-start | bytes 1016072 | tf_op jit(solution)/shard_map/ppermute | solution.py:12
Sparse Core Ops, SparseCore 0:
  10.3 135.4 all-gather.4
  148.8 137.1 all-gather.2
  307.8 48.8 reduce-scatter.1
where the time goes:
time: 393 us; the launch traced here: 387 us
  other arithmetic  204 us (52%)
  waiting for transfers between devices  113 us (29%)
  local copies, waits for them, and re-layouts  27 us (7%)
  matrix products  21.7 us (6%)
  between operations  14.1 us (4%)
  starting transfers between devices  7.98 us (2%)
    reduce_sum x1, other arithmetic, encode(): ln_mean = jnp.mean(conv_out, axis=1, keepdims=True)  180 us
    all_gather x1, waiting for transfers between devices, encode(): lax.all_gather(w_up, 'seq', axis=0, tiled=True)  66.1 us
    reduce_scatter x1, waiting for transfers between devices, encode(): lax.psum_scatter(partial_value.astype(jnp.bfloat16), 'tp', scatter_dimens...  34.8 us
    dot_general x1, matrix products, encode(): jnp.dot(hidden, down_whole, preferred_element_type=jnp.float32)  21.7 us
    ppermute x2, waiting for transfers between devices, from_behind(): return lax.ppermute(block, axis, route)  10.3 us
    reshape x1, local copies, waits for them, and re-layouts, encode(): (conv_sum + conv_bias.astype(jnp.float32)).reshape(cell_rows, channels)  9.44 us
    reshape x1, local copies, waits for them, and re-layouts, encode(): block_in.reshape(cell_rows, channels)  9.35 us
    ppermute x2, starting transfers between devices, from_behind(): return lax.ppermute(block, axis, route)  7.9 us
  transfers between devices with their start and end apart: 5, of which 4 were waited for; matrix products, arithmetic and copies ran while one was open for 59% of the time, Pallas kernels for 0%

commit v1 on v0

v1 whole, which is shorter than its diff:
```python
import jax
import jax.numpy as jnp
from jax import lax
from jax.sharding import Mesh, PartitionSpec as P

NY, NZ, NX, NCORE = 4, 16, 4, 2
SEQ = ("y", "z")
TP = ("x", "core")
PER_DEV = 2
KSIDE = 7


def shift(block, axis, distance, size):
    return lax.ppermute(block, axis, [(i, (i + distance) % size) for i in range(size)])


def gather_weights(w_up, w_down):
    both = jnp.stack([w_up, w_down.T])
    over_y = lax.all_gather(both, "y", axis=1)
    over_z = lax.all_gather(over_y, "z", axis=2)
    return over_z.reshape(2, NY * NZ * w_up.shape[0], w_up.shape[1])


def regroup(slots, seq_index, first_crop):
    count = NY * NZ
    first = first_crop[seq_index]
    limit = jnp.where(
        seq_index + 1 < count, first_crop[jnp.minimum(seq_index + 1, count - 1)], PER_DEV * count
    )
    last_slot = slots.shape[0] - 1

    def crop(number):
        return lax.dynamic_index_in_dim(
            slots, jnp.clip(number - first, 0, last_slot), 0, keepdims=False
        )

    target = PER_DEV * seq_index
    up = lax.ppermute(
        crop(target + PER_DEV), SEQ, [(i, i + 1) for i in range(count - 1)]
    )
    down = lax.ppermute(crop(target - 1), SEQ, [(i + 1, i) for i in range(count - 1)])
    crop_a = jnp.where(first <= target, crop(target), up)
    crop_b = jnp.where(limit > target + 1, crop(target + 1), down)
    return jnp.stack([crop_a, crop_b])


def depthwise(block_in, weight, bias):
    side = block_in.shape[1]
    padded = jnp.pad(block_in, ((0, 0), (3, 3), (3, 3), (0, 0)))
    total = jnp.zeros_like(block_in)
    for a in range(KSIDE):
        for b in range(KSIDE):
            total = total + padded[:, a : a + side, b : b + side, :] * weight[a * KSIDE + b]
    return total + bias


def scatter_sum(partial, width):
    core = lax.axis_index("core")
    x = lax.axis_index("x")
    parts = partial.reshape(NX, NCORE, width, partial.shape[1])
    mine = lax.dynamic_index_in_dim(parts, core, 1, keepdims=False)
    other = lax.dynamic_index_in_dim(parts, 1 - core, 1, keepdims=False)
    other = shift(other, "core", 1, NCORE)
    pair = (mine.astype(jnp.float32) + other.astype(jnp.float32)).astype(jnp.bfloat16)

    def part(distance):
        return lax.dynamic_index_in_dim(pair, lax.rem(x + distance, NX), 0, keepdims=False)

    total = part(0).astype(jnp.float32)
    for distance in (2, 1, 3):
        total = total + shift(part(distance), "x", distance, NX).astype(jnp.float32)
    return total


def per_device(
    crop_features, crop_counts, first_crop, tile_embed, dw_weight, conv_bias,
    ln_gain, ln_bias, w_up, b_up, w_down, b_down, gamma,
):
    f32 = jnp.float32
    width = b_down.shape[0]
    side = crop_features.shape[1]
    seq_index = lax.axis_index(SEQ)
    start = lax.axis_index(TP) * width
    weights = gather_weights(w_up, w_down)

    def channels(array):
        return lax.dynamic_slice_in_dim(array, start, width, array.ndim - 1)

    crops = regroup(channels(crop_features), seq_index, first_crop)
    crop_ids = PER_DEV * seq_index + jnp.arange(PER_DEV, dtype=jnp.int32)
    image_start = jnp.cumsum(crop_counts) - crop_counts
    begin = jnp.max(
        jnp.where(image_start[None, :] <= crop_ids[:, None], image_start[None, :], 0), axis=1
    )
    choose = (crop_ids - begin)[:, None] == jnp.arange(tile_embed.shape[0])[None, :]
    tile = jnp.sum(
        jnp.where(choose[:, :, None], channels(tile_embed).astype(f32)[None], 0.0), axis=1
    )
    block_in = crops.astype(f32) + tile[:, None, None, :]
    conv = depthwise(block_in, channels(dw_weight).astype(f32), channels(conv_bias).astype(f32))
    cells = PER_DEV * side * side
    conv_t = conv.reshape(cells, width).T.astype(jnp.float16)
    conv_all = lax.all_gather(conv_t, TP, axis=0, tiled=True).astype(f32)
    mean = jnp.mean(conv_all, axis=0, keepdims=True)
    var = jnp.mean((conv_all - mean) ** 2, axis=0, keepdims=True)
    normed = (
        (conv_all - mean) / jnp.sqrt(var + 1e-6) * ln_gain.astype(f32)[:, None]
        + ln_bias.astype(f32)[:, None]
    ).astype(jnp.bfloat16)
    pre_act = lax.dot_general(
        weights[0], normed, (((0,), (0,)), ((), ())), preferred_element_type=f32
    )
    hidden = jax.nn.gelu(pre_act + b_up.astype(f32)[:, None], approximate=False).astype(jnp.bfloat16)
    partial = jnp.dot(weights[1], hidden, preferred_element_type=f32).astype(jnp.bfloat16)
    branch = scatter_sum(partial, width)
    scaled = (gamma[:, None] * (branch + b_down.astype(f32)[:, None])).T
    result = block_in.reshape(cells, width) + scaled
    return result.astype(jnp.bfloat16).reshape(PER_DEV, side, side, width)


def solution(mesh):
    fine = Mesh(mesh.devices.reshape(NY, NZ, NX, NCORE), SEQ + TP)
    placed = (
        P(SEQ, None, None, None), P(), P(), P(), P(), P(), P(), P(),
        P(SEQ, TP), P(TP), P(TP, SEQ), P(TP), P(TP),
    )
    return jax.shard_map(
        per_device,
        mesh=fine,
        in_specs=placed,
        out_specs=P(SEQ, None, None, TP),
        check_vma=False,
    )
```

time: 393 us -> 179 us (0.46)
  other arithmetic: 204 us -> 20.4 us
  waiting for transfers between devices: 113 us -> 38.3 us
  blocking collectives: 0 us -> 31.6 us
  starting transfers between devices: 7.98 us -> 32.5 us
  local copies, waits for them, and re-layouts: 27 us -> 19.9 us
  matrix products: 21.7 us -> 15.2 us
    reduce_sum x3, other arithmetic: 185 us -> 1.35 us  [the longest x1 0.81 us: per_device(): var = jnp.mean((conv_all - mean) ** 2, axis=0, keepdims=True)]
    all_gather x2 -> x1, waiting for transfers between devices: 66.1 us -> 20.4 us  [gather_weights(): over_z = lax.all_gather(over_y, 'z', axis=2)]
    reduce_scatter x1 -> x0, waiting for transfers between devices: 34.8 us -> none  [encode(): lax.psum_scatter(partial_value.astype(jnp.bfloat16), 'tp', scatter_dimens...]
    all_gather x0 -> x2, blocking collectives: none -> 31.6 us  [the longest x1 21.4 us: per_device(): conv_all = lax.all_gather(conv_t, TP, axis=0, tiled=True).astype(f32)]
    ppermute x2 -> x6, starting transfers between devices: 7.9 us -> 32.5 us  [the longest x4 20 us: shift(): lax.ppermute(block, axis, [(i, (i + distance) % size) for i in range(size)])]
    reshape x3 -> x2, local copies, waits for them, and re-layouts: 19.1 us -> 1.32 us  [per_device(): return result.astype(jnp.bfloat16).reshape(PER_DEV, side, side, width)]
    convert_element_type x11 -> x10, other arithmetic: 7.32 us -> 15.5 us  [the longest x1 7.87 us: per_device(): conv_t = conv.reshape(cells, width).T.astype(jnp.float16)]
    add x3 -> x2, other arithmetic: 7.92 us -> 0.12 us  [the longest x1 0.12 us: per_device(): block_in = crops.astype(f32) + tile[:, None, None, :]]
  transfers between devices with their start and end apart: 5 -> 7, of which waited for: 4 -> 5; matrix products, arithmetic and copies ran while one was open for 59% -> 12% of each run, Pallas kernels for 0% -> 0%
where the time goes in v1:
time: 179 us; the launch traced here: 175 us
  waiting for transfers between devices  38.3 us (21%)
  starting transfers between devices  32.5 us (18%)
  blocking collectives  31.6 us (18%)
  other arithmetic  20.4 us (11%)
  local copies, waits for them, and re-layouts  19.9 us (11%)
  between operations  17.5 us (10%)
  matrix products  15.2 us (8%)
    all_gather x1, blocking collectives, per_device(): conv_all = lax.all_gather(conv_t, TP, axis=0, tiled=True).astype(f32)  21.4 us
    all_gather x1, waiting for transfers between devices, gather_weights(): over_z = lax.all_gather(over_y, 'z', axis=2)  20.4 us
    ppermute x4, starting transfers between devices, shift(): lax.ppermute(block, axis, [(i, (i + distance) % size) for i in range(size)])  20 us
    ppermute x4, waiting for transfers between devices, shift(): lax.ppermute(block, axis, [(i, (i + distance) % size) for i in range(size)])  17.8 us
    dot_general x1, matrix products, per_device(): jnp.dot(weights[1], hidden, preferred_element_type=f32).astype(jnp.bfloat16)  15.2 us
    all_gather x1, blocking collectives, gather_weights(): over_y = lax.all_gather(both, 'y', axis=1)  10.2 us
    ppermute x1, starting transfers between devices, regroup(): lax.ppermute(crop(target - 1), SEQ, [(i + 1, i) for i in range(count - 1)])  8.98 us
    convert_element_type x1, other arithmetic, per_device(): conv_t = conv.reshape(cells, width).T.astype(jnp.float16)  7.87 us
  transfers between devices with their start and end apart: 7, of which 5 were waited for; matrix products, arithmetic and copies ran while one was open for 12% of the time, Pallas kernels for 0%

profile of v1, /device:TPU:25, one launch (start us, length us, event | category | flops | bytes accessed | tf_op | source)
XLA Modules:
  0.0 175.3 jit_solution(3609400214587048692)
XLA Ops:
  7.3 10.2 %all-gather = bf16[2,96,768]{2,1,0:T(8,128)(2,1)} all-gather(bf16[2,24,768]{2,1,0:T(8,128)(2,1)S(1)} %pad_maximum_fusion), channel_id=2, replica_groups=mesh['y'=4,'z'=16,'x'=4,'core'=2] {'y'}, dimensions={1}, use_global_device_ids=true | all-gather | bytes 368640 | tf_op jit(solution)/shard_map/all_gather | solution.py:19
  17.5 1.3 fusion.175
  20.2 1.4 dynamic-slice_bitcast_fusion.5
  21.5 3.5 %collective-permute-start = (bf16[21,21,192]{2,1,0:T(8,128)(2,1)S(1)}, bf16[21,21,192]{2,1,0:T(8,128)(2,1)S(1)}, u32[]{:S(2)}, u32[]{:S(2)}) collective-permute-start(bf16[21,21,192]{2,1,0:T(8,128)(2,1)S(1)} %get-tuple-element.9), channel_id=1, source_target_pairs={{0,8},{8,16},{16,24},{24,32},{32,40},{40,48},{48,56},{56,64},{64,7... | collective-permute-start | bytes 508040 | tf_op jit(solution)/shard_map/ppermute | solution.py:38
  25.1 9.0 %collective-permute-start.1 = (bf16[21,21,192]{2,1,0:T(8,128)(2,1)S(1)}, bf16[21,21,192]{2,1,0:T(8,128)(2,1)S(1)}, u32[]{:S(2)}, u32[]{:S(2)}) collective-permute-start(bf16[21,21,192]{2,1,0:T(8,128)(2,1)S(1)} %get-tuple-element.10), channel_id=1, source_target_pairs={{8,0},{16,8},{24,16},{32,24},{40,32},{48,40},{56,48},{64,56},{72,6... | collective-permute-start | bytes 508040 | tf_op jit(solution)/shard_map/ppermute | solution.py:41
  43.1 1.4 fusion.137
  45.6 7.9 %fusion.131 = f16[2,21,21,192]{3,2,1,0:T(8,128)(2,1)S(1)} fusion(f32[2,21,21,192]{3,2,1,0:T(8,128)S(1)} %convert_add_fusion.1, f32[192]{0:T(256)S(1)} %dynamic-slice_convert_fusion.1, f32[192]{0:T(256)S(1)} %bitcast.125, f32[192]{0:T(256)S(1)} %bitcast.126, f32[192]{0:T(256)S(1)} %bitcast.127, f32[192]{0:T(256)S(1)} %bitcast.128, f32[192]{0:T(256)S(1)} %bitcast.129, ...), kind=kLoop, calls=%fused_computation.188 | loop fusion | flops 16765056 | bytes 1054464 | tf_op jit(solution)/shard_map/convert_element_type | solution.py:102
  54.1 21.4 %all-gather.6 = f16[1536,882]{1,0:T(8,128)(2,1)S(1)} all-gather(f16[192,882]{1,0:T(8,128)(2,1)S(1)} %copy.31), channel_id=1, replica_groups=mesh['y'=4,'z'=16,'x'=4,'core'=2] {'x','core'}, dimensions={0}, use_global_device_ids=true | all-gather | bytes 3048192 | tf_op jit(solution)/shard_map/all_gather | solution.py:103
  76.8 20.4 %all-gather.5.cloned.1.call-done = bf16[2,4,384,768]{3,2,1,0:T(8,128)(2,1)} async-done(((bf16[2,4,24,768]{3,2,1,0:T(8,128)(2,1)}), bf16[2,4,384,768]{3,2,1,0:T(8,128)(2,1)}) %all-gather.5.cloned.1.call-update) | async-done | bytes 4718608 | tf_op jit(solution)/shard_map/all_gather | solution.py:20
  97.2 4.8 %fusion.171 = (bf16[1,4,384,768]{3,2,1,0:T(8,128)(2,1)}, bf16[1,4,384,768]{3,2,1,0:T(8,128)(2,1)}) fusion(bf16[2,4,384,768]{3,2,1,0:T(8,128)(2,1)} %all-gather.5.cloned.1.call-done), kind=kLoop, calls=%fused_computation.248 | loop fusion | bytes 9437184 | tf_op jit(solution)/shard_map/slice | solution.py:111
  102.1 15.2 %convolution_convert_fusion = bf16[1536,882]{0,1:T(8,128)(2,1)} fusion(bf16[1536,768]{1,0:T(8,128)(2,1)} %bitcast.100, bf16[1536,768]{1,0:T(8,128)(2,1)} %bitcast.99, f16[1536,882]{1,0:T(8,128)(2,1)S(1)} %all-gather.6, f32[1536]{0:T(1024)S(1)} %convert_element_type.88, f32[1536]{0:T(1024)S(1)} %convert_element_type.87, f32[882]{0:T(1024)S(1)} %add_sqrt_fusion, ...), kind=kOutput, calls=%fused_computation.57 | convolution fusion | flops 4215988224 | bytes 10160016 | tf_op jit(solution)/shard_map/dot_general | solution.py:114
  117.2 3.3 %copy.32 = bf16[1536,882]{1,0:T(8,128)(2,1)S(1)} copy(bf16[1536,882]{0,1:T(8,128)(2,1)} %convolution_convert_fusion) | data formatting | bytes 5419008 | tf_op jit(solution)/shard_map/convert_element_type | solution.py:114
  120.5 1.2 dynamic-slice_bitcast_fusion
  121.7 10.2 %collective-permute-start.2 = (bf16[4,192,882]{2,1,0:T(8,128)(2,1)}, bf16[4,192,882]{2,1,0:T(8,128)(2,1)}, u32[]{:S(2)}, u32[]{:S(2)}) collective-permute-start(bf16[4,192,882]{2,1,0:T(8,128)(2,1)} %dynamic-slice_bitcast_fusion), channel_id=1, source_target_pairs={{0,1},{1,0},{2,3},{3,2},{4,5},{5,4},{6,7},{7,6},{8,9},{9,8},{10,11... | collective-permute-start | bytes 4064264 | tf_op jit(solution)/shard_map/ppermute | solution.py:14
  132.0 3.0 %collective-permute-done.2 = bf16[4,192,882]{2,1,0:T(8,128)(2,1)} collective-permute-done((bf16[4,192,882]{2,1,0:T(8,128)(2,1)}, bf16[4,192,882]{2,1,0:T(8,128)(2,1)}, u32[]{:S(2)}, u32[]{:S(2)}) %collective-permute-start.2) | collective-permute-done | bytes 1354784 | tf_op jit(solution)/shard_map/ppermute | solution.py:14
  135.0 1.7 fusion.6
  139.8 2.8 %collective-permute-start.4 = (bf16[192,882]{0,1:T(8,128)(2,1)}, bf16[192,882]{0,1:T(8,128)(2,1)S(1)}, u32[]{:S(2)}, u32[]{:S(2)}) collective-permute-start(bf16[192,882]{0,1:T(8,128)(2,1)} %copy.35), channel_id=1, source_target_pairs={{0,2},{2,4},{4,6},{6,0},{1,3},{3,5},{5,7},{7,1},{8,10},{10,12},{12... | collective-permute-start | bytes 1016072 | tf_op jit(solution)/shard_map/ppermute | solution.py:14
  142.6 3.7 %collective-permute-start.5 = (bf16[192,882]{0,1:T(8,128)(2,1)}, bf16[192,882]{0,1:T(8,128)(2,1)S(1)}, u32[]{:S(2)}, u32[]{:S(2)}) collective-permute-start(bf16[192,882]{0,1:T(8,128)(2,1)} %copy.36), channel_id=1, source_target_pairs={{0,6},{2,0},{4,2},{6,4},{1,7},{3,1},{5,3},{7,5},{8,14},{10,8},{12,... | collective-permute-start | bytes 1016072 | tf_op jit(solution)/shard_map/ppermute | solution.py:14
  146.3 3.3 %collective-permute-start.3 = (bf16[192,882]{0,1:T(8,128)(2,1)}, bf16[192,882]{0,1:T(8,128)(2,1)}, u32[]{:S(2)}, u32[]{:S(2)}) collective-permute-start(bf16[192,882]{0,1:T(8,128)(2,1)} %copy.33), channel_id=1, source_target_pairs={{0,4},{2,6},{4,0},{6,2},{1,5},{3,7},{5,1},{7,3},{8,12},{10,14},{12... | collective-permute-start | bytes 1016072 | tf_op jit(solution)/shard_map/ppermute | solution.py:14
  150.1 4.7 %collective-permute-done.4 = bf16[192,882]{0,1:T(8,128)(2,1)S(1)} collective-permute-done((bf16[192,882]{0,1:T(8,128)(2,1)}, bf16[192,882]{0,1:T(8,128)(2,1)S(1)}, u32[]{:S(2)}, u32[]{:S(2)}) %collective-permute-start.4) | collective-permute-done | bytes 338720 | tf_op jit(solution)/shard_map/ppermute | solution.py:14
  154.8 1.3 collective-permute-done.5
  156.8 8.8 %collective-permute-done.3 = bf16[192,882]{0,1:T(8,128)(2,1)} collective-permute-done((bf16[192,882]{0,1:T(8,128)(2,1)}, bf16[192,882]{0,1:T(8,128)(2,1)}, u32[]{:S(2)}, u32[]{:S(2)}) %collective-permute-start.3) | collective-permute-done | bytes 338720 | tf_op jit(solution)/shard_map/ppermute | solution.py:14
  165.7 1.5 fusion.135
  167.3 1.1 copy.37
  (48 shorter events, 14.7 us)
Async XLA Ops:
  6.5 90.7 %all-gather.5.cloned.1.call-start = ((), (), s32[]{:S(2)}) async-start(), calls=%async_computation | async-start | bytes 5013504 | tf_op jit(solution)/shard_map/all_gather | solution.py:20
  21.5 21.5 %collective-permute-start = (bf16[21,21,192]{2,1,0:T(8,128)(2,1)S(1)}, bf16[21,21,192]{2,1,0:T(8,128)(2,1)S(1)}, u32[]{:S(2)}, u32[]{:S(2)}) collective-permute-start(bf16[21,21,192]{2,1,0:T(8,128)(2,1)S(1)} %get-tuple-element.9), channel_id=1, source_target_pairs={{0,8},{8,16},{16,24},{24,32},{32,40},{40,48},{48,56},{56,64},{64,7... | collective-permute-start | bytes 508040 | tf_op jit(solution)/shard_map/ppermute | solution.py:38
  25.1 18.0 %collective-permute-start.1 = (bf16[21,21,192]{2,1,0:T(8,128)(2,1)S(1)}, bf16[21,21,192]{2,1,0:T(8,128)(2,1)S(1)}, u32[]{:S(2)}, u32[]{:S(2)}) collective-permute-start(bf16[21,21,192]{2,1,0:T(8,128)(2,1)S(1)} %get-tuple-element.10), channel_id=1, source_target_pairs={{8,0},{16,8},{24,16},{32,24},{40,32},{48,40},{56,48},{64,56},{72,6... | collective-permute-start | bytes 508040 | tf_op jit(solution)/shard_map/ppermute | solution.py:41
  44.6 1.0 copy-start
  121.7 13.3 %collective-permute-start.2 = (bf16[4,192,882]{2,1,0:T(8,128)(2,1)}, bf16[4,192,882]{2,1,0:T(8,128)(2,1)}, u32[]{:S(2)}, u32[]{:S(2)}) collective-permute-start(bf16[4,192,882]{2,1,0:T(8,128)(2,1)} %dynamic-slice_bitcast_fusion), channel_id=1, source_target_pairs={{0,1},{1,0},{2,3},{3,2},{4,5},{5,4},{6,7},{7,6},{8,9},{9,8},{10,11... | collective-permute-start | bytes 4064264 | tf_op jit(solution)/shard_map/ppermute | solution.py:14
  136.7 12.9 %copy-start.4 = (bf16[192]{0:T(256)(128)(2,1)S(1)}, bf16[192]{0:T(256)(128)(2,1)}, u32[]{:S(2)}) copy-start(bf16[192]{0:T(256)(128)(2,1)} %param.24) | copy-start | bytes 1156
  136.7 13.0 %copy-start.1 = (f32[2,21,21,192]{3,2,1,0:T(8,128)S(1)}, f32[2,21,21,192]{3,2,1,0:T(8,128)}, u32[]{:S(2)}) copy-start(f32[2,21,21,192]{3,2,1,0:T(8,128)} %copy-done) | copy-start | bytes 2032132
  137.9 27.8 %copy-start.3 = (f32[192]{0:T(256)S(1)}, f32[192]{0:T(256)}, u32[]{:S(2)}) copy-start(f32[192]{0:T(256)} %param.25) | copy-start | bytes 2308
  139.8 14.9 %collective-permute-start.4 = (bf16[192,882]{0,1:T(8,128)(2,1)}, bf16[192,882]{0,1:T(8,128)(2,1)S(1)}, u32[]{:S(2)}, u32[]{:S(2)}) collective-permute-start(bf16[192,882]{0,1:T(8,128)(2,1)} %copy.35), channel_id=1, source_target_pairs={{0,2},{2,4},{4,6},{6,0},{1,3},{3,5},{5,7},{7,1},{8,10},{10,12},{12... | collective-permute-start | bytes 1016072 | tf_op jit(solution)/shard_map/ppermute | solution.py:14
  142.6 13.4 %collective-permute-start.5 = (bf16[192,882]{0,1:T(8,128)(2,1)}, bf16[192,882]{0,1:T(8,128)(2,1)S(1)}, u32[]{:S(2)}, u32[]{:S(2)}) collective-permute-start(bf16[192,882]{0,1:T(8,128)(2,1)} %copy.36), channel_id=1, source_target_pairs={{0,6},{2,0},{4,2},{6,4},{1,7},{3,1},{5,3},{7,5},{8,14},{10,8},{12,... | collective-permute-start | bytes 1016072 | tf_op jit(solution)/shard_map/ppermute | solution.py:14
  146.3 19.3 %collective-permute-start.3 = (bf16[192,882]{0,1:T(8,128)(2,1)}, bf16[192,882]{0,1:T(8,128)(2,1)}, u32[]{:S(2)}, u32[]{:S(2)}) collective-permute-start(bf16[192,882]{0,1:T(8,128)(2,1)} %copy.33), channel_id=1, source_target_pairs={{0,4},{2,6},{4,0},{6,2},{1,5},{3,7},{5,1},{7,3},{8,12},{10,14},{12... | collective-permute-start | bytes 1016072 | tf_op jit(solution)/shard_map/ppermute | solution.py:14
  156.1 0.8 copy-start.2
Sparse Core Ops, SparseCore 0:
  17.6 79.5 all-gather.4

commit v2 on v1

--- a/solution.py
+++ b/solution.py
@@ -1,6 +1,8 @@
 import jax
 import jax.numpy as jnp
 from jax import lax
+from jax.experimental import pallas as pl
+from jax.experimental.pallas import tpu as pltpu
 from jax.sharding import Mesh, PartitionSpec as P
 
 NY, NZ, NX, NCORE = 4, 16, 4, 2
@@ -54,22 +56,138 @@
     return total + bias
 
 
-def scatter_sum(partial, width):
-    core = lax.axis_index("core")
-    x = lax.axis_index("x")
-    parts = partial.reshape(NX, NCORE, width, partial.shape[1])
-    mine = lax.dynamic_index_in_dim(parts, core, 1, keepdims=False)
-    other = lax.dynamic_index_in_dim(parts, 1 - core, 1, keepdims=False)
+def whole(space=pltpu.VMEM):
+    return pl.BlockSpec(memory_space=space)
+
+
+def copy_down_rows(weights, buffer, sems, core):
+    width = buffer.shape[0] // NX
+    copies = []
+    for x in range(NX):
+        row = pl.multiple_of((x * NCORE + core) * width, width)
+        copies.append(
+            pltpu.make_async_copy(
+                weights.at[1, pl.ds(row, width), :],
+                buffer.at[pl.ds(x * width, width), :],
+                sems.at[x],
+            )
+        )
+    return copies
+
+
+def down_product(buffer, hidden, out):
+    width = buffer.shape[0] // NX
+    product = lax.dot_general(
+        buffer[...], hidden, (((1,), (1,)), ((), ())), preferred_element_type=jnp.float32
+    )
+    for x in range(NX):
+        out[x] = product[x * width : (x + 1) * width].astype(out.dtype)
+
+
+def first_kernel(core, normed, b_up, weights, hidden, out, up, down, up_sem, down_sem):
+    units = up.shape[1]
+    pieces = up_sem.shape[0]
+    step = units // pieces
+    ups = []
+    for p in range(pieces):
+        span = pl.ds(p * step, step)
+        ups.append(
+            pltpu.make_async_copy(weights.at[0, :, span], up.at[:, span], up_sem.at[p])
+        )
+    for copy in ups:
+        copy.start()
+    downs = copy_down_rows(weights, down, down_sem, 1 - core[0])
+    for copy in downs:
+        copy.start()
+    for p in range(pieces):
+        span = pl.ds(p * step, step)
+        ups[p].wait()
+        pre = jnp.dot(normed[...], up[:, span], preferred_element_type=jnp.float32)
+        pre = pre + b_up[:, span]
+        act = 0.5 * pre * (1.0 + lax.erf(pre * 0.5**0.5))
+        hidden[:, span] = act.astype(hidden.dtype)
+    for copy in downs:
+        copy.wait()
+    down_product(down, hidden[...], out)
+
+
+def second_kernel(core, hidden, weights, out, down, down_sem):
+    downs = copy_down_rows(weights, down, down_sem, core[0])
+    for copy in downs:
+        copy.start()
+    for copy in downs:
+        copy.wait()
+    down_product(down, hidden[...], out)
+
+
+def pair_kernel(x, mine, other, own, ahead, behind, far_a, far_b):
+    def pair(distance):
+        i = lax.rem(x[0] + distance, NX)
+        return mine[i].astype(jnp.float32) + other[i].astype(jnp.float32)
+
+    half = far_a.shape[0]
+    own[...] = pair(0)
+    ahead[...] = pair(1).astype(ahead.dtype)
+    behind[...] = pair(3).astype(behind.dtype)
+    far = pair(2)
+    far_a[...] = far[:half].astype(far_a.dtype)
+    far_b[...] = far[half:].astype(far_b.dtype)
+
+
+def last_kernel(own, ahead, behind, b_down, gamma, residual, out):
+    total = own[...] + ahead[...].astype(jnp.float32) + behind[...].astype(jnp.float32)
+    scaled = gamma[...] * (total + b_down[...])
+    rows = residual.shape[0]
+    out[...] = (residual[...] + scaled.T[:rows]).astype(out.dtype)
+
+
+def mlp_sum(normed, weights, b_up, width):
+    bf16, f32 = jnp.bfloat16, jnp.float32
+    cells, units = normed.shape[0], b_up.shape[0]
+    core = lax.axis_index("core").astype(jnp.int32).reshape(1)
+    x = lax.axis_index("x").astype(jnp.int32).reshape(1)
+    params = pltpu.CompilerParams(vmem_limit_bytes=48 * 2**20)
+    half_out = jax.ShapeDtypeStruct((NX, width, cells), bf16)
+    down = pltpu.VMEM((NX * width, units), bf16)
+    hidden, other = pl.pallas_call(
+        first_kernel,
+        out_shape=(jax.ShapeDtypeStruct((cells, units), bf16), half_out),
+        in_specs=[whole(pltpu.SMEM), whole(), whole(), whole(pl.ANY)],
+        out_specs=(whole(), whole()),
+        scratch_shapes=[
+            pltpu.VMEM(weights.shape[1:], bf16),
+            down,
+            pltpu.SemaphoreType.DMA((3,)),
+            pltpu.SemaphoreType.DMA((NX,)),
+        ],
+        compiler_params=params,
+        name="up_and_down",
+    )(core, normed, b_up.astype(f32)[None, :], weights)
     other = shift(other, "core", 1, NCORE)
-    pair = (mine.astype(jnp.float32) + other.astype(jnp.float32)).astype(jnp.bfloat16)
-
-    def part(distance):
-        return lax.dynamic_index_in_dim(pair, lax.rem(x + distance, NX), 0, keepdims=False)
-
-    total = part(0).astype(jnp.float32)
-    for distance in (2, 1, 3):
-        total = total + shift(part(distance), "x", distance, NX).astype(jnp.float32)
-    return total
+    mine = pl.pallas_call(
+        second_kernel,
+        out_shape=half_out,
+        in_specs=[whole(pltpu.SMEM), whole(), whole(pl.ANY)],
+        out_specs=whole(),
+        scratch_shapes=[down, pltpu.SemaphoreType.DMA((NX,))],
+        compiler_params=params,
+        name="down_own",
+    )(core, hidden, weights)
+    full = jax.ShapeDtypeStruct((width, cells), bf16)
+    half = jax.ShapeDtypeStruct((width // 2, cells), bf16)
+    own, ahead, behind, far_a, far_b = pl.pallas_call(
+        pair_kernel,
+        out_shape=(jax.ShapeDtypeStruct((width, cells), f32), full, full, half, half),
+        in_specs=[whole(pltpu.SMEM), whole(), whole()],
+        out_specs=(whole(),) * 5,
+        compiler_params=params,
+        name="pair",
+    )(x, mine, other)
+    far_a = shift(far_a, "x", 1, NX)
+    far_b = shift(far_b, "x", -1, NX)
+    ahead = jnp.concatenate([ahead[: width // 2] + far_a, ahead[width // 2 :]])
+    behind = jnp.concatenate([behind[: width // 2], behind[width // 2 :] + far_b])
+    return own, shift(ahead, "x", 1, NX), shift(behind, "x", -1, NX)
 
 
 def per_device(
@@ -99,23 +217,25 @@
     block_in = crops.astype(f32) + tile[:, None, None, :]
     conv = depthwise(block_in, channels(dw_weight).astype(f32), channels(conv_bias).astype(f32))
     cells = PER_DEV * side * side
-    conv_t = conv.reshape(cells, width).T.astype(jnp.float16)
+    padding = -cells % 128
+    conv_t = jnp.pad(conv.reshape(cells, width), ((0, padding), (0, 0))).T.astype(jnp.float16)
     conv_all = lax.all_gather(conv_t, TP, axis=0, tiled=True).astype(f32)
     mean = jnp.mean(conv_all, axis=0, keepdims=True)
     var = jnp.mean((conv_all - mean) ** 2, axis=0, keepdims=True)
     normed = (
         (conv_all - mean) / jnp.sqrt(var + 1e-6) * ln_gain.astype(f32)[:, None]
         + ln_bias.astype(f32)[:, None]
-    ).astype(jnp.bfloat16)
-    pre_act = lax.dot_general(
-        weights[0], normed, (((0,), (0,)), ((), ())), preferred_element_type=f32
-    )
-    hidden = jax.nn.gelu(pre_act + b_up.astype(f32)[:, None], approximate=False).astype(jnp.bfloat16)
-    partial = jnp.dot(weights[1], hidden, preferred_element_type=f32).astype(jnp.bfloat16)
-    branch = scatter_sum(partial, width)
-    scaled = (gamma[:, None] * (branch + b_down.astype(f32)[:, None])).T
-    result = block_in.reshape(cells, width) + scaled
-    return result.astype(jnp.bfloat16).reshape(PER_DEV, side, side, width)
+    ).astype(jnp.bfloat16).T
+    own, ahead, behind = mlp_sum(normed, weights, b_up, width)
+    result = pl.pallas_call(
+        last_kernel,
+        out_shape=jax.ShapeDtypeStruct((cells, width), jnp.bfloat16),
+        in_specs=[whole()] * 6,
+        out_specs=whole(),
+        compiler_params=pltpu.CompilerParams(vmem_limit_bytes=48 * 2**20),
+        name="result",
+    )(own, ahead, behind, b_down.astype(f32)[:, None], gamma[:, None], block_in.reshape(cells, width))
+    return result.reshape(PER_DEV, side, side, width)
 
 
 def solution(mesh):

time: 179 us -> 156 us (0.87)
  waiting for transfers between devices: 38.3 us -> 21.3 us
  matrix products: 15.2 us -> 0 us
  Pallas kernels: 0 us -> 11.3 us
  local copies, waits for them, and re-layouts: 19.9 us -> 11.9 us
  starting transfers between devices: 32.5 us -> 36.6 us
  other arithmetic: 20.4 us -> 22.2 us
    dot_general x1 -> x0, matrix products: 15.2 us -> none  [per_device(): jnp.dot(weights[1], hidden, preferred_element_type=f32).astype(jnp.bfloat16)]
    convert_element_type x5 -> x0, other arithmetic: 11.7 us -> none  [the longest x1 7.87 us: per_device(): conv_t = conv.reshape(cells, width).T.astype(jnp.float16)]
    pallas_call x0 -> x4, Pallas kernels: none -> 11.3 us  [the longest x1 7.85 us: mlp_sum(): pl.pallas_call(first_kernel, out_shape=(jax.ShapeDtypeStruct((cells, unit...]
    all_gather x1, waiting for transfers between devices: 20.4 us -> 10.3 us  [gather_weights(): over_z = lax.all_gather(over_y, 'z', axis=2)]
    another operation x2 -> x3, other arithmetic: 0.2 us -> 8.05 us
    ppermute x4 -> x5, waiting for transfers between devices: 17.8 us -> 10.9 us  [shift(): lax.ppermute(block, axis, [(i, (i + distance) % size) for i in range(size)])]
    slice x1 -> x0, local copies, waits for them, and re-layouts: 4.84 us -> none  [per_device(): weights[0]]
    transpose x0 -> x1, other arithmetic: none -> 4.18 us  [per_device(): normed = ((conv_all - mean) / jnp.sqrt(var + 1e-06) * ln_gain.astype(f32)...]
  transfers between devices with their start and end apart: 7 -> 8, of which waited for: 5 -> 4; matrix products, arithmetic and copies ran while one was open for 12% -> 20% of each run, Pallas kernels for 0% -> 2%
where the time goes in v2:
time: 156 us; the launch traced here: 154 us
  starting transfers between devices  36.6 us (23%)
  blocking collectives  32.5 us (21%)
  other arithmetic  22.2 us (14%)
  waiting for transfers between devices  21.3 us (14%)
  between operations  17.9 us (11%)
  local copies, waits for them, and re-layouts  11.9 us (8%)
  Pallas kernels  11.3 us (7%)
    ppermute x5, starting transfers between devices, shift(): lax.ppermute(block, axis, [(i, (i + distance) % size) for i in range(size)])  24 us
    all_gather x1, blocking collectives, per_device(): conv_all = lax.all_gather(conv_t, TP, axis=0, tiled=True).astype(f32)  22.3 us
    ppermute x5, waiting for transfers between devices, shift(): lax.ppermute(block, axis, [(i, (i + distance) % size) for i in range(size)])  10.9 us
    all_gather x1, waiting for transfers between devices, gather_weights(): over_z = lax.all_gather(over_y, 'z', axis=2)  10.3 us
    all_gather x1, blocking collectives, gather_weights(): over_y = lax.all_gather(both, 'y', axis=1)  10.2 us
    ppermute x1, starting transfers between devices, regroup(): lax.ppermute(crop(target - 1), SEQ, [(i + 1, i) for i in range(count - 1)])  8.98 us
    another operation x3, other arithmetic  8.05 us
    pallas_call x1, Pallas kernels, mlp_sum(): pl.pallas_call(first_kernel, out_shape=(jax.ShapeDtypeStruct((cells, unit...  7.85 us
  transfers between devices with their start and end apart: 8, of which 4 were waited for; matrix products, arithmetic and copies ran while one was open for 20% of the time, Pallas kernels for 2%

profile of v2, /device:TPU:25, one launch (start us, length us, event | category | flops | bytes accessed | tf_op | source)
XLA Modules:
  0.0 153.6 jit_solution(10019912986963223707)
XLA Ops:
  7.3 10.2 %all-gather = bf16[2,96,768]{2,1,0:T(8,128)(2,1)} all-gather(bf16[2,24,768]{2,1,0:T(8,128)(2,1)S(1)} %pad_maximum_fusion.2), channel_id=2, replica_groups=mesh['y'=4,'z'=16,'x'=4,'core'=2] {'y'}, dimensions={1}, use_global_device_ids=true | all-gather | bytes 368640 | tf_op jit(solution)/shard_map/all_gather | solution.py:21
  17.5 1.4 fusion.113
  20.3 1.4 dynamic-slice_bitcast_fusion.1
  21.7 3.5 %collective-permute-start = (bf16[21,21,192]{2,1,0:T(8,128)(2,1)S(1)}, bf16[21,21,192]{2,1,0:T(8,128)(2,1)S(1)}, u32[]{:S(2)}, u32[]{:S(2)}) collective-permute-start(bf16[21,21,192]{2,1,0:T(8,128)(2,1)S(1)} %get-tuple-element.21), channel_id=1, source_target_pairs={{0,8},{8,16},{16,24},{24,32},{32,40},{40,48},{48,56},{56,64},{64,7... | collective-permute-start | bytes 508040 | tf_op jit(solution)/shard_map/ppermute | solution.py:40
  25.3 9.0 %collective-permute-start.1 = (bf16[21,21,192]{2,1,0:T(8,128)(2,1)S(1)}, bf16[21,21,192]{2,1,0:T(8,128)(2,1)S(1)}, u32[]{:S(2)}, u32[]{:S(2)}) collective-permute-start(bf16[21,21,192]{2,1,0:T(8,128)(2,1)S(1)} %get-tuple-element.22), channel_id=1, source_target_pairs={{8,0},{16,8},{24,16},{32,24},{40,32},{48,40},{56,48},{64,56},{72,6... | collective-permute-start | bytes 508040 | tf_op jit(solution)/shard_map/ppermute | solution.py:43
  43.5 1.4 fusion.106
  45.0 1.0 copy-done.1
  46.0 7.8 %fusion.101 = f16[2,21,21,192]{3,2,1,0:T(8,128)(2,1)S(1)} fusion(f32[2,21,21,192]{3,2,1,0:T(8,128)S(1)} %convert_add_fusion, f32[192]{0:T(256)S(1)} %dynamic-slice_convert_fusion.2, f32[192]{0:T(256)S(1)} %bitcast.88, f32[192]{0:T(256)S(1)} %bitcast.89, f32[192]{0:T(256)S(1)} %bitcast.90, f32[192]{0:T(256)S(1)} %bitcast.91, f32[192]{0:T(256)S(1)} %bitcast.92, ...), kind=kLoop, calls=%fused_computation.151 | loop fusion | flops 16765056 | bytes 1054464 | tf_op jit(solution)/shard_map/convert.4
  54.6 22.3 %all-gather.6 = f16[1536,896]{1,0:T(8,128)(2,1)} all-gather(f16[192,896]{1,0:T(8,128)(2,1)S(1)} %copy.27), channel_id=1, replica_groups=mesh['y'=4,'z'=16,'x'=4,'core'=2] {'x','core'}, dimensions={0}, use_global_device_ids=true | all-gather | bytes 3096576 | tf_op jit(solution)/shard_map/all_gather | solution.py:222
  76.9 4.1 %copy.28 = f16[1536,896]{0,1:T(8,128)(2,1)S(1)} copy(f16[1536,896]{1,0:T(8,128)(2,1)} %all-gather.6) | data formatting | bytes 5505024 | tf_op jit(solution)/shard_map/all_gather | solution.py:222
  81.4 0.9 fusion.2
  82.6 4.2 %fusion.6.normed = bf16[896,1536]{1,0:T(8,128)(2,1)S(1)} fusion(f16[1536,896]{0,1:T(8,128)(2,1)} %copy-done, f32[1536]{0:T(1024)S(1)} %convert_element_type.43, f32[1536]{0:T(1024)S(1)} %convert_element_type.42, f32[896]{0:T(1024)S(1)} %add_sqrt_fusion, f32[896]{0:T(1024)S(1)} %broadcast_multiply_fusion), kind=kLoop, calls=%fused_computation.56 | loop fusion | flops 8257536 | bytes 5524480 | tf_op jit(solution)/shard_map/transpose | solution.py:228
  86.7 10.3 %all-gather.5.cloned.1.call-done = bf16[2,4,384,768]{3,2,1,0:T(8,128)(2,1)} async-done(((bf16[2,4,24,768]{3,2,1,0:T(8,128)(2,1)}), bf16[2,4,384,768]{3,2,1,0:T(8,128)(2,1)}) %all-gather.5.cloned.1.call-update) | async-done | bytes 4718608 | tf_op jit(solution)/shard_map/all_gather | solution.py:22
  97.1 7.9 %up_and_down.1 = (bf16[896,768]{1,0:T(8,128)(2,1)S(1)}, bf16[4,192,896]{2,1,0:T(8,128)(2,1)S(1)}) custom-call(s32[1]{0:T(128)} %bitcast.1.core, bf16[896,1536]{1,0:T(8,128)(2,1)S(1)} %fusion.6.normed, f32[1,768]{1,0:T(1,128)S(1)} %reshape.150.b_up, bf16[2,1536,768]{2,1,0:T(8,128)(2,1)} %bitcast.82), custom_call_target="tpu_custom_call" | custom-call | tf_op jit(solution)/shard_map/up_and_down/pallas_call | solution.py:152
  105.0 10.4 %collective-permute-start.2 = (bf16[4,192,896]{2,1,0:T(8,128)(2,1)S(1)}, bf16[4,192,896]{2,1,0:T(8,128)(2,1)S(1)}, u32[]{:S(2)}, u32[]{:S(2)}) collective-permute-start(bf16[4,192,896]{2,1,0:T(8,128)(2,1)S(1)} %get-tuple-element.13), channel_id=1, source_target_pairs={{0,1},{1,0},{2,3},{3,2},{4,5},{5,4},{6,7},{7,6},{8,9},{9,8},{10,11... | collective-permute-start | bytes 4128776 | tf_op jit(solution)/shard_map/ppermute | solution.py:16
  115.4 2.7 %down_own.1.mine = bf16[4,192,896]{2,1,0:T(8,128)(2,1)S(1)} custom-call(s32[1]{0:T(128)} %bitcast.1.core, bf16[896,768]{1,0:T(8,128)(2,1)S(1)} %get-tuple-element.12.hidden, bf16[2,1536,768]{2,1,0:T(8,128)(2,1)} %bitcast.83), custom_call_target="tpu_custom_call" | custom-call | tf_op jit(solution)/shard_map/down_own/pallas_call | solution.py:167
  118.4 4.5 %collective-permute-start.5 = (bf16[96,896]{1,0:T(8,128)(2,1)S(1)}, bf16[96,896]{1,0:T(8,128)(2,1)S(1)}, u32[]{:S(2)}, u32[]{:S(2)}) collective-permute-start(bf16[96,896]{1,0:T(8,128)(2,1)S(1)} %get-tuple-element.18), channel_id=1, source_target_pairs={{0,6},{2,0},{4,2},{6,4},{1,7},{3,1},{5,3},{7,5},{8,14},{10,8},{12,... | collective-permute-start | bytes 516104 | tf_op jit(solution)/shard_map/ppermute | solution.py:16
  122.9 1.9 %collective-permute-start.3 = (bf16[96,896]{1,0:T(8,128)(2,1)S(1)}, bf16[96,896]{1,0:T(8,128)(2,1)S(1)}, u32[]{:S(2)}, u32[]{:S(2)}) collective-permute-start(bf16[96,896]{1,0:T(8,128)(2,1)S(1)} %get-tuple-element.16), channel_id=1, source_target_pairs={{0,2},{2,4},{4,6},{6,0},{1,3},{3,5},{5,7},{7,1},{8,10},{10,12},{12... | collective-permute-start | bytes 516104 | tf_op jit(solution)/shard_map/ppermute | solution.py:16
  124.9 1.7 %collective-permute-done.5 = bf16[96,896]{1,0:T(8,128)(2,1)S(1)} collective-permute-done((bf16[96,896]{1,0:T(8,128)(2,1)S(1)}, bf16[96,896]{1,0:T(8,128)(2,1)S(1)}, u32[]{:S(2)}, u32[]{:S(2)}) %collective-permute-start.5) | collective-permute-done | bytes 172064 | tf_op jit(solution)/shard_map/ppermute | solution.py:16
  127.3 5.3 %collective-permute-start.6 = (bf16[192,896]{1,0:T(8,128)(2,1)}, bf16[192,896]{1,0:T(8,128)(2,1)S(1)}, u32[]{:S(2)}, u32[]{:S(2)}) collective-permute-start(bf16[192,896]{1,0:T(8,128)(2,1)} %pad_maximum_fusion.1), channel_id=1, source_target_pairs={{0,6},{2,0},{4,2},{6,4},{1,7},{3,1},{5,3},{7,5},{8,14},{10,8},{12,... | collective-permute-start | bytes 1032200 | tf_op jit(solution)/shard_map/ppermute | solution.py:16
  133.5 1.9 %collective-permute-start.4 = (bf16[192,896]{1,0:T(8,128)(2,1)}, bf16[192,896]{1,0:T(8,128)(2,1)S(1)}, u32[]{:S(2)}, u32[]{:S(2)}) collective-permute-start(bf16[192,896]{1,0:T(8,128)(2,1)} %pad_maximum_fusion), channel_id=1, source_target_pairs={{0,2},{2,4},{4,6},{6,0},{1,3},{3,5},{5,7},{7,1},{8,10},{10,12},{12... | collective-permute-start | bytes 1032200 | tf_op jit(solution)/shard_map/ppermute | solution.py:16
  135.8 3.5 %collective-permute-done.6.behind = bf16[192,896]{1,0:T(8,128)(2,1)S(1)} collective-permute-done((bf16[192,896]{1,0:T(8,128)(2,1)}, bf16[192,896]{1,0:T(8,128)(2,1)S(1)}, u32[]{:S(2)}, u32[]{:S(2)}) %collective-permute-start.6) | collective-permute-done | bytes 344096 | tf_op jit(solution)/shard_map/ppermute | solution.py:16
  139.3 5.7 %collective-permute-done.4.ahead = bf16[192,896]{1,0:T(8,128)(2,1)S(1)} collective-permute-done((bf16[192,896]{1,0:T(8,128)(2,1)}, bf16[192,896]{1,0:T(8,128)(2,1)S(1)}, u32[]{:S(2)}, u32[]{:S(2)}) %collective-permute-start.4) | collective-permute-done | bytes 344096 | tf_op jit(solution)/shard_map/ppermute | solution.py:16
  145.7 1.1 copy.31
  (52 shorter events, 11.6 us)
Async XLA Ops:
  6.5 90.6 %all-gather.5.cloned.1.call-start = ((), (), s32[]{:S(2)}) async-start(), calls=%async_computation | async-start | bytes 5013504 | tf_op jit(solution)/shard_map/all_gather | solution.py:22
  21.7 21.7 %collective-permute-start = (bf16[21,21,192]{2,1,0:T(8,128)(2,1)S(1)}, bf16[21,21,192]{2,1,0:T(8,128)(2,1)S(1)}, u32[]{:S(2)}, u32[]{:S(2)}) collective-permute-start(bf16[21,21,192]{2,1,0:T(8,128)(2,1)S(1)} %get-tuple-element.21), channel_id=1, source_target_pairs={{0,8},{8,16},{16,24},{24,32},{32,40},{40,48},{48,56},{56,64},{64,7... | collective-permute-start | bytes 508040 | tf_op jit(solution)/shard_map/ppermute | solution.py:40
  25.3 18.2 %collective-permute-start.1 = (bf16[21,21,192]{2,1,0:T(8,128)(2,1)S(1)}, bf16[21,21,192]{2,1,0:T(8,128)(2,1)S(1)}, u32[]{:S(2)}, u32[]{:S(2)}) collective-permute-start(bf16[21,21,192]{2,1,0:T(8,128)(2,1)S(1)} %get-tuple-element.22), channel_id=1, source_target_pairs={{8,0},{16,8},{24,16},{32,24},{40,32},{48,40},{56,48},{64,56},{72,6... | collective-permute-start | bytes 508040 | tf_op jit(solution)/shard_map/ppermute | solution.py:43
  45.0 1.0 copy-start.1
  81.0 1.6 %copy-start = (f16[1536,896]{0,1:T(8,128)(2,1)}, f16[1536,896]{0,1:T(8,128)(2,1)S(1)}, u32[]{:S(2)}) copy-start(f16[1536,896]{0,1:T(8,128)(2,1)S(1)} %copy.28) | copy-start | bytes 8257540
  105.0 13.1 %collective-permute-start.2 = (bf16[4,192,896]{2,1,0:T(8,128)(2,1)S(1)}, bf16[4,192,896]{2,1,0:T(8,128)(2,1)S(1)}, u32[]{:S(2)}, u32[]{:S(2)}) collective-permute-start(bf16[4,192,896]{2,1,0:T(8,128)(2,1)S(1)} %get-tuple-element.13), channel_id=1, source_target_pairs={{0,1},{1,0},{2,3},{3,2},{4,5},{5,4},{6,7},{7,6},{8,9},{9,8},{10,11... | collective-permute-start | bytes 4128776 | tf_op jit(solution)/shard_map/ppermute | solution.py:16
  118.1 17.3 %copy-start.4 = (bf16[192]{0:T(256)(128)(2,1)S(1)}, bf16[192]{0:T(256)(128)(2,1)}, u32[]{:S(2)}) copy-start(bf16[192]{0:T(256)(128)(2,1)} %param.24) | copy-start | bytes 1156
  118.1 17.5 %copy-start.3 = (f32[192]{0:T(256)S(1)}, f32[192]{0:T(256)}, u32[]{:S(2)}) copy-start(f32[192]{0:T(256)} %param.25) | copy-start | bytes 2308
  118.1 17.6 %copy-start.2 = (f32[2,21,21,192]{3,2,1,0:T(8,128)S(1)}, f32[2,21,21,192]{3,2,1,0:T(8,128)}, u32[]{:S(2)}) copy-start(f32[2,21,21,192]{3,2,1,0:T(8,128)} %copy-done.1) | copy-start | bytes 2032132
  118.4 8.1 %collective-permute-start.5 = (bf16[96,896]{1,0:T(8,128)(2,1)S(1)}, bf16[96,896]{1,0:T(8,128)(2,1)S(1)}, u32[]{:S(2)}, u32[]{:S(2)}) collective-permute-start(bf16[96,896]{1,0:T(8,128)(2,1)S(1)} %get-tuple-element.18), channel_id=1, source_target_pairs={{0,6},{2,0},{4,2},{6,4},{1,7},{3,1},{5,3},{7,5},{8,14},{10,8},{12,... | collective-permute-start | bytes 516104 | tf_op jit(solution)/shard_map/ppermute | solution.py:16
  122.9 9.7 %collective-permute-start.3 = (bf16[96,896]{1,0:T(8,128)(2,1)S(1)}, bf16[96,896]{1,0:T(8,128)(2,1)S(1)}, u32[]{:S(2)}, u32[]{:S(2)}) collective-permute-start(bf16[96,896]{1,0:T(8,128)(2,1)S(1)} %get-tuple-element.16), channel_id=1, source_target_pairs={{0,2},{2,4},{4,6},{6,0},{1,3},{3,5},{5,7},{7,1},{8,10},{10,12},{12... | collective-permute-start | bytes 516104 | tf_op jit(solution)/shard_map/ppermute | solution.py:16
  127.3 12.0 %collective-permute-start.6 = (bf16[192,896]{1,0:T(8,128)(2,1)}, bf16[192,896]{1,0:T(8,128)(2,1)S(1)}, u32[]{:S(2)}, u32[]{:S(2)}) collective-permute-start(bf16[192,896]{1,0:T(8,128)(2,1)} %pad_maximum_fusion.1), channel_id=1, source_target_pairs={{0,6},{2,0},{4,2},{6,4},{1,7},{3,1},{5,3},{7,5},{8,14},{10,8},{12,... | collective-permute-start | bytes 1032200 | tf_op jit(solution)/shard_map/ppermute | solution.py:16
  133.5 11.6 %collective-permute-start.4 = (bf16[192,896]{1,0:T(8,128)(2,1)}, bf16[192,896]{1,0:T(8,128)(2,1)S(1)}, u32[]{:S(2)}, u32[]{:S(2)}) collective-permute-start(bf16[192,896]{1,0:T(8,128)(2,1)} %pad_maximum_fusion), channel_id=1, source_target_pairs={{0,2},{2,4},{4,6},{6,0},{1,3},{3,5},{5,7},{7,1},{8,10},{10,12},{12... | collective-permute-start | bytes 1032200 | tf_op jit(solution)/shard_map/ppermute | solution.py:16
Sparse Core Ops, SparseCore 0:
  17.6 79.4 all-gather.4

commit v3 on v2

--- a/solution.py
+++ b/solution.py
@@ -10,6 +10,7 @@
 TP = ("x", "core")
 PER_DEV = 2
 KSIDE = 7
+DISTANCES = (2, 1, 3)
 
 
 def shift(block, axis, distance, size):
@@ -85,27 +86,26 @@
 
 
 def first_kernel(core, normed, b_up, weights, hidden, out, up, down, up_sem, down_sem):
-    units = up.shape[1]
+    ups = []
     pieces = up_sem.shape[0]
-    step = units // pieces
-    ups = []
+    step = up.shape[0] // pieces
     for p in range(pieces):
         span = pl.ds(p * step, step)
-        ups.append(
-            pltpu.make_async_copy(weights.at[0, :, span], up.at[:, span], up_sem.at[p])
-        )
+        ups.append(pltpu.make_async_copy(weights.at[0, span, :], up.at[span, :], up_sem.at[p]))
     for copy in ups:
         copy.start()
     downs = copy_down_rows(weights, down, down_sem, 1 - core[0])
     for copy in downs:
         copy.start()
-    for p in range(pieces):
-        span = pl.ds(p * step, step)
-        ups[p].wait()
-        pre = jnp.dot(normed[...], up[:, span], preferred_element_type=jnp.float32)
-        pre = pre + b_up[:, span]
+    for copy in ups:
+        copy.wait()
+    cells = normed.shape[0]
+    rows = cells // 4
+    for r in range(0, cells, rows):
+        pre = jnp.dot(normed[r : r + rows], up[...], preferred_element_type=jnp.float32)
+        pre = pre + b_up[...]
         act = 0.5 * pre * (1.0 + lax.erf(pre * 0.5**0.5))
-        hidden[:, span] = act.astype(hidden.dtype)
+        hidden[r : r + rows] = act.astype(hidden.dtype)
     for copy in downs:
         copy.wait()
     down_product(down, hidden[...], out)
@@ -120,22 +120,20 @@
     down_product(down, hidden[...], out)
 
 
-def pair_kernel(x, mine, other, own, ahead, behind, far_a, far_b):
+def pair_kernel(x, mine, other, own, *sent):
     def pair(distance):
         i = lax.rem(x[0] + distance, NX)
         return mine[i].astype(jnp.float32) + other[i].astype(jnp.float32)
 
-    half = far_a.shape[0]
     own[...] = pair(0)
-    ahead[...] = pair(1).astype(ahead.dtype)
-    behind[...] = pair(3).astype(behind.dtype)
-    far = pair(2)
-    far_a[...] = far[:half].astype(far_a.dtype)
-    far_b[...] = far[half:].astype(far_b.dtype)
-
-
-def last_kernel(own, ahead, behind, b_down, gamma, residual, out):
-    total = own[...] + ahead[...].astype(jnp.float32) + behind[...].astype(jnp.float32)
+    for distance, block in zip(DISTANCES, sent):
+        block[...] = pair(distance).astype(block.dtype)
+
+
+def last_kernel(own, first, second, third, b_down, gamma, residual, out):
+    total = own[...]
+    for block in (first, second, third):
+        total = total + block[...].astype(jnp.float32)
     scaled = gamma[...] * (total + b_down[...])
     rows = residual.shape[0]
     out[...] = (residual[...] + scaled.T[:rows]).astype(out.dtype)
@@ -157,7 +155,7 @@
         scratch_shapes=[
             pltpu.VMEM(weights.shape[1:], bf16),
             down,
-            pltpu.SemaphoreType.DMA((3,)),
+            pltpu.SemaphoreType.DMA((4,)),
             pltpu.SemaphoreType.DMA((NX,)),
         ],
         compiler_params=params,
@@ -173,21 +171,16 @@
         compiler_params=params,
         name="down_own",
     )(core, hidden, weights)
-    full = jax.ShapeDtypeStruct((width, cells), bf16)
-    half = jax.ShapeDtypeStruct((width // 2, cells), bf16)
-    own, ahead, behind, far_a, far_b = pl.pallas_call(
+    block = jax.ShapeDtypeStruct((width, cells), bf16)
+    own, *sent = pl.pallas_call(
         pair_kernel,
-        out_shape=(jax.ShapeDtypeStruct((width, cells), f32), full, full, half, half),
+        out_shape=(jax.ShapeDtypeStruct((width, cells), f32),) + (block,) * len(DISTANCES),
         in_specs=[whole(pltpu.SMEM), whole(), whole()],
-        out_specs=(whole(),) * 5,
+        out_specs=(whole(),) * (1 + len(DISTANCES)),
         compiler_params=params,
         name="pair",
     )(x, mine, other)
-    far_a = shift(far_a, "x", 1, NX)
-    far_b = shift(far_b, "x", -1, NX)
-    ahead = jnp.concatenate([ahead[: width // 2] + far_a, ahead[width // 2 :]])
-    behind = jnp.concatenate([behind[: width // 2], behind[width // 2 :] + far_b])
-    return own, shift(ahead, "x", 1, NX), shift(behind, "x", -1, NX)
+    return own, *(shift(block, "x", d, NX) for d, block in zip(DISTANCES, sent))
 
 
 def per_device(
@@ -226,15 +219,15 @@
         (conv_all - mean) / jnp.sqrt(var + 1e-6) * ln_gain.astype(f32)[:, None]
         + ln_bias.astype(f32)[:, None]
     ).astype(jnp.bfloat16).T
-    own, ahead, behind = mlp_sum(normed, weights, b_up, width)
+    sums = mlp_sum(normed, weights, b_up, width)
     result = pl.pallas_call(
         last_kernel,
         out_shape=jax.ShapeDtypeStruct((cells, width), jnp.bfloat16),
-        in_specs=[whole()] * 6,
+        in_specs=[whole()] * (len(sums) + 3),
         out_specs=whole(),
         compiler_params=pltpu.CompilerParams(vmem_limit_bytes=48 * 2**20),
         name="result",
-    )(own, ahead, behind, b_down.astype(f32)[:, None], gamma[:, None], block_in.reshape(cells, width))
+    )(*sums, b_down.astype(f32)[:, None], gamma[:, None], block_in.reshape(cells, width))
     return result.reshape(PER_DEV, side, side, width)
 
 

time: 156 us -> 154 us (0.987)
  other arithmetic: 22.2 us -> 45.8 us
  starting transfers between devices: 36.6 us -> 24.3 us
  waiting for transfers between devices: 21.3 us -> 9.83 us
    another operation x3, other arithmetic: 8.05 us -> 32.3 us
    ppermute x5 -> x4, starting transfers between devices: 24 us -> 11.8 us  [shift(): lax.ppermute(block, axis, [(i, (i + distance) % size) for i in range(size)])]
    all_gather x1, waiting for transfers between devices: 10.3 us -> 0.02 us  [gather_weights(): over_z = lax.all_gather(over_y, 'z', axis=2)]
    pallas_call x1, Pallas kernels: 7.85 us -> 5.72 us  [mlp_sum(): pl.pallas_call(first_kernel, out_shape=(jax.ShapeDtypeStruct((cells, unit...]
    ppermute x5 -> x4, waiting for transfers between devices: 10.9 us -> 9.78 us  [shift(): lax.ppermute(block, axis, [(i, (i + distance) % size) for i in range(size)])]
  transfers between devices with their start and end apart: 8 -> 7, of which waited for: 4 -> 2; matrix products, arithmetic and copies ran while one was open for 20% -> 37% of each run, Pallas kernels for 2% -> 2%
where the time goes in v3:
time: 154 us; the launch traced here: 152 us
  other arithmetic  45.8 us (30%)
  blocking collectives  32.5 us (21%)
  starting transfers between devices  24.3 us (16%)
  between operations  17.4 us (11%)
  local copies, waits for them, and re-layouts  12.1 us (8%)
  Pallas kernels  9.89 us (6%)
  waiting for transfers between devices  9.83 us (6%)
    another operation x3, other arithmetic  32.3 us
    all_gather x1, blocking collectives, per_device(): conv_all = lax.all_gather(conv_t, TP, axis=0, tiled=True).astype(f32)  22.3 us
    ppermute x4, starting transfers between devices, shift(): lax.ppermute(block, axis, [(i, (i + distance) % size) for i in range(size)])  11.8 us
    all_gather x1, blocking collectives, gather_weights(): over_y = lax.all_gather(both, 'y', axis=1)  10.2 us
    ppermute x4, waiting for transfers between devices, shift(): lax.ppermute(block, axis, [(i, (i + distance) % size) for i in range(size)])  9.78 us
    ppermute x1, starting transfers between devices, regroup(): lax.ppermute(crop(target - 1), SEQ, [(i + 1, i) for i in range(count - 1)])  8.98 us
    pallas_call x1, Pallas kernels, mlp_sum(): pl.pallas_call(first_kernel, out_shape=(jax.ShapeDtypeStruct((cells, unit...  5.72 us
    transpose x1, other arithmetic, per_device(): normed = ((conv_all - mean) / jnp.sqrt(var + 1e-06) * ln_gain.astype(f32)...  4.18 us
  transfers between devices with their start and end apart: 7, of which 2 were waited for; matrix products, arithmetic and copies ran while one was open for 37% of the time, Pallas kernels for 2%

profile of v3, /device:TPU:25, one launch (start us, length us, event | category | flops | bytes accessed | tf_op | source)
XLA Modules:
  0.0 151.9 jit_solution(1406974484861646688)
XLA Ops:
  7.3 10.2 %all-gather = bf16[2,96,768]{2,1,0:T(8,128)(2,1)} all-gather(bf16[2,24,768]{2,1,0:T(8,128)(2,1)S(1)} %pad_maximum_fusion), channel_id=2, replica_groups=mesh['y'=4,'z'=16,'x'=4,'core'=2] {'y'}, dimensions={1}, use_global_device_ids=true | all-gather | bytes 368640 | tf_op jit(solution)/shard_map/all_gather | solution.py:22
  17.5 1.4 fusion.112
  20.2 1.4 dynamic-slice_bitcast_fusion.1
  21.6 3.5 %collective-permute-start = (bf16[21,21,192]{2,1,0:T(8,128)(2,1)S(1)}, bf16[21,21,192]{2,1,0:T(8,128)(2,1)S(1)}, u32[]{:S(2)}, u32[]{:S(2)}) collective-permute-start(bf16[21,21,192]{2,1,0:T(8,128)(2,1)S(1)} %get-tuple-element.19), channel_id=1, source_target_pairs={{0,8},{8,16},{16,24},{24,32},{32,40},{40,48},{48,56},{56,64},{64,7... | collective-permute-start | bytes 508040 | tf_op jit(solution)/shard_map/ppermute | solution.py:41
  25.1 9.0 %collective-permute-start.1 = (bf16[21,21,192]{2,1,0:T(8,128)(2,1)S(1)}, bf16[21,21,192]{2,1,0:T(8,128)(2,1)S(1)}, u32[]{:S(2)}, u32[]{:S(2)}) collective-permute-start(bf16[21,21,192]{2,1,0:T(8,128)(2,1)S(1)} %get-tuple-element.20), channel_id=1, source_target_pairs={{8,0},{16,8},{24,16},{32,24},{40,32},{48,40},{56,48},{64,56},{72,6... | collective-permute-start | bytes 508040 | tf_op jit(solution)/shard_map/ppermute | solution.py:44
  41.8 0.9 dynamic-slice_convert_fusion
  43.0 1.4 fusion.106
  44.4 1.1 convert_add_fusion
  45.5 32.1 %fusion.101 = f16[2,21,21,192]{3,2,1,0:T(8,128)(2,1)S(1)} fusion(f32[2,21,21,192]{3,2,1,0:T(8,128)} %convert_add_fusion, f32[192]{0:T(256)S(1)} %dynamic-slice_convert_fusion.2, f32[192]{0:T(256)S(1)} %bitcast.88, f32[192]{0:T(256)S(1)} %bitcast.89, f32[192]{0:T(256)S(1)} %bitcast.90, f32[192]{0:T(256)S(1)} %bitcast.91, f32[192]{0:T(256)S(1)} %bitcast.92, ...), kind=kLoop, calls=%fused_computation.151 | loop fusion | flops 16765056 | bytes 1054464 | tf_op jit(solution)/shard_map/convert.4
  78.4 22.3 %all-gather.6 = f16[1536,896]{1,0:T(8,128)(2,1)} all-gather(f16[192,896]{1,0:T(8,128)(2,1)S(1)} %copy.27), channel_id=1, replica_groups=mesh['y'=4,'z'=16,'x'=4,'core'=2] {'x','core'}, dimensions={0}, use_global_device_ids=true | all-gather | bytes 3096576 | tf_op jit(solution)/shard_map/all_gather | solution.py:215
  100.7 4.0 %copy.28 = f16[1536,896]{0,1:T(8,128)(2,1)S(1)} copy(f16[1536,896]{1,0:T(8,128)(2,1)} %all-gather.6) | data formatting | bytes 5505024 | tf_op jit(solution)/shard_map/all_gather | solution.py:215
  105.2 0.9 fusion.2
  106.3 4.2 %fusion.6.normed = bf16[896,1536]{1,0:T(8,128)(2,1)S(1)} fusion(f16[1536,896]{0,1:T(8,128)(2,1)} %copy-done, f32[1536]{0:T(1024)S(1)} %convert_element_type.43, f32[1536]{0:T(1024)S(1)} %convert_element_type.42, f32[896]{0:T(1024)S(1)} %add_sqrt_fusion, f32[896]{0:T(1024)S(1)} %broadcast_multiply_fusion), kind=kLoop, calls=%fused_computation.56 | loop fusion | flops 8257536 | bytes 5524480 | tf_op jit(solution)/shard_map/transpose | solution.py:221
  110.5 5.7 %up_and_down.1 = (bf16[896,768]{1,0:T(8,128)(2,1)S(1)}, bf16[4,192,896]{2,1,0:T(8,128)(2,1)S(1)}) custom-call(s32[1]{0:T(128)} %bitcast.1.core, bf16[896,1536]{1,0:T(8,128)(2,1)S(1)} %fusion.6.normed, f32[1,768]{1,0:T(1,128)S(1)} %reshape.150.b_up, bf16[2,1536,768]{2,1,0:T(8,128)(2,1)} %bitcast.82), custom_call_target="tpu_custom_call" | custom-call | tf_op jit(solution)/shard_map/up_and_down/pallas_call | solution.py:150
  116.2 2.2 %collective-permute-start.2 = (bf16[4,192,896]{2,1,0:T(8,128)(2,1)S(1)}, bf16[4,192,896]{2,1,0:T(8,128)(2,1)S(1)}, u32[]{:S(2)}, u32[]{:S(2)}) collective-permute-start(bf16[4,192,896]{2,1,0:T(8,128)(2,1)S(1)} %get-tuple-element.12), channel_id=1, source_target_pairs={{0,1},{1,0},{2,3},{3,2},{4,5},{5,4},{6,7},{7,6},{8,9},{9,8},{10,11... | collective-permute-start | bytes 4128776 | tf_op jit(solution)/shard_map/ppermute | solution.py:17
  118.5 2.7 %down_own.1.mine = bf16[4,192,896]{2,1,0:T(8,128)(2,1)S(1)} custom-call(s32[1]{0:T(128)} %bitcast.1.core, bf16[896,768]{1,0:T(8,128)(2,1)S(1)} %get-tuple-element.11.hidden, bf16[2,1536,768]{2,1,0:T(8,128)(2,1)} %bitcast.83), custom_call_target="tpu_custom_call" | custom-call | tf_op jit(solution)/shard_map/down_own/pallas_call | solution.py:165
  121.2 1.1 pair.1
  122.3 3.1 %collective-permute-start.3 = (bf16[192,896]{1,0:T(8,128)(2,1)}, bf16[192,896]{1,0:T(8,128)(2,1)S(1)}, u32[]{:S(2)}, u32[]{:S(2)}) collective-permute-start(bf16[192,896]{1,0:T(8,128)(2,1)} %get-tuple-element.14), channel_id=1, source_target_pairs={{0,4},{2,6},{4,0},{6,2},{1,5},{3,7},{5,1},{7,3},{8,12},{10,14},{12... | collective-permute-start | bytes 1032200 | tf_op jit(solution)/shard_map/ppermute | solution.py:17
  125.4 1.9 %collective-permute-start.4 = (bf16[192,896]{1,0:T(8,128)(2,1)}, bf16[192,896]{1,0:T(8,128)(2,1)S(1)}, u32[]{:S(2)}, u32[]{:S(2)}) collective-permute-start(bf16[192,896]{1,0:T(8,128)(2,1)} %get-tuple-element.15), channel_id=1, source_target_pairs={{0,2},{2,4},{4,6},{6,0},{1,3},{3,5},{5,7},{7,1},{8,10},{10,12},{12... | collective-permute-start | bytes 1032200 | tf_op jit(solution)/shard_map/ppermute | solution.py:17
  127.3 4.6 %collective-permute-start.5 = (bf16[192,896]{1,0:T(8,128)(2,1)S(1)}, bf16[192,896]{1,0:T(8,128)(2,1)S(1)}, u32[]{:S(2)}, u32[]{:S(2)}) collective-permute-start(bf16[192,896]{1,0:T(8,128)(2,1)S(1)} %get-tuple-element.16), channel_id=1, source_target_pairs={{0,6},{2,0},{4,2},{6,4},{1,7},{3,1},{5,3},{7,5},{8,14},{10,8},{12,... | collective-permute-start | bytes 1032200 | tf_op jit(solution)/shard_map/ppermute | solution.py:17
  132.2 1.3 add.317.residual
  133.5 1.7 %collective-permute-done.3.first = bf16[192,896]{1,0:T(8,128)(2,1)S(1)} collective-permute-done((bf16[192,896]{1,0:T(8,128)(2,1)}, bf16[192,896]{1,0:T(8,128)(2,1)S(1)}, u32[]{:S(2)}, u32[]{:S(2)}) %collective-permute-start.3) | collective-permute-done | bytes 344096 | tf_op jit(solution)/shard_map/ppermute | solution.py:17
  135.3 8.0 %collective-permute-done.4.second = bf16[192,896]{1,0:T(8,128)(2,1)S(1)} collective-permute-done((bf16[192,896]{1,0:T(8,128)(2,1)}, bf16[192,896]{1,0:T(8,128)(2,1)S(1)}, u32[]{:S(2)}, u32[]{:S(2)}) %collective-permute-start.4) | collective-permute-done | bytes 344096 | tf_op jit(solution)/shard_map/ppermute | solution.py:17
  143.9 1.1 copy.31
  (42 shorter events, 8.7 us)
Async XLA Ops:
  6.5 104.0 %all-gather.5.cloned.1.call-start = ((), (), s32[]{:S(2)}) async-start(), calls=%async_computation | async-start | bytes 5013504 | tf_op jit(solution)/shard_map/all_gather | solution.py:23
  21.6 21.4 %collective-permute-start = (bf16[21,21,192]{2,1,0:T(8,128)(2,1)S(1)}, bf16[21,21,192]{2,1,0:T(8,128)(2,1)S(1)}, u32[]{:S(2)}, u32[]{:S(2)}) collective-permute-start(bf16[21,21,192]{2,1,0:T(8,128)(2,1)S(1)} %get-tuple-element.19), channel_id=1, source_target_pairs={{0,8},{8,16},{16,24},{24,32},{32,40},{40,48},{48,56},{56,64},{64,7... | collective-permute-start | bytes 508040 | tf_op jit(solution)/shard_map/ppermute | solution.py:41
  25.1 17.9 %collective-permute-start.1 = (bf16[21,21,192]{2,1,0:T(8,128)(2,1)S(1)}, bf16[21,21,192]{2,1,0:T(8,128)(2,1)S(1)}, u32[]{:S(2)}, u32[]{:S(2)}) collective-permute-start(bf16[21,21,192]{2,1,0:T(8,128)(2,1)S(1)} %get-tuple-element.20), channel_id=1, source_target_pairs={{8,0},{16,8},{24,16},{32,24},{40,32},{48,40},{56,48},{64,56},{72,6... | collective-permute-start | bytes 508040 | tf_op jit(solution)/shard_map/ppermute | solution.py:44
  104.7 1.5 %copy-start = (f16[1536,896]{0,1:T(8,128)(2,1)}, f16[1536,896]{0,1:T(8,128)(2,1)S(1)}, u32[]{:S(2)}) copy-start(f16[1536,896]{0,1:T(8,128)(2,1)S(1)} %copy.28) | copy-start | bytes 8257540
  116.2 5.0 %collective-permute-start.2 = (bf16[4,192,896]{2,1,0:T(8,128)(2,1)S(1)}, bf16[4,192,896]{2,1,0:T(8,128)(2,1)S(1)}, u32[]{:S(2)}, u32[]{:S(2)}) collective-permute-start(bf16[4,192,896]{2,1,0:T(8,128)(2,1)S(1)} %get-tuple-element.12), channel_id=1, source_target_pairs={{0,1},{1,0},{2,3},{3,2},{4,5},{5,4},{6,7},{7,6},{8,9},{9,8},{10,11... | collective-permute-start | bytes 4128776 | tf_op jit(solution)/shard_map/ppermute | solution.py:17
  118.5 13.4 %copy-start.2 = (bf16[192]{0:T(256)(128)(2,1)S(1)}, bf16[192]{0:T(256)(128)(2,1)}, u32[]{:S(2)}) copy-start(bf16[192]{0:T(256)(128)(2,1)} %param.24) | copy-start | bytes 1156
  118.5 13.6 %copy-start.1 = (f32[192]{0:T(256)S(1)}, f32[192]{0:T(256)}, u32[]{:S(2)}) copy-start(f32[192]{0:T(256)} %param.25) | copy-start | bytes 2308
  122.3 13.0 %collective-permute-start.3 = (bf16[192,896]{1,0:T(8,128)(2,1)}, bf16[192,896]{1,0:T(8,128)(2,1)S(1)}, u32[]{:S(2)}, u32[]{:S(2)}) collective-permute-start(bf16[192,896]{1,0:T(8,128)(2,1)} %get-tuple-element.14), channel_id=1, source_target_pairs={{0,4},{2,6},{4,0},{6,2},{1,5},{3,7},{5,1},{7,3},{8,12},{10,14},{12... | collective-permute-start | bytes 1032200 | tf_op jit(solution)/shard_map/ppermute | solution.py:17
  125.4 17.9 %collective-permute-start.4 = (bf16[192,896]{1,0:T(8,128)(2,1)}, bf16[192,896]{1,0:T(8,128)(2,1)S(1)}, u32[]{:S(2)}, u32[]{:S(2)}) collective-permute-start(bf16[192,896]{1,0:T(8,128)(2,1)} %get-tuple-element.15), channel_id=1, source_target_pairs={{0,2},{2,4},{4,6},{6,0},{1,3},{3,5},{5,7},{7,1},{8,10},{10,12},{12... | collective-permute-start | bytes 1032200 | tf_op jit(solution)/shard_map/ppermute | solution.py:17
  127.3 15.9 %collective-permute-start.5 = (bf16[192,896]{1,0:T(8,128)(2,1)S(1)}, bf16[192,896]{1,0:T(8,128)(2,1)S(1)}, u32[]{:S(2)}, u32[]{:S(2)}) collective-permute-start(bf16[192,896]{1,0:T(8,128)(2,1)S(1)} %get-tuple-element.16), channel_id=1, source_target_pairs={{0,6},{2,0},{4,2},{6,4},{1,7},{3,1},{5,3},{7,5},{8,14},{10,8},{12,... | collective-permute-start | bytes 1032200 | tf_op jit(solution)/shard_map/ppermute | solution.py:17
Sparse Core Ops, SparseCore 0:
  17.6 79.2 all-gather.4

commit v4 on v3

--- a/solution.py
+++ b/solution.py
@@ -24,12 +24,9 @@
     return over_z.reshape(2, NY * NZ * w_up.shape[0], w_up.shape[1])
 
 
-def regroup(slots, seq_index, first_crop):
+def exchange(slots, seq_index, first_crop):
     count = NY * NZ
     first = first_crop[seq_index]
-    limit = jnp.where(
-        seq_index + 1 < count, first_crop[jnp.minimum(seq_index + 1, count - 1)], PER_DEV * count
-    )
     last_slot = slots.shape[0] - 1
 
     def crop(number):
@@ -38,23 +35,91 @@
         )
 
     target = PER_DEV * seq_index
-    up = lax.ppermute(
+    before = lax.ppermute(
         crop(target + PER_DEV), SEQ, [(i, i + 1) for i in range(count - 1)]
     )
-    down = lax.ppermute(crop(target - 1), SEQ, [(i + 1, i) for i in range(count - 1)])
-    crop_a = jnp.where(first <= target, crop(target), up)
-    crop_b = jnp.where(limit > target + 1, crop(target + 1), down)
-    return jnp.stack([crop_a, crop_b])
-
-
-def depthwise(block_in, weight, bias):
+    after = lax.ppermute(crop(target - 1), SEQ, [(i + 1, i) for i in range(count - 1)])
+    return before, after
+
+
+def conv_kernel(
+    seq, first_crop, crop_counts, slots, before, after, table, block_in, conv, padded, shifted, taps
+):
+    f32 = jnp.float32
     side = block_in.shape[1]
-    padded = jnp.pad(block_in, ((0, 0), (3, 3), (3, 3), (0, 0)))
-    total = jnp.zeros_like(block_in)
-    for a in range(KSIDE):
+    shards = first_crop.shape[0]
+    margin = KSIDE // 2
+    here = seq[0]
+    first = first_crop[here]
+    limit = jnp.where(
+        here + 1 < shards, first_crop[jnp.minimum(here + 1, shards - 1)], PER_DEV * shards
+    )
+    tile_at = KSIDE * KSIDE
+    bias = table[tile_at + 3 : tile_at + 4, :].astype(f32)
+    for t in range(KSIDE * KSIDE):
+        taps[t] = jnp.broadcast_to(table[t : t + 1, :].astype(f32), taps.shape[1:])
+    padded[...] = jnp.zeros_like(padded)
+    shifted[...] = jnp.zeros_like(shifted)
+    for n in range(PER_DEV):
+        target = PER_DEV * here + n
+
+        def image(i, carry):
+            start, begin = carry
+            return start + crop_counts[i], jnp.where(start <= target, start, begin)
+
+        _, begin = lax.fori_loop(0, crop_counts.shape[0], image, (jnp.int32(0), jnp.int32(0)))
+        place = target - begin
+        tile = jnp.zeros_like(bias)
+        for p in range(3):
+            row = table[tile_at + p : tile_at + p + 1, :].astype(f32)
+            tile = jnp.where(place == p, row, tile)
+        mine = slots[jnp.clip(target - first, 0, slots.shape[0] - 1)].astype(f32)
+        received = (before if n == 0 else after)[...].astype(f32)
+        held = (first <= target) & (target < limit)
+        crop = jnp.where(held, mine, received) + tile
+        block_in[n] = crop
+        padded[:, margin : margin + side, :] = crop
         for b in range(KSIDE):
-            total = total + padded[:, a : a + side, b : b + side, :] * weight[a * KSIDE + b]
-    return total + bias
+            shifted[b, n, margin : margin + side] = padded[:, b : b + shifted.shape[3], :]
+    columns, width = shifted.shape[3:]
+    groups = side // 3
+
+    def three_rows(g, _):
+        n, top = lax.div(g, groups), lax.rem(g, groups) * 3
+        sums = [jnp.zeros((columns // 8, 8, width), f32) for _ in range(3)]
+        for b in range(KSIDE):
+            for r in range(KSIDE + 2):
+                row = shifted[b, n, top + r].reshape(columns // 8, 8, width)
+                for o in range(3):
+                    if 0 <= r - o < KSIDE:
+                        sums[o] = sums[o] + row * taps[(r - o) * KSIDE + b][None]
+        for o in range(3):
+            conv[n, top + o] = sums[o].reshape(columns, width) + bias
+        return 0
+
+    lax.fori_loop(0, PER_DEV * groups, three_rows, 0)
+
+
+def depthwise(seq_index, first_crop, crop_counts, slots, before, after, table):
+    f32 = jnp.float32
+    side, width = slots.shape[1], slots.shape[3]
+    columns = 24
+    return pl.pallas_call(
+        conv_kernel,
+        out_shape=(
+            jax.ShapeDtypeStruct((PER_DEV, side, side, width), f32),
+            jax.ShapeDtypeStruct((PER_DEV, side, columns, width), f32),
+        ),
+        in_specs=[whole(pltpu.SMEM)] * 3 + [whole()] * 4,
+        out_specs=(whole(), whole()),
+        scratch_shapes=[
+            pltpu.VMEM((side, columns + 8, width), f32),
+            pltpu.VMEM((KSIDE, PER_DEV, side + 6, columns, width), f32),
+            pltpu.VMEM((KSIDE * KSIDE, 8, width), f32),
+        ],
+        compiler_params=pltpu.CompilerParams(vmem_limit_bytes=48 * 2**20),
+        name="conv",
+    )(seq_index.astype(jnp.int32).reshape(1), first_crop, crop_counts, slots, before, after, table)
 
 
 def whole(space=pltpu.VMEM):
@@ -197,21 +262,16 @@
     def channels(array):
         return lax.dynamic_slice_in_dim(array, start, width, array.ndim - 1)
 
-    crops = regroup(channels(crop_features), seq_index, first_crop)
-    crop_ids = PER_DEV * seq_index + jnp.arange(PER_DEV, dtype=jnp.int32)
-    image_start = jnp.cumsum(crop_counts) - crop_counts
-    begin = jnp.max(
-        jnp.where(image_start[None, :] <= crop_ids[:, None], image_start[None, :], 0), axis=1
-    )
-    choose = (crop_ids - begin)[:, None] == jnp.arange(tile_embed.shape[0])[None, :]
-    tile = jnp.sum(
-        jnp.where(choose[:, :, None], channels(tile_embed).astype(f32)[None], 0.0), axis=1
-    )
-    block_in = crops.astype(f32) + tile[:, None, None, :]
-    conv = depthwise(block_in, channels(dw_weight).astype(f32), channels(conv_bias).astype(f32))
+    slots = channels(crop_features)
+    before, after = exchange(slots, seq_index, first_crop)
+    table = channels(jnp.concatenate([dw_weight, tile_embed, conv_bias[None, :]]))
+    block_in, conv = depthwise(
+        seq_index, first_crop, crop_counts, slots, before, after, table
+    )
     cells = PER_DEV * side * side
     padding = -cells % 128
-    conv_t = jnp.pad(conv.reshape(cells, width), ((0, padding), (0, 0))).T.astype(jnp.float16)
+    conv_t = jnp.pad(conv[:, :, :side].reshape(cells, width), ((0, padding), (0, 0))).T
+    conv_t = conv_t.astype(jnp.float16)
     conv_all = lax.all_gather(conv_t, TP, axis=0, tiled=True).astype(f32)
     mean = jnp.mean(conv_all, axis=0, keepdims=True)
     var = jnp.mean((conv_all - mean) ** 2, axis=0, keepdims=True)

time: 154 us -> 150 us (0.974)
  other arithmetic: 45.8 us -> 8.65 us
  waiting for transfers between devices: 9.83 us -> 23.5 us
  starting transfers between devices: 24.3 us -> 34 us
  Pallas kernels: 9.89 us -> 19.3 us
  local copies, waits for them, and re-layouts: 12.1 us -> 14.6 us
  between operations: 17.4 us -> 15 us
    another operation x4 -> x1, other arithmetic: 33.7 us -> 0.09 us
    all_gather x1, waiting for transfers between devices: 0.02 us -> 14 us  [gather_weights(): over_z = lax.all_gather(over_y, 'z', axis=2)]
    ppermute x4, starting transfers between devices: 11.8 us -> 21.5 us  [shift(): lax.ppermute(block, axis, [(i, (i + distance) % size) for i in range(size)])]
    pallas_call x0 -> x1, Pallas kernels: none -> 8.37 us  [depthwise(): pl.pallas_call(conv_kernel, out_shape=(jax.ShapeDtypeStruct((PER_DEV, sid...]
    unnamed x6 -> x14, local copies, waits for them, and re-layouts: 0.25 us -> 2.63 us
    convert_element_type x3 -> x0, other arithmetic: 2.38 us -> none  [the longest x1 0.86 us: per_device(): channels(dw_weight).astype(f32)]
  transfers between devices with their start and end apart: 7 -> 7, of which waited for: 2 -> 3; matrix products, arithmetic and copies ran while one was open for 37% -> 13% of each run, Pallas kernels for 2% -> 8%
where the time goes in v4:
time: 150 us; the launch traced here: 148 us
  starting transfers between devices  34 us (23%)
  blocking collectives  32.6 us (22%)
  waiting for transfers between devices  23.5 us (16%)
  Pallas kernels  19.3 us (13%)
  between operations  15 us (10%)
  local copies, waits for them, and re-layouts  14.6 us (10%)
  other arithmetic  8.65 us (6%)
    all_gather x1, blocking collectives, per_device(): conv_all = lax.all_gather(conv_t, TP, axis=0, tiled=True).astype(f32)  22.4 us
    ppermute x4, starting transfers between devices, shift(): lax.ppermute(block, axis, [(i, (i + distance) % size) for i in range(size)])  21.5 us
    all_gather x1, waiting for transfers between devices, gather_weights(): over_z = lax.all_gather(over_y, 'z', axis=2)  14 us
    all_gather x1, blocking collectives, gather_weights(): over_y = lax.all_gather(both, 'y', axis=1)  10.2 us
    ppermute x4, waiting for transfers between devices, shift(): lax.ppermute(block, axis, [(i, (i + distance) % size) for i in range(size)])  9.48 us
    ppermute x1, starting transfers between devices, exchange(): lax.ppermute(crop(target - 1), SEQ, [(i + 1, i) for i in range(count - 1)])  8.98 us
    pallas_call x1, Pallas kernels, depthwise(): pl.pallas_call(conv_kernel, out_shape=(jax.ShapeDtypeStruct((PER_DEV, sid...  8.37 us
    pallas_call x1, Pallas kernels, mlp_sum(): pl.pallas_call(first_kernel, out_shape=(jax.ShapeDtypeStruct((cells, unit...  5.71 us
  transfers between devices with their start and end apart: 7, of which 3 were waited for; matrix products, arithmetic and copies ran while one was open for 13% of the time, Pallas kernels for 8%

profile of v4, /device:TPU:25, one launch (start us, length us, event | category | flops | bytes accessed | tf_op | source)
XLA Modules:
  0.0 147.6 jit_solution(10509072519461954758)
XLA Ops:
  7.3 10.2 %all-gather = bf16[2,96,768]{2,1,0:T(8,128)(2,1)} all-gather(bf16[2,24,768]{2,1,0:T(8,128)(2,1)S(1)} %pad_maximum_fusion), channel_id=2, replica_groups=mesh['y'=4,'z'=16,'x'=4,'core'=2] {'y'}, dimensions={1}, use_global_device_ids=true | all-gather | bytes 368640 | tf_op jit(solution)/shard_map/all_gather | solution.py:22
  17.5 1.2 dynamic_slice.19
  20.1 1.3 dynamic-slice_bitcast_fusion
  21.5 3.5 %collective-permute-start = (bf16[21,21,192]{2,1,0:T(8,128)(2,1)S(1)}, bf16[21,21,192]{2,1,0:T(8,128)(2,1)S(1)}, u32[]{:S(2)}, u32[]{:S(2)}) collective-permute-start(bf16[21,21,192]{2,1,0:T(8,128)(2,1)S(1)} %get-tuple-element.22), channel_id=1, source_target_pairs={{0,8},{8,16},{16,24},{24,32},{32,40},{40,48},{48,56},{56,64},{64,7... | collective-permute-start | bytes 508040 | tf_op jit(solution)/shard_map/ppermute | solution.py:38
  25.0 9.0 %collective-permute-start.1 = (bf16[21,21,192]{2,1,0:T(8,128)(2,1)S(1)}, bf16[21,21,192]{2,1,0:T(8,128)(2,1)S(1)}, u32[]{:S(2)}, u32[]{:S(2)}) collective-permute-start(bf16[21,21,192]{2,1,0:T(8,128)(2,1)S(1)} %get-tuple-element.21), channel_id=1, source_target_pairs={{8,0},{16,8},{24,16},{32,24},{40,32},{48,40},{56,48},{64,56},{72,6... | collective-permute-start | bytes 508040 | tf_op jit(solution)/shard_map/ppermute | solution.py:41
  34.7 0.9 fusion.8.table
  37.6 1.6 %constant_dynamic-slice_fusion.slots = bf16[3,21,21,192]{3,2,1,0:T(8,128)(2,1)S(1)} fusion(bf16[3,21,21,1536]{3,2,1,0:T(8,128)(2,1)} %param.13, s32[]{:T(128)S(6)} %select_n.12), kind=kLoop, calls=%fused_computation.21 | loop fusion | bytes 1016068 | tf_op jit(solution)/shard_map/dynamic_slice | solution.py:263
  40.6 8.4 %conv.1 = (f32[2,21,21,192]{3,2,1,0:T(8,128)S(1)}, f32[2,21,24,192]{3,2,1,0:T(8,128)S(1)}) custom-call(s32[1]{0:T(128)} %bitcast.2.seq, s32[64]{0:T(128)S(1)} %copy-done.2, s32[64]{0:T(128)S(1)} %copy-done.3, bf16[3,21,21,192]{3,2,1,0:T(8,128)(2,1)S(1)} %constant_dynamic-slice_fusion.slots, bf16[21,21,192]{2,1,0:T(8,128)(2,1)S(1)} %collective-permute-done.before, ...), custom_call_target="tpu_custom_call" | custom-call | tf_op jit(solution)/shard_map/conv/pallas_call | solution.py:107
  48.9 1.0 copy-done
  50.8 22.4 %all-gather.6 = f16[1536,896]{1,0:T(8,128)(2,1)} all-gather(f16[192,896]{1,0:T(8,128)(2,1)S(1)} %copy.18), channel_id=1, replica_groups=mesh['y'=4,'z'=16,'x'=4,'core'=2] {'x','core'}, dimensions={0}, use_global_device_ids=true | all-gather | bytes 3096576 | tf_op jit(solution)/shard_map/all_gather | solution.py:275
  73.2 4.1 %copy.19 = f16[1536,896]{0,1:T(8,128)(2,1)S(1)} copy(f16[1536,896]{1,0:T(8,128)(2,1)} %all-gather.6) | data formatting | bytes 5505024 | tf_op jit(solution)/shard_map/all_gather | solution.py:275
  78.8 4.2 %fusion.6.normed = bf16[896,1536]{1,0:T(8,128)(2,1)S(1)} fusion(f16[1536,896]{0,1:T(8,128)(2,1)} %copy-done.4, f32[1536]{0:T(1024)S(1)} %convert_element_type.23, f32[1536]{0:T(1024)S(1)} %convert_element_type.22, f32[896]{0:T(1024)S(1)} %add_sqrt_fusion, f32[896]{0:T(1024)S(1)} %broadcast_multiply_fusion), kind=kLoop, calls=%fused_computation.8 | loop fusion | flops 8257536 | bytes 5524480 | tf_op jit(solution)/shard_map/transpose | solution.py:281
  83.0 14.0 %all-gather.5.cloned.1.call-done = bf16[2,4,384,768]{3,2,1,0:T(8,128)(2,1)} async-done(((bf16[2,4,24,768]{3,2,1,0:T(8,128)(2,1)}), bf16[2,4,384,768]{3,2,1,0:T(8,128)(2,1)}) %all-gather.5.cloned.1.call-update) | async-done | bytes 4718608 | tf_op jit(solution)/shard_map/all_gather | solution.py:23
  97.0 5.7 %up_and_down.1 = (bf16[896,768]{1,0:T(8,128)(2,1)S(1)}, bf16[4,192,896]{2,1,0:T(8,128)(2,1)S(1)}) custom-call(s32[1]{0:T(128)} %bitcast.1.core, bf16[896,1536]{1,0:T(8,128)(2,1)S(1)} %fusion.6.normed, f32[1,768]{1,0:T(1,128)S(1)} %reshape.43.b_up, bf16[2,1536,768]{2,1,0:T(8,128)(2,1)} %bitcast.20), custom_call_target="tpu_custom_call" | custom-call | tf_op jit(solution)/shard_map/up_and_down/pallas_call | solution.py:215
  102.7 10.4 %collective-permute-start.2 = (bf16[4,192,896]{2,1,0:T(8,128)(2,1)S(1)}, bf16[4,192,896]{2,1,0:T(8,128)(2,1)S(1)}, u32[]{:S(2)}, u32[]{:S(2)}) collective-permute-start(bf16[4,192,896]{2,1,0:T(8,128)(2,1)S(1)} %get-tuple-element.15), channel_id=1, source_target_pairs={{0,1},{1,0},{2,3},{3,2},{4,5},{5,4},{6,7},{7,6},{8,9},{9,8},{10,11... | collective-permute-start | bytes 4128776 | tf_op jit(solution)/shard_map/ppermute | solution.py:17
  113.2 2.8 %down_own.1.mine = bf16[4,192,896]{2,1,0:T(8,128)(2,1)S(1)} custom-call(s32[1]{0:T(128)} %bitcast.1.core, bf16[896,768]{1,0:T(8,128)(2,1)S(1)} %get-tuple-element.14.hidden, bf16[2,1536,768]{2,1,0:T(8,128)(2,1)} %bitcast.21), custom_call_target="tpu_custom_call" | custom-call | tf_op jit(solution)/shard_map/down_own/pallas_call | solution.py:230
  116.0 1.1 pair.1
  117.1 4.6 %collective-permute-start.3 = (bf16[192,896]{1,0:T(8,128)(2,1)}, bf16[192,896]{1,0:T(8,128)(2,1)S(1)}, u32[]{:S(2)}, u32[]{:S(2)}) collective-permute-start(bf16[192,896]{1,0:T(8,128)(2,1)} %get-tuple-element.17), channel_id=1, source_target_pairs={{0,4},{2,6},{4,0},{6,2},{1,5},{3,7},{5,1},{7,3},{8,12},{10,14},{12... | collective-permute-start | bytes 1032200 | tf_op jit(solution)/shard_map/ppermute | solution.py:17
  121.6 2.4 %collective-permute-start.4 = (bf16[192,896]{1,0:T(8,128)(2,1)}, bf16[192,896]{1,0:T(8,128)(2,1)S(1)}, u32[]{:S(2)}, u32[]{:S(2)}) collective-permute-start(bf16[192,896]{1,0:T(8,128)(2,1)} %get-tuple-element.18), channel_id=1, source_target_pairs={{0,2},{2,4},{4,6},{6,0},{1,3},{3,5},{5,7},{7,1},{8,10},{10,12},{12... | collective-permute-start | bytes 1032200 | tf_op jit(solution)/shard_map/ppermute | solution.py:17
  124.0 4.1 %collective-permute-start.5 = (bf16[192,896]{1,0:T(8,128)(2,1)}, bf16[192,896]{1,0:T(8,128)(2,1)}, u32[]{:S(2)}, u32[]{:S(2)}) collective-permute-start(bf16[192,896]{1,0:T(8,128)(2,1)} %get-tuple-element.19), channel_id=1, source_target_pairs={{0,6},{2,0},{4,2},{6,4},{1,7},{3,1},{5,3},{7,5},{8,14},{10,8},{12,... | collective-permute-start | bytes 1032200 | tf_op jit(solution)/shard_map/ppermute | solution.py:17
  128.6 1.7 %collective-permute-done.3.first = bf16[192,896]{1,0:T(8,128)(2,1)S(1)} collective-permute-done((bf16[192,896]{1,0:T(8,128)(2,1)}, bf16[192,896]{1,0:T(8,128)(2,1)S(1)}, u32[]{:S(2)}, u32[]{:S(2)}) %collective-permute-start.3) | collective-permute-done | bytes 344096 | tf_op jit(solution)/shard_map/ppermute | solution.py:17
  130.3 7.7 %collective-permute-done.4.second = bf16[192,896]{1,0:T(8,128)(2,1)S(1)} collective-permute-done((bf16[192,896]{1,0:T(8,128)(2,1)}, bf16[192,896]{1,0:T(8,128)(2,1)S(1)}, u32[]{:S(2)}, u32[]{:S(2)}) %collective-permute-start.4) | collective-permute-done | bytes 344096 | tf_op jit(solution)/shard_map/ppermute | solution.py:17
  138.0 1.4 result.1
  139.6 1.1 copy.22
  (37 shorter events, 7.8 us)
Async XLA Ops:
  6.5 90.5 %all-gather.5.cloned.1.call-start = ((), (), s32[]{:S(2)}) async-start(), calls=%async_computation | async-start | bytes 5013504 | tf_op jit(solution)/shard_map/all_gather | solution.py:23
  21.5 17.8 %collective-permute-start = (bf16[21,21,192]{2,1,0:T(8,128)(2,1)S(1)}, bf16[21,21,192]{2,1,0:T(8,128)(2,1)S(1)}, u32[]{:S(2)}, u32[]{:S(2)}) collective-permute-start(bf16[21,21,192]{2,1,0:T(8,128)(2,1)S(1)} %get-tuple-element.22), channel_id=1, source_target_pairs={{0,8},{8,16},{16,24},{24,32},{32,40},{40,48},{48,56},{56,64},{64,7... | collective-permute-start | bytes 508040 | tf_op jit(solution)/shard_map/ppermute | solution.py:38
  25.0 14.2 %collective-permute-start.1 = (bf16[21,21,192]{2,1,0:T(8,128)(2,1)S(1)}, bf16[21,21,192]{2,1,0:T(8,128)(2,1)S(1)}, u32[]{:S(2)}, u32[]{:S(2)}) collective-permute-start(bf16[21,21,192]{2,1,0:T(8,128)(2,1)S(1)} %get-tuple-element.21), channel_id=1, source_target_pairs={{8,0},{16,8},{24,16},{32,24},{40,32},{48,40},{56,48},{64,56},{72,6... | collective-permute-start | bytes 508040 | tf_op jit(solution)/shard_map/ppermute | solution.py:41
  39.2 0.7 copy-start.2
  39.9 0.7 copy-start.3
  48.9 1.1 copy-start
  77.3 1.6 %copy-start.4 = (f16[1536,896]{0,1:T(8,128)(2,1)}, f16[1536,896]{0,1:T(8,128)(2,1)S(1)}, u32[]{:S(2)}) copy-start(f16[1536,896]{0,1:T(8,128)(2,1)S(1)} %copy.19) | copy-start | bytes 8257540
  102.7 13.2 %collective-permute-start.2 = (bf16[4,192,896]{2,1,0:T(8,128)(2,1)S(1)}, bf16[4,192,896]{2,1,0:T(8,128)(2,1)S(1)}, u32[]{:S(2)}, u32[]{:S(2)}) collective-permute-start(bf16[4,192,896]{2,1,0:T(8,128)(2,1)S(1)} %get-tuple-element.15), channel_id=1, source_target_pairs={{0,1},{1,0},{2,3},{3,2},{4,5},{5,4},{6,7},{7,6},{8,9},{9,8},{10,11... | collective-permute-start | bytes 4128776 | tf_op jit(solution)/shard_map/ppermute | solution.py:17
  113.2 15.0 %copy-start.6 = (bf16[192]{0:T(256)(128)(2,1)S(1)}, bf16[192]{0:T(256)(128)(2,1)}, u32[]{:S(2)}) copy-start(bf16[192]{0:T(256)(128)(2,1)} %param.24) | copy-start | bytes 1156
  113.2 15.1 %copy-start.5 = (f32[192]{0:T(256)S(1)}, f32[192]{0:T(256)}, u32[]{:S(2)}) copy-start(f32[192]{0:T(256)} %param.25) | copy-start | bytes 2308
  113.2 15.2 %copy-start.1 = (f32[2,21,21,192]{3,2,1,0:T(8,128)S(1)}, f32[2,21,21,192]{3,2,1,0:T(8,128)}, u32[]{:S(2)}) copy-start(f32[2,21,21,192]{3,2,1,0:T(8,128)} %copy-done) | copy-start | bytes 2032132
  117.1 13.3 %collective-permute-start.3 = (bf16[192,896]{1,0:T(8,128)(2,1)}, bf16[192,896]{1,0:T(8,128)(2,1)S(1)}, u32[]{:S(2)}, u32[]{:S(2)}) collective-permute-start(bf16[192,896]{1,0:T(8,128)(2,1)} %get-tuple-element.17), channel_id=1, source_target_pairs={{0,4},{2,6},{4,0},{6,2},{1,5},{3,7},{5,1},{7,3},{8,12},{10,14},{12... | collective-permute-start | bytes 1032200 | tf_op jit(solution)/shard_map/ppermute | solution.py:17
  121.6 16.4 %collective-permute-start.4 = (bf16[192,896]{1,0:T(8,128)(2,1)}, bf16[192,896]{1,0:T(8,128)(2,1)S(1)}, u32[]{:S(2)}, u32[]{:S(2)}) collective-permute-start(bf16[192,896]{1,0:T(8,128)(2,1)} %get-tuple-element.18), channel_id=1, source_target_pairs={{0,2},{2,4},{4,6},{6,0},{1,3},{3,5},{5,7},{7,1},{8,10},{10,12},{12... | collective-permute-start | bytes 1032200 | tf_op jit(solution)/shard_map/ppermute | solution.py:17
  124.0 14.0 %collective-permute-start.5 = (bf16[192,896]{1,0:T(8,128)(2,1)}, bf16[192,896]{1,0:T(8,128)(2,1)}, u32[]{:S(2)}, u32[]{:S(2)}) collective-permute-start(bf16[192,896]{1,0:T(8,128)(2,1)} %get-tuple-element.19), channel_id=1, source_target_pairs={{0,6},{2,0},{4,2},{6,4},{1,7},{3,1},{5,3},{7,5},{8,14},{10,8},{12,... | collective-permute-start | bytes 1032200 | tf_op jit(solution)/shard_map/ppermute | solution.py:17
Sparse Core Ops, SparseCore 0:
  17.6 79.3 all-gather.4

commit v5 on v4

--- a/solution.py
+++ b/solution.py
@@ -17,11 +17,18 @@
     return lax.ppermute(block, axis, [(i, (i + distance) % size) for i in range(size)])
 
 
-def gather_weights(w_up, w_down):
-    both = jnp.stack([w_up, w_down.T])
-    over_y = lax.all_gather(both, "y", axis=1)
-    over_z = lax.all_gather(over_y, "z", axis=2)
-    return over_z.reshape(2, NY * NZ * w_up.shape[0], w_up.shape[1])
+def gather_z(w_up, w_down):
+    both = jnp.stack([w_up, w_down.T]).astype(jnp.float32) * 2.0**18
+    over_z = lax.all_gather(both.astype(jnp.float16), "z", axis=1, tiled=True)
+    return (over_z.astype(jnp.float32) * 2.0**-18).astype(jnp.bfloat16)
+
+
+def gather_y(own):
+    behind = shift(own, "y", 1, NY)
+    ahead = shift(own, "y", -1, NY)
+    far_up = shift(behind[0], "y", 1, NY)
+    far_down = shift(ahead[1], "y", -1, NY)
+    return own, ahead, behind, far_up, far_down
 
 
 def exchange(slots, seq_index, first_crop):
@@ -126,16 +133,22 @@
     return pl.BlockSpec(memory_space=space)
 
 
-def copy_down_rows(weights, buffer, sems, core):
+def split_blocks(blocks):
+    own, ahead, behind, far_up, far_down = blocks
+    ups = (own.at[0], ahead.at[0], far_up, behind.at[0])
+    downs = (own.at[1], ahead.at[1], far_down, behind.at[1])
+    return ups, downs
+
+
+def copy_down_rows(blocks, buffer, sems, y, core):
     width = buffer.shape[0] // NX
     copies = []
-    for x in range(NX):
-        row = pl.multiple_of((x * NCORE + core) * width, width)
+    for d, block in enumerate(split_blocks(blocks)[1]):
+        source = pl.multiple_of(core * width, width)
+        target = pl.multiple_of(lax.rem(y + d, NY) * width, width)
         copies.append(
             pltpu.make_async_copy(
-                weights.at[1, pl.ds(row, width), :],
-                buffer.at[pl.ds(x * width, width), :],
-                sems.at[x],
+                block.at[pl.ds(source, width), :], buffer.at[pl.ds(target, width), :], sems.at[d]
             )
         )
     return copies
@@ -150,16 +163,17 @@
         out[x] = product[x * width : (x + 1) * width].astype(out.dtype)
 
 
-def first_kernel(core, normed, b_up, weights, hidden, out, up, down, up_sem, down_sem):
+def first_kernel(place, normed, b_up, *refs):
+    blocks, (hidden, out, up, down, up_sem, down_sem) = refs[:5], refs[5:]
+    y, core = place[0], place[2]
     ups = []
-    pieces = up_sem.shape[0]
-    step = up.shape[0] // pieces
-    for p in range(pieces):
-        span = pl.ds(p * step, step)
-        ups.append(pltpu.make_async_copy(weights.at[0, span, :], up.at[span, :], up_sem.at[p]))
+    for d, block in enumerate(split_blocks(blocks)[0]):
+        rows = block.shape[0]
+        target = pl.multiple_of(lax.rem(y + d, NY) * rows, rows)
+        ups.append(pltpu.make_async_copy(block, up.at[pl.ds(target, rows), :], up_sem.at[d]))
     for copy in ups:
         copy.start()
-    downs = copy_down_rows(weights, down, down_sem, 1 - core[0])
+    downs = copy_down_rows(blocks, down, down_sem, y, 1 - core)
     for copy in downs:
         copy.start()
     for copy in ups:
@@ -176,8 +190,9 @@
     down_product(down, hidden[...], out)
 
 
-def second_kernel(core, hidden, weights, out, down, down_sem):
-    downs = copy_down_rows(weights, down, down_sem, core[0])
+def second_kernel(place, hidden, *refs):
+    blocks, (out, down, down_sem) = refs[:5], refs[5:]
+    downs = copy_down_rows(blocks, down, down_sem, place[0], place[2])
     for copy in downs:
         copy.start()
     for copy in downs:
@@ -185,9 +200,9 @@
     down_product(down, hidden[...], out)
 
 
-def pair_kernel(x, mine, other, own, *sent):
+def pair_kernel(place, mine, other, own, *sent):
     def pair(distance):
-        i = lax.rem(x[0] + distance, NX)
+        i = lax.rem(place[1] + distance, NX)
         return mine[i].astype(jnp.float32) + other[i].astype(jnp.float32)
 
     own[...] = pair(0)
@@ -204,38 +219,37 @@
     out[...] = (residual[...] + scaled.T[:rows]).astype(out.dtype)
 
 
-def mlp_sum(normed, weights, b_up, width):
+def mlp_sum(normed, blocks, b_up, width):
     bf16, f32 = jnp.bfloat16, jnp.float32
     cells, units = normed.shape[0], b_up.shape[0]
-    core = lax.axis_index("core").astype(jnp.int32).reshape(1)
-    x = lax.axis_index("x").astype(jnp.int32).reshape(1)
+    place = jnp.stack([lax.axis_index(a).astype(jnp.int32) for a in ("y", "x", "core")])
     params = pltpu.CompilerParams(vmem_limit_bytes=48 * 2**20)
     half_out = jax.ShapeDtypeStruct((NX, width, cells), bf16)
     down = pltpu.VMEM((NX * width, units), bf16)
     hidden, other = pl.pallas_call(
         first_kernel,
         out_shape=(jax.ShapeDtypeStruct((cells, units), bf16), half_out),
-        in_specs=[whole(pltpu.SMEM), whole(), whole(), whole(pl.ANY)],
+        in_specs=[whole(pltpu.SMEM), whole(), whole()] + [whole(pl.ANY)] * len(blocks),
         out_specs=(whole(), whole()),
         scratch_shapes=[
-            pltpu.VMEM(weights.shape[1:], bf16),
+            pltpu.VMEM((normed.shape[1], units), bf16),
             down,
             pltpu.SemaphoreType.DMA((4,)),
             pltpu.SemaphoreType.DMA((NX,)),
         ],
         compiler_params=params,
         name="up_and_down",
-    )(core, normed, b_up.astype(f32)[None, :], weights)
+    )(place, normed, b_up.astype(f32)[None, :], *blocks)
     other = shift(other, "core", 1, NCORE)
     mine = pl.pallas_call(
         second_kernel,
         out_shape=half_out,
-        in_specs=[whole(pltpu.SMEM), whole(), whole(pl.ANY)],
+        in_specs=[whole(pltpu.SMEM), whole()] + [whole(pl.ANY)] * len(blocks),
         out_specs=whole(),
         scratch_shapes=[down, pltpu.SemaphoreType.DMA((NX,))],
         compiler_params=params,
         name="down_own",
-    )(core, hidden, weights)
+    )(place, hidden, *blocks)
     block = jax.ShapeDtypeStruct((width, cells), bf16)
     own, *sent = pl.pallas_call(
         pair_kernel,
@@ -244,7 +258,7 @@
         out_specs=(whole(),) * (1 + len(DISTANCES)),
         compiler_params=params,
         name="pair",
-    )(x, mine, other)
+    )(place, mine, other)
     return own, *(shift(block, "x", d, NX) for d, block in zip(DISTANCES, sent))
 
 
@@ -257,7 +271,7 @@
     side = crop_features.shape[1]
     seq_index = lax.axis_index(SEQ)
     start = lax.axis_index(TP) * width
-    weights = gather_weights(w_up, w_down)
+    blocks = gather_y(gather_z(w_up, w_down))
 
     def channels(array):
         return lax.dynamic_slice_in_dim(array, start, width, array.ndim - 1)
@@ -279,7 +293,7 @@
         (conv_all - mean) / jnp.sqrt(var + 1e-6) * ln_gain.astype(f32)[:, None]
         + ln_bias.astype(f32)[:, None]
     ).astype(jnp.bfloat16).T
-    sums = mlp_sum(normed, weights, b_up, width)
+    sums = mlp_sum(normed, blocks, b_up, width)
     result = pl.pallas_call(
         last_kernel,
         out_shape=jax.ShapeDtypeStruct((cells, width), jnp.bfloat16),

time: 150 us -> 173 us (1.15)
  blocking collectives: 32.6 us -> 63.4 us
  between operations: 15 us -> 1.7 us
  local copies, waits for them, and re-layouts: 14.6 us -> 19.2 us
  other arithmetic: 8.65 us -> 12.4 us
  Pallas kernels: 19.3 us -> 22.8 us
  starting transfers between devices: 34 us -> 30.6 us
  waiting for transfers between devices: 23.5 us -> 21.1 us
    all_gather x1, blocking collectives: 10.2 us -> 36 us  [gather_z(): over_z = lax.all_gather(both.astype(jnp.float16), 'z', axis=1, tiled=True)]
    all_gather x1 -> x0, waiting for transfers between devices: 14 us -> none  [gather_weights(): over_z = lax.all_gather(over_y, 'z', axis=2)]
    ppermute x4 -> x8, waiting for transfers between devices: 9.48 us -> 21.1 us  [shift(): lax.ppermute(block, axis, [(i, (i + distance) % size) for i in range(size)])]
    all_gather x1, blocking collectives: 22.4 us -> 27.4 us  [per_device(): conv_all = lax.all_gather(conv_t, TP, axis=0, tiled=True).astype(f32)]
    ppermute x1, starting transfers between devices: 8.98 us -> 5.47 us  [exchange(): lax.ppermute(crop(target - 1), SEQ, [(i + 1, i) for i in range(count - 1)])]
    convert_element_type x2, local copies, waits for them, and re-layouts: 0.47 us -> 3.93 us  [per_device(): conv_t = conv_t.astype(jnp.float16)]
    reduce_sum x1, other arithmetic: 0.43 us -> 2.36 us  [per_device(): mean = jnp.mean(conv_all, axis=0, keepdims=True)]
    reshape x1, local copies, waits for them, and re-layouts: 0.24 us -> 2.05 us  [per_device(): conv[:, :, :side].reshape(cells, width)]
  transfers between devices with their start and end apart: 7 -> 10, of which waited for: 3 -> 4; matrix products, arithmetic and copies ran while one was open for 13% -> 16% of each run, Pallas kernels for 8% -> 7%
where the time goes in v5:
time: 173 us; the launch traced here: 171 us
  blocking collectives  63.4 us (37%)
  starting transfers between devices  30.6 us (18%)
  Pallas kernels  22.8 us (13%)
  waiting for transfers between devices  21.1 us (12%)
  local copies, waits for them, and re-layouts  19.2 us (11%)
  other arithmetic  12.4 us (7%)
    all_gather x1, blocking collectives, gather_z(): over_z = lax.all_gather(both.astype(jnp.float16), 'z', axis=1, tiled=True)  36 us
    all_gather x1, blocking collectives, per_device(): conv_all = lax.all_gather(conv_t, TP, axis=0, tiled=True).astype(f32)  27.4 us
    ppermute x8, starting transfers between devices, shift(): lax.ppermute(block, axis, [(i, (i + distance) % size) for i in range(size)])  23.2 us
    ppermute x8, waiting for transfers between devices, shift(): lax.ppermute(block, axis, [(i, (i + distance) % size) for i in range(size)])  21.1 us
    pallas_call x1, Pallas kernels, depthwise(): pl.pallas_call(conv_kernel, out_shape=(jax.ShapeDtypeStruct((PER_DEV, sid...  9.25 us
    pallas_call x1, Pallas kernels, mlp_sum(): pl.pallas_call(first_kernel, out_shape=(jax.ShapeDtypeStruct((cells, unit...  7.51 us
    ppermute x1, starting transfers between devices, exchange(): lax.ppermute(crop(target - 1), SEQ, [(i + 1, i) for i in range(count - 1)])  5.47 us
    all_gather x1, local copies, waits for them, and re-layouts, per_device(): conv_all = lax.all_gather(conv_t, TP, axis=0, tiled=True).astype(f32)  4.96 us
  transfers between devices with their start and end apart: 10, of which 4 were waited for; matrix products, arithmetic and copies ran while one was open for 16% of the time, Pallas kernels for 7%

profile of v5, /device:TPU:25, one launch (start us, length us, event | category | flops | bytes accessed | tf_op | source)
XLA Modules:
  0.0 171.2 jit_solution(5072970661463650464)
XLA Ops:
  0.9 36.0 %all-gather.3 = f16[2,384,768]{2,1,0:T(8,128)(2,1)S(1)} all-gather(f16[2,24,768]{2,1,0:T(8,128)(2,1)S(1)} %multiply_convert_fusion.1), channel_id=1, replica_groups=mesh['y'=4,'z'=16,'x'=4,'core'=2] {'z'}, dimensions={1}, use_global_device_ids=true | all-gather | bytes 1253376 | tf_op jit(solution)/shard_map/all_gather | solution.py:22
  37.1 1.9 %collective-permute-start.3 = (bf16[2,384,768]{2,1,0:T(8,128)(2,1)S(1)}, bf16[2,384,768]{2,1,0:T(8,128)(2,1)S(1)}, u32[]{:S(2)}, u32[]{:S(2)}) collective-permute-start(bf16[2,384,768]{2,1,0:T(8,128)(2,1)S(1)} %multiply_convert_fusion.refs_0_), channel_id=1, source_target_pairs={{0,128},{128,256},{256,384},{384,0},{1,129},{129,257},{257,385},{3... | collective-permute-start | bytes 3538952 | tf_op jit(solution)/shard_map/ppermute | solution.py:17
  39.0 3.4 %collective-permute-start.2 = (bf16[2,384,768]{2,1,0:T(8,128)(2,1)S(1)}, bf16[2,384,768]{2,1,0:T(8,128)(2,1)S(1)}, u32[]{:S(2)}, u32[]{:S(2)}) collective-permute-start(bf16[2,384,768]{2,1,0:T(8,128)(2,1)S(1)} %multiply_convert_fusion.refs_0_), channel_id=1, source_target_pairs={{0,384},{128,0},{256,128},{384,256},{1,385},{129,1},{257,129},{385... | collective-permute-start | bytes 3538952 | tf_op jit(solution)/shard_map/ppermute | solution.py:17
  45.7 1.9 %collective-permute-start = (bf16[21,21,192]{2,1,0:T(8,128)(2,1)S(1)}, bf16[21,21,192]{2,1,0:T(8,128)(2,1)S(1)}, u32[]{:S(2)}, u32[]{:S(2)}) collective-permute-start(bf16[21,21,192]{2,1,0:T(8,128)(2,1)S(1)} %get-tuple-element.22), channel_id=1, source_target_pairs={{0,8},{8,16},{16,24},{24,32},{32,40},{40,48},{48,56},{56,64},{64,7... | collective-permute-start | bytes 508040 | tf_op jit(solution)/shard_map/ppermute | solution.py:45
  47.6 5.5 %collective-permute-start.1 = (bf16[21,21,192]{2,1,0:T(8,128)(2,1)S(1)}, bf16[21,21,192]{2,1,0:T(8,128)(2,1)S(1)}, u32[]{:S(2)}, u32[]{:S(2)}) collective-permute-start(bf16[21,21,192]{2,1,0:T(8,128)(2,1)S(1)} %get-tuple-element.21), channel_id=1, source_target_pairs={{8,0},{16,8},{24,16},{32,24},{40,32},{48,40},{56,48},{64,56},{72,6... | collective-permute-start | bytes 508040 | tf_op jit(solution)/shard_map/ppermute | solution.py:48
  58.2 9.2 %conv.1 = (f32[2,21,21,192]{3,2,1,0:T(8,128)S(1)}, f32[2,21,24,192]{3,2,1,0:T(8,128)S(1)}) custom-call(s32[1]{0:T(128)} %bitcast.3.seq, s32[64]{0:T(128)S(1)} %copy-done.3, s32[64]{0:T(128)S(1)} %copy-done.4, bf16[3,21,21,192]{3,2,1,0:T(8,128)(2,1)S(1)} %constant_dynamic-slice_fusion.slots, bf16[21,21,192]{2,1,0:T(8,128)(2,1)S(1)} %collective-permute-done.before, ...), custom_call_target="tpu_custom_call" | custom-call | tf_op jit(solution)/shard_map/conv/pallas_call | solution.py:114
  69.4 2.0 %reshape.28 = f16[882,192]{1,0:T(8,128)(2,1)} reshape(f16[2,21,21,192]{3,2,1,0:T(8,128)(2,1)} %slice_convert_fusion) | data formatting | bytes 677376 | tf_op jit(solution)/shard_map/reshape | solution.py:287
  73.3 2.0 %copy.18 = f16[192,896]{1,0:T(8,128)(2,1)} copy(f16[192,896]{0,1:T(8,128)(2,1)} %pad_bitcast_fusion) | data formatting | bytes 688128 | tf_op jit(solution)/shard_map/convert_element_type | solution.py:288
  75.3 27.4 %all-gather.2 = f16[1536,896]{1,0:T(8,128)(2,1)} all-gather(f16[192,896]{1,0:T(8,128)(2,1)} %copy.18), channel_id=1, replica_groups=mesh['y'=4,'z'=16,'x'=4,'core'=2] {'x','core'}, dimensions={0}, use_global_device_ids=true | all-gather | bytes 3096576 | tf_op jit(solution)/shard_map/all_gather | solution.py:289
  102.7 5.0 %copy.19 = f16[1536,896]{0,1:T(8,128)(2,1)} copy(f16[1536,896]{1,0:T(8,128)(2,1)} %all-gather.2) | data formatting | bytes 5505024 | tf_op jit(solution)/shard_map/all_gather | solution.py:289
  107.7 2.4 %convert_reduce_fusion = f32[896]{0:T(1024)S(1)} fusion(f16[1536,896]{0,1:T(8,128)(2,1)} %copy.19), kind=kLoop, calls=%fused_computation.1 | loop fusion | flops 2751616 | bytes 2756096 | tf_op jit(solution)/shard_map/reduce_sum | solution.py:290
  111.2 1.9 %collective-permute-start.4 = (bf16[384,768]{1,0:T(8,128)(2,1)S(1)}, bf16[384,768]{1,0:T(8,128)(2,1)S(1)}, u32[]{:S(2)}, u32[]{:S(2)}) collective-permute-start(bf16[384,768]{1,0:T(8,128)(2,1)S(1)} %slice_bitcast_fusion.1), channel_id=1, source_target_pairs={{0,128},{128,256},{256,384},{384,0},{1,129},{129,257},{257,385},{3... | collective-permute-start | bytes 1769480 | tf_op jit(solution)/shard_map/ppermute | solution.py:17
  113.2 3.4 %collective-permute-start.5 = (bf16[384,768]{1,0:T(8,128)(2,1)S(1)}, bf16[384,768]{1,0:T(8,128)(2,1)S(1)}, u32[]{:S(2)}, u32[]{:S(2)}) collective-permute-start(bf16[384,768]{1,0:T(8,128)(2,1)S(1)} %slice_bitcast_fusion), channel_id=1, source_target_pairs={{0,384},{128,0},{256,128},{384,256},{1,385},{129,1},{257,129},{385... | collective-permute-start | bytes 1769480 | tf_op jit(solution)/shard_map/ppermute | solution.py:17
  116.6 4.4 %fusion.6.normed = bf16[896,1536]{1,0:T(8,128)(2,1)} fusion(f16[1536,896]{0,1:T(8,128)(2,1)S(1)} %copy-done.5, f32[1536]{0:T(1024)S(1)} %copy-done.7, f32[1536]{0:T(1024)S(1)} %copy-done.6, f32[896]{0:T(1024)S(1)} %add_sqrt_fusion, f32[896]{0:T(1024)S(1)} %broadcast_multiply_fusion), kind=kLoop, calls=%fused_computation.8 | loop fusion | flops 8257536 | bytes 5524480 | tf_op jit(solution)/shard_map/transpose | solution.py:295
  121.0 6.9 %collective-permute-done.4.refs_3_ = bf16[384,768]{1,0:T(8,128)(2,1)S(1)} collective-permute-done((bf16[384,768]{1,0:T(8,128)(2,1)S(1)}, bf16[384,768]{1,0:T(8,128)(2,1)S(1)}, u32[]{:S(2)}, u32[]{:S(2)}) %collective-permute-start.4) | collective-permute-done | bytes 589856 | tf_op jit(solution)/shard_map/ppermute | solution.py:17
  127.9 3.2 %collective-permute-done.5.refs_4_ = bf16[384,768]{1,0:T(8,128)(2,1)S(1)} collective-permute-done((bf16[384,768]{1,0:T(8,128)(2,1)S(1)}, bf16[384,768]{1,0:T(8,128)(2,1)S(1)}, u32[]{:S(2)}, u32[]{:S(2)}) %collective-permute-start.5) | collective-permute-done | bytes 589856 | tf_op jit(solution)/shard_map/ppermute | solution.py:17
  131.1 7.5 %up_and_down.1 = (bf16[896,768]{1,0:T(8,128)(2,1)S(1)}, bf16[4,192,896]{2,1,0:T(8,128)(2,1)}) custom-call(s32[3]{0:T(128)S(1)} %pad_add_fusion.place, bf16[896,1536]{1,0:T(8,128)(2,1)} %fusion.6.normed, f32[1,768]{1,0:T(1,128)S(1)} %reshape.31.b_up, bf16[2,384,768]{2,1,0:T(8,128)(2,1)S(1)} %multiply_convert_fusion.refs_0_, ...), custom_call_target="tpu_custom_call" | custom-call | tf_op jit(solution)/shard_map/up_and_down/pallas_call | solution.py:229
  139.7 3.0 %collective-permute-start.6 = (bf16[4,192,896]{2,1,0:T(8,128)(2,1)}, bf16[4,192,896]{2,1,0:T(8,128)(2,1)S(1)}, u32[]{:S(2)}, u32[]{:S(2)}) collective-permute-start(bf16[4,192,896]{2,1,0:T(8,128)(2,1)} %get-tuple-element.15), channel_id=1, source_target_pairs={{0,1},{1,0},{2,3},{3,2},{4,5},{5,4},{6,7},{7,6},{8,9},{9,8},{10,11... | collective-permute-start | bytes 4128776 | tf_op jit(solution)/shard_map/ppermute | solution.py:17
  142.8 3.1 %down_own.1.mine = bf16[4,192,896]{2,1,0:T(8,128)(2,1)S(1)} custom-call(s32[3]{0:T(128)S(1)} %pad_add_fusion.place, bf16[896,768]{1,0:T(8,128)(2,1)} %copy-done, bf16[2,384,768]{2,1,0:T(8,128)(2,1)S(1)} %multiply_convert_fusion.refs_0_, bf16[2,384,768]{2,1,0:T(8,128)(2,1)S(1)} %collective-permute-done.2.refs_1_, ...), custom_call_target="tpu_custom_call" | custom-call | tf_op jit(solution)/shard_map/down_own/pallas_call | solution.py:244
  147.5 3.1 %collective-permute-start.7 = (bf16[192,896]{1,0:T(8,128)(2,1)}, bf16[192,896]{1,0:T(8,128)(2,1)S(1)}, u32[]{:S(2)}, u32[]{:S(2)}) collective-permute-start(bf16[192,896]{1,0:T(8,128)(2,1)} %get-tuple-element.17), channel_id=1, source_target_pairs={{0,4},{2,6},{4,0},{6,2},{1,5},{3,7},{5,1},{7,3},{8,12},{10,14},{12... | collective-permute-start | bytes 1032200 | tf_op jit(solution)/shard_map/ppermute | solution.py:17
  150.6 2.1 %collective-permute-start.8 = (bf16[192,896]{1,0:T(8,128)(2,1)}, bf16[192,896]{1,0:T(8,128)(2,1)S(1)}, u32[]{:S(2)}, u32[]{:S(2)}) collective-permute-start(bf16[192,896]{1,0:T(8,128)(2,1)} %get-tuple-element.18), channel_id=1, source_target_pairs={{0,2},{2,4},{4,6},{6,0},{1,3},{3,5},{5,7},{7,1},{8,10},{10,12},{12... | collective-permute-start | bytes 1032200 | tf_op jit(solution)/shard_map/ppermute | solution.py:17
  152.7 4.4 %collective-permute-start.9 = (bf16[192,896]{1,0:T(8,128)(2,1)}, bf16[192,896]{1,0:T(8,128)(2,1)}, u32[]{:S(2)}, u32[]{:S(2)}) collective-permute-start(bf16[192,896]{1,0:T(8,128)(2,1)} %get-tuple-element.19), channel_id=1, source_target_pairs={{0,6},{2,0},{4,2},{6,4},{1,7},{3,1},{5,3},{7,5},{8,14},{10,8},{12,... | collective-permute-start | bytes 1032200 | tf_op jit(solution)/shard_map/ppermute | solution.py:17
  157.5 3.3 %collective-permute-done.7.first = bf16[192,896]{1,0:T(8,128)(2,1)S(1)} collective-permute-done((bf16[192,896]{1,0:T(8,128)(2,1)}, bf16[192,896]{1,0:T(8,128)(2,1)S(1)}, u32[]{:S(2)}, u32[]{:S(2)}) %collective-permute-start.7) | collective-permute-done | bytes 344096 | tf_op jit(solution)/shard_map/ppermute | solution.py:17
  160.8 7.7 %collective-permute-done.8.second = bf16[192,896]{1,0:T(8,128)(2,1)S(1)} collective-permute-done((bf16[192,896]{1,0:T(8,128)(2,1)}, bf16[192,896]{1,0:T(8,128)(2,1)S(1)}, u32[]{:S(2)}, u32[]{:S(2)}) %collective-permute-start.8) | collective-permute-done | bytes 344096 | tf_op jit(solution)/shard_map/ppermute | solution.py:17
  (56 shorter events, 18.8 us)
Async XLA Ops:
  0.0 42.4 %copy-start.3 = (s32[64]{0:T(128)S(1)}, s32[64]{0:T(128)}, u32[]{:S(2)}) copy-start(s32[64]{0:T(128)} %first_crop.1) | copy-start | bytes 772
  0.0 53.1 %copy-start.9 = (bf16[1536]{0:T(1024)(128)(2,1)S(1)}, bf16[1536]{0:T(1024)(128)(2,1)}, u32[]{:S(2)}) copy-start(bf16[1536]{0:T(1024)(128)(2,1)} %param.18) | copy-start | bytes 9220
  0.0 54.1 %copy-start.8 = (bf16[1536]{0:T(1024)(128)(2,1)S(1)}, bf16[1536]{0:T(1024)(128)(2,1)}, u32[]{:S(2)}) copy-start(bf16[1536]{0:T(1024)(128)(2,1)} %param.19) | copy-start | bytes 9220
  36.9 21.4 %copy-start.4 = (s32[64]{0:T(128)S(1)}, s32[64]{0:T(128)}, u32[]{:S(2)}) copy-start(s32[64]{0:T(128)} %crop_counts.1) | copy-start | bytes 772
  37.1 74.1 %collective-permute-start.3 = (bf16[2,384,768]{2,1,0:T(8,128)(2,1)S(1)}, bf16[2,384,768]{2,1,0:T(8,128)(2,1)S(1)}, u32[]{:S(2)}, u32[]{:S(2)}) collective-permute-start(bf16[2,384,768]{2,1,0:T(8,128)(2,1)S(1)} %multiply_convert_fusion.refs_0_), channel_id=1, source_target_pairs={{0,128},{128,256},{256,384},{384,0},{1,129},{129,257},{257,385},{3... | collective-permute-start | bytes 3538952 | tf_op jit(solution)/shard_map/ppermute | solution.py:17
  39.0 74.2 %collective-permute-start.2 = (bf16[2,384,768]{2,1,0:T(8,128)(2,1)S(1)}, bf16[2,384,768]{2,1,0:T(8,128)(2,1)S(1)}, u32[]{:S(2)}, u32[]{:S(2)}) collective-permute-start(bf16[2,384,768]{2,1,0:T(8,128)(2,1)S(1)} %multiply_convert_fusion.refs_0_), channel_id=1, source_target_pairs={{0,384},{128,0},{256,128},{384,256},{1,385},{129,1},{257,129},{385... | collective-permute-start | bytes 3538952 | tf_op jit(solution)/shard_map/ppermute | solution.py:17
  45.7 12.6 %collective-permute-start = (bf16[21,21,192]{2,1,0:T(8,128)(2,1)S(1)}, bf16[21,21,192]{2,1,0:T(8,128)(2,1)S(1)}, u32[]{:S(2)}, u32[]{:S(2)}) collective-permute-start(bf16[21,21,192]{2,1,0:T(8,128)(2,1)S(1)} %get-tuple-element.22), channel_id=1, source_target_pairs={{0,8},{8,16},{16,24},{24,32},{32,40},{40,48},{48,56},{56,64},{64,7... | collective-permute-start | bytes 508040 | tf_op jit(solution)/shard_map/ppermute | solution.py:45
  47.6 10.6 %collective-permute-start.1 = (bf16[21,21,192]{2,1,0:T(8,128)(2,1)S(1)}, bf16[21,21,192]{2,1,0:T(8,128)(2,1)S(1)}, u32[]{:S(2)}, u32[]{:S(2)}) collective-permute-start(bf16[21,21,192]{2,1,0:T(8,128)(2,1)S(1)} %get-tuple-element.21), channel_id=1, source_target_pairs={{8,0},{16,8},{24,16},{32,24},{40,32},{48,40},{56,48},{64,56},{72,6... | collective-permute-start | bytes 508040 | tf_op jit(solution)/shard_map/ppermute | solution.py:48
  67.5 1.0 copy-start.1
  107.7 2.6 %copy-start.5 = (f16[1536,896]{0,1:T(8,128)(2,1)S(1)}, f16[1536,896]{0,1:T(8,128)(2,1)}, u32[]{:S(2)}) copy-start(f16[1536,896]{0,1:T(8,128)(2,1)} %copy.19) | copy-start | bytes 8257540
  110.1 6.5 %copy-start.6 = (f32[1536]{0:T(1024)S(1)}, f32[1536]{0:T(1024)}, u32[]{:S(2)}) copy-start(f32[1536]{0:T(1024)} %convert_element_type.34) | copy-start | bytes 18436
  110.1 6.5 %copy-start.7 = (f32[1536]{0:T(1024)S(1)}, f32[1536]{0:T(1024)}, u32[]{:S(2)}) copy-start(f32[1536]{0:T(1024)} %convert_element_type.35) | copy-start | bytes 18436
  111.2 16.7 %collective-permute-start.4 = (bf16[384,768]{1,0:T(8,128)(2,1)S(1)}, bf16[384,768]{1,0:T(8,128)(2,1)S(1)}, u32[]{:S(2)}, u32[]{:S(2)}) collective-permute-start(bf16[384,768]{1,0:T(8,128)(2,1)S(1)} %slice_bitcast_fusion.1), channel_id=1, source_target_pairs={{0,128},{128,256},{256,384},{384,0},{1,129},{129,257},{257,385},{3... | collective-permute-start | bytes 1769480 | tf_op jit(solution)/shard_map/ppermute | solution.py:17
  113.2 17.9 %collective-permute-start.5 = (bf16[384,768]{1,0:T(8,128)(2,1)S(1)}, bf16[384,768]{1,0:T(8,128)(2,1)S(1)}, u32[]{:S(2)}, u32[]{:S(2)}) collective-permute-start(bf16[384,768]{1,0:T(8,128)(2,1)S(1)} %slice_bitcast_fusion), channel_id=1, source_target_pairs={{0,384},{128,0},{256,128},{384,256},{1,385},{129,1},{257,129},{385... | collective-permute-start | bytes 1769480 | tf_op jit(solution)/shard_map/ppermute | solution.py:17
  138.6 1.1 copy-start
  139.7 6.2 %collective-permute-start.6 = (bf16[4,192,896]{2,1,0:T(8,128)(2,1)}, bf16[4,192,896]{2,1,0:T(8,128)(2,1)S(1)}, u32[]{:S(2)}, u32[]{:S(2)}) collective-permute-start(bf16[4,192,896]{2,1,0:T(8,128)(2,1)} %get-tuple-element.15), channel_id=1, source_target_pairs={{0,1},{1,0},{2,3},{3,2},{4,5},{5,4},{6,7},{7,6},{8,9},{9,8},{10,11... | collective-permute-start | bytes 4128776 | tf_op jit(solution)/shard_map/ppermute | solution.py:17
  145.8 11.2 %copy-start.11 = (bf16[192]{0:T(256)(128)(2,1)S(1)}, bf16[192]{0:T(256)(128)(2,1)}, u32[]{:S(2)}) copy-start(bf16[192]{0:T(256)(128)(2,1)} %param.24) | copy-start | bytes 1156
  145.8 11.4 %copy-start.10 = (f32[192]{0:T(256)S(1)}, f32[192]{0:T(256)}, u32[]{:S(2)}) copy-start(f32[192]{0:T(256)} %param.25) | copy-start | bytes 2308
  145.9 11.5 %copy-start.2 = (f32[2,21,21,192]{3,2,1,0:T(8,128)S(1)}, f32[2,21,21,192]{3,2,1,0:T(8,128)}, u32[]{:S(2)}) copy-start(f32[2,21,21,192]{3,2,1,0:T(8,128)} %copy-done.1) | copy-start | bytes 2032132
  147.5 13.3 %collective-permute-start.7 = (bf16[192,896]{1,0:T(8,128)(2,1)}, bf16[192,896]{1,0:T(8,128)(2,1)S(1)}, u32[]{:S(2)}, u32[]{:S(2)}) collective-permute-start(bf16[192,896]{1,0:T(8,128)(2,1)} %get-tuple-element.17), channel_id=1, source_target_pairs={{0,4},{2,6},{4,0},{6,2},{1,5},{3,7},{5,1},{7,3},{8,12},{10,14},{12... | collective-permute-start | bytes 1032200 | tf_op jit(solution)/shard_map/ppermute | solution.py:17
  150.6 17.9 %collective-permute-start.8 = (bf16[192,896]{1,0:T(8,128)(2,1)}, bf16[192,896]{1,0:T(8,128)(2,1)S(1)}, u32[]{:S(2)}, u32[]{:S(2)}) collective-permute-start(bf16[192,896]{1,0:T(8,128)(2,1)} %get-tuple-element.18), channel_id=1, source_target_pairs={{0,2},{2,4},{4,6},{6,0},{1,3},{3,5},{5,7},{7,1},{8,10},{10,12},{12... | collective-permute-start | bytes 1032200 | tf_op jit(solution)/shard_map/ppermute | solution.py:17
  152.7 15.8 %collective-permute-start.9 = (bf16[192,896]{1,0:T(8,128)(2,1)}, bf16[192,896]{1,0:T(8,128)(2,1)}, u32[]{:S(2)}, u32[]{:S(2)}) collective-permute-start(bf16[192,896]{1,0:T(8,128)(2,1)} %get-tuple-element.19), channel_id=1, source_target_pairs={{0,6},{2,0},{4,2},{6,4},{1,7},{3,1},{5,3},{7,5},{8,14},{10,8},{12,... | collective-permute-start | bytes 1032200 | tf_op jit(solution)/shard_map/ppermute | solution.py:17

commit v6 on v4

--- a/solution.py
+++ b/solution.py
@@ -10,7 +10,6 @@
 TP = ("x", "core")
 PER_DEV = 2
 KSIDE = 7
-DISTANCES = (2, 1, 3)
 
 
 def shift(block, axis, distance, size):
@@ -117,9 +116,13 @@
             pltpu.VMEM((KSIDE, PER_DEV, side + 6, columns, width), f32),
             pltpu.VMEM((KSIDE * KSIDE, 8, width), f32),
         ],
-        compiler_params=pltpu.CompilerParams(vmem_limit_bytes=48 * 2**20),
+        compiler_params=vmem(16),
         name="conv",
     )(seq_index.astype(jnp.int32).reshape(1), first_crop, crop_counts, slots, before, after, table)
+
+
+def vmem(mebibytes):
+    return pltpu.CompilerParams(vmem_limit_bytes=mebibytes * 2**20)
 
 
 def whole(space=pltpu.VMEM):
@@ -185,20 +188,15 @@
     down_product(down, hidden[...], out)
 
 
-def pair_kernel(x, mine, other, own, *sent):
-    def pair(distance):
-        i = lax.rem(x[0] + distance, NX)
-        return mine[i].astype(jnp.float32) + other[i].astype(jnp.float32)
-
-    own[...] = pair(0)
-    for distance, block in zip(DISTANCES, sent):
-        block[...] = pair(distance).astype(block.dtype)
-
-
-def last_kernel(own, first, second, third, b_down, gamma, residual, out):
-    total = own[...]
-    for block in (first, second, third):
-        total = total + block[...].astype(jnp.float32)
+def pair_kernel(mine, other, out):
+    total = mine[...].astype(jnp.float32) + other[...].astype(jnp.float32)
+    out[...] = total.astype(out.dtype)
+
+
+def last_kernel(parts, b_down, gamma, residual, out):
+    total = parts[0].astype(jnp.float32)
+    for i in range(1, NX):
+        total = total + parts[i].astype(jnp.float32)
     scaled = gamma[...] * (total + b_down[...])
     rows = residual.shape[0]
     out[...] = (residual[...] + scaled.T[:rows]).astype(out.dtype)
@@ -208,10 +206,9 @@
     bf16, f32 = jnp.bfloat16, jnp.float32
     cells, units = normed.shape[0], b_up.shape[0]
     core = lax.axis_index("core").astype(jnp.int32).reshape(1)
-    x = lax.axis_index("x").astype(jnp.int32).reshape(1)
-    params = pltpu.CompilerParams(vmem_limit_bytes=48 * 2**20)
     half_out = jax.ShapeDtypeStruct((NX, width, cells), bf16)
     down = pltpu.VMEM((NX * width, units), bf16)
+    weights = pltpu.with_memory_space_constraint(weights, pltpu.HBM)
     hidden, other = pl.pallas_call(
         first_kernel,
         out_shape=(jax.ShapeDtypeStruct((cells, units), bf16), half_out),
@@ -223,7 +220,7 @@
             pltpu.SemaphoreType.DMA((4,)),
             pltpu.SemaphoreType.DMA((NX,)),
         ],
-        compiler_params=params,
+        compiler_params=vmem(20),
         name="up_and_down",
     )(core, normed, b_up.astype(f32)[None, :], weights)
     other = shift(other, "core", 1, NCORE)
@@ -233,19 +230,18 @@
         in_specs=[whole(pltpu.SMEM), whole(), whole(pl.ANY)],
         out_specs=whole(),
         scratch_shapes=[down, pltpu.SemaphoreType.DMA((NX,))],
-        compiler_params=params,
+        compiler_params=vmem(12),
         name="down_own",
     )(core, hidden, weights)
-    block = jax.ShapeDtypeStruct((width, cells), bf16)
-    own, *sent = pl.pallas_call(
+    pairs = pl.pallas_call(
         pair_kernel,
-        out_shape=(jax.ShapeDtypeStruct((width, cells), f32),) + (block,) * len(DISTANCES),
-        in_specs=[whole(pltpu.SMEM), whole(), whole()],
-        out_specs=(whole(),) * (1 + len(DISTANCES)),
-        compiler_params=params,
+        out_shape=half_out,
+        in_specs=[whole(), whole()],
+        out_specs=whole(),
+        compiler_params=vmem(12),
         name="pair",
-    )(x, mine, other)
-    return own, *(shift(block, "x", d, NX) for d, block in zip(DISTANCES, sent))
+    )(mine, other)
+    return lax.all_to_all(pairs, "x", split_axis=0, concat_axis=0, tiled=True)
 
 
 def per_device(
@@ -279,15 +275,15 @@
         (conv_all - mean) / jnp.sqrt(var + 1e-6) * ln_gain.astype(f32)[:, None]
         + ln_bias.astype(f32)[:, None]
     ).astype(jnp.bfloat16).T
-    sums = mlp_sum(normed, weights, b_up, width)
+    parts = mlp_sum(normed, weights, b_up, width)
     result = pl.pallas_call(
         last_kernel,
         out_shape=jax.ShapeDtypeStruct((cells, width), jnp.bfloat16),
-        in_specs=[whole()] * (len(sums) + 3),
+        in_specs=[whole()] * 4,
         out_specs=whole(),
-        compiler_params=pltpu.CompilerParams(vmem_limit_bytes=48 * 2**20),
+        compiler_params=vmem(12),
         name="result",
-    )(*sums, b_down.astype(f32)[:, None], gamma[:, None], block_in.reshape(cells, width))
+    )(parts, b_down.astype(f32)[:, None], gamma[:, None], block_in.reshape(cells, width))
     return result.reshape(PER_DEV, side, side, width)
 
 

time: 150 us -> 150 us (level)
  waiting for transfers between devices: 23.5 us -> 31.9 us
  starting transfers between devices: 34 us -> 27 us
    all_to_all x0 -> x1, waiting for transfers between devices: none -> 17.8 us  [mlp_sum(): return lax.all_to_all(pairs, 'x', split_axis=0, concat_axis=0, tiled=True)]
    ppermute x4 -> x1, starting transfers between devices: 21.5 us -> 10.4 us  [shift(): lax.ppermute(block, axis, [(i, (i + distance) % size) for i in range(size)])]
    ppermute x4 -> x1, waiting for transfers between devices: 9.48 us -> 0.01 us  [shift(): lax.ppermute(block, axis, [(i, (i + distance) % size) for i in range(size)])]
    all_to_all x0 -> x1, starting transfers between devices: none -> 4.08 us  [mlp_sum(): return lax.all_to_all(pairs, 'x', split_axis=0, concat_axis=0, tiled=True)]
  transfers between devices with their start and end apart: 7 -> 5, of which waited for: 3 -> 2; matrix products, arithmetic and copies ran while one was open for 13% -> 13% of each run, Pallas kernels for 8% -> 7%
where the time goes in v6:
time: 150 us; the launch traced here: 148 us
  blocking collectives  32.6 us (22%)
  waiting for transfers between devices  31.9 us (21%)
  starting transfers between devices  27 us (18%)
  Pallas kernels  18.6 us (12%)
  between operations  14.9 us (10%)
  local copies, waits for them, and re-layouts  14.6 us (10%)
  other arithmetic  8.65 us (6%)
    all_gather x1, blocking collectives, per_device(): conv_all = lax.all_gather(conv_t, TP, axis=0, tiled=True).astype(f32)  22.4 us
    all_to_all x1, waiting for transfers between devices, mlp_sum(): return lax.all_to_all(pairs, 'x', split_axis=0, concat_axis=0, tiled=True)  17.8 us
    all_gather x1, waiting for transfers between devices, gather_weights(): over_z = lax.all_gather(over_y, 'z', axis=2)  14 us
    ppermute x1, starting transfers between devices, shift(): lax.ppermute(block, axis, [(i, (i + distance) % size) for i in range(size)])  10.4 us
    all_gather x1, blocking collectives, gather_weights(): over_y = lax.all_gather(both, 'y', axis=1)  10.2 us
    ppermute x1, starting transfers between devices, exchange(): lax.ppermute(crop(target - 1), SEQ, [(i + 1, i) for i in range(count - 1)])  8.98 us
    pallas_call x1, Pallas kernels, depthwise(): pl.pallas_call(conv_kernel, out_shape=(jax.ShapeDtypeStruct((PER_DEV, sid...  8.37 us
    pallas_call x1, Pallas kernels, mlp_sum(): pl.pallas_call(first_kernel, out_shape=(jax.ShapeDtypeStruct((cells, unit...  5.72 us
  transfers between devices with their start and end apart: 5, of which 2 were waited for; matrix products, arithmetic and copies ran while one was open for 13% of the time, Pallas kernels for 7%

profile of v6, /device:TPU:25, one launch (start us, length us, event | category | flops | bytes accessed | tf_op | source)
XLA Modules:
  0.0 148.2 jit_solution(7958476207644455755)
XLA Ops:
  6.5 0.8 pad_maximum_fusion
  7.3 10.2 %all-gather = bf16[2,96,768]{2,1,0:T(8,128)(2,1)} all-gather(bf16[2,24,768]{2,1,0:T(8,128)(2,1)S(1)} %pad_maximum_fusion), channel_id=2, replica_groups=mesh['y'=4,'z'=16,'x'=4,'core'=2] {'y'}, dimensions={1}, use_global_device_ids=true | all-gather | bytes 368640 | tf_op jit(solution)/shard_map/all_gather | solution.py:21
  17.5 1.2 dynamic_slice.19
  20.1 1.3 dynamic-slice_bitcast_fusion
  21.5 3.5 %collective-permute-start = (bf16[21,21,192]{2,1,0:T(8,128)(2,1)S(1)}, bf16[21,21,192]{2,1,0:T(8,128)(2,1)S(1)}, u32[]{:S(2)}, u32[]{:S(2)}) collective-permute-start(bf16[21,21,192]{2,1,0:T(8,128)(2,1)S(1)} %get-tuple-element.14), channel_id=1, source_target_pairs={{0,8},{8,16},{16,24},{24,32},{32,40},{40,48},{48,56},{56,64},{64,7... | collective-permute-start | bytes 508040 | tf_op jit(solution)/shard_map/ppermute | solution.py:37
  25.0 9.0 %collective-permute-start.1 = (bf16[21,21,192]{2,1,0:T(8,128)(2,1)S(1)}, bf16[21,21,192]{2,1,0:T(8,128)(2,1)S(1)}, u32[]{:S(2)}, u32[]{:S(2)}) collective-permute-start(bf16[21,21,192]{2,1,0:T(8,128)(2,1)S(1)} %get-tuple-element.13), channel_id=1, source_target_pairs={{8,0},{16,8},{24,16},{32,24},{40,32},{48,40},{56,48},{64,56},{72,6... | collective-permute-start | bytes 508040 | tf_op jit(solution)/shard_map/ppermute | solution.py:40
  34.0 0.7 broadcast_in_dim.20
  34.7 0.9 fusion.8.table
  35.6 0.7 convert_element_type.22
  37.6 1.6 %constant_dynamic-slice_fusion.slots = bf16[3,21,21,192]{3,2,1,0:T(8,128)(2,1)S(1)} fusion(bf16[3,21,21,1536]{3,2,1,0:T(8,128)(2,1)} %param.13, s32[]{:T(128)S(6)} %select_n.12), kind=kLoop, calls=%fused_computation.21 | loop fusion | bytes 1016068 | tf_op jit(solution)/shard_map/dynamic_slice | solution.py:259
  40.6 8.4 %conv.1 = (f32[2,21,21,192]{3,2,1,0:T(8,128)S(1)}, f32[2,21,24,192]{3,2,1,0:T(8,128)S(1)}) custom-call(s32[1]{0:T(128)} %bitcast.1.seq, s32[64]{0:T(128)S(1)} %copy-done.2, s32[64]{0:T(128)S(1)} %copy-done.3, bf16[3,21,21,192]{3,2,1,0:T(8,128)(2,1)S(1)} %constant_dynamic-slice_fusion.slots, bf16[21,21,192]{2,1,0:T(8,128)(2,1)S(1)} %collective-permute-done.before, ...), custom_call_target="tpu_custom_call" | custom-call | tf_op jit(solution)/shard_map/conv/pallas_call | solution.py:106
  48.9 1.0 copy-done
  50.8 22.4 %all-gather.6 = f16[1536,896]{1,0:T(8,128)(2,1)} all-gather(f16[192,896]{1,0:T(8,128)(2,1)S(1)} %copy.18), channel_id=1, replica_groups=mesh['y'=4,'z'=16,'x'=4,'core'=2] {'x','core'}, dimensions={0}, use_global_device_ids=true | all-gather | bytes 3096576 | tf_op jit(solution)/shard_map/all_gather | solution.py:271
  73.2 4.1 %copy.19 = f16[1536,896]{0,1:T(8,128)(2,1)S(1)} copy(f16[1536,896]{1,0:T(8,128)(2,1)} %all-gather.6) | data formatting | bytes 5505024 | tf_op jit(solution)/shard_map/all_gather | solution.py:271
  77.7 0.9 fusion.2
  78.8 4.2 %fusion.6.normed = bf16[896,1536]{1,0:T(8,128)(2,1)S(1)} fusion(f16[1536,896]{0,1:T(8,128)(2,1)} %copy-done.4, f32[1536]{0:T(1024)S(1)} %convert_element_type.23, f32[1536]{0:T(1024)S(1)} %convert_element_type.22, f32[896]{0:T(1024)S(1)} %add_sqrt_fusion, f32[896]{0:T(1024)S(1)} %broadcast_multiply_fusion), kind=kLoop, calls=%fused_computation.8 | loop fusion | flops 8257536 | bytes 5524480 | tf_op jit(solution)/shard_map/transpose | solution.py:277
  83.0 14.0 %all-gather.5.cloned.1.call-done = bf16[2,4,384,768]{3,2,1,0:T(8,128)(2,1)} async-done(((bf16[2,4,24,768]{3,2,1,0:T(8,128)(2,1)}), bf16[2,4,384,768]{3,2,1,0:T(8,128)(2,1)}) %all-gather.5.cloned.1.call-update) | async-done | bytes 4718608 | tf_op jit(solution)/shard_map/all_gather | solution.py:22
  97.0 5.7 %up_and_down.1 = (bf16[896,768]{1,0:T(8,128)(2,1)S(1)}, bf16[4,192,896]{2,1,0:T(8,128)(2,1)S(1)}) custom-call(s32[1]{0:T(128)} %bitcast.core, bf16[896,1536]{1,0:T(8,128)(2,1)S(1)} %fusion.6.normed, f32[1,768]{1,0:T(1,128)S(1)} %reshape.39.b_up, bf16[2,1536,768]{2,1,0:T(8,128)(2,1)} %bitcast.19), custom_call_target="tpu_custom_call" | custom-call | tf_op jit(solution)/shard_map/up_and_down/pallas_call | solution.py:212
  102.8 10.4 %collective-permute-start.2 = (bf16[4,192,896]{2,1,0:T(8,128)(2,1)S(1)}, bf16[4,192,896]{2,1,0:T(8,128)(2,1)S(1)}, u32[]{:S(2)}, u32[]{:S(2)}) collective-permute-start(bf16[4,192,896]{2,1,0:T(8,128)(2,1)S(1)} %get-tuple-element.11), channel_id=1, source_target_pairs={{0,1},{1,0},{2,3},{3,2},{4,5},{5,4},{6,7},{7,6},{8,9},{9,8},{10,11... | collective-permute-start | bytes 4128776 | tf_op jit(solution)/shard_map/ppermute | solution.py:16
  113.2 2.7 %down_own.1.mine = bf16[4,192,896]{2,1,0:T(8,128)(2,1)S(1)} custom-call(s32[1]{0:T(128)} %bitcast.core, bf16[896,768]{1,0:T(8,128)(2,1)S(1)} %get-tuple-element.10.hidden, bf16[2,1536,768]{2,1,0:T(8,128)(2,1)} %bitcast.20), custom_call_target="tpu_custom_call" | custom-call | tf_op jit(solution)/shard_map/down_own/pallas_call | solution.py:227
  115.9 1.4 pair.1
  117.3 4.1 %all-to-all-start = ((bf16[4,192,896]{2,1,0:T(8,128)(2,1)}), bf16[4,192,896]{2,1,0:T(8,128)(2,1)S(1)}, u32[]{:S(2)}, u32[]{:S(2)}) async-start(bf16[4,192,896]{2,1,0:T(8,128)(2,1)} %pair.1), calls=%async_computation | async-start | bytes 2752512 | tf_op jit(solution)/shard_map/all_to_all | solution.py:244
  121.8 17.8 %all-to-all-done.parts = bf16[4,192,896]{2,1,0:T(8,128)(2,1)S(1)} async-done(((bf16[4,192,896]{2,1,0:T(8,128)(2,1)}), bf16[4,192,896]{2,1,0:T(8,128)(2,1)S(1)}, u32[]{:S(2)}, u32[]{:S(2)}) %all-to-all-start) | async-done | bytes 1376288 | tf_op jit(solution)/shard_map/all_to_all | solution.py:244
  140.3 1.1 copy.22
  (33 shorter events, 5.2 us)
Async XLA Ops:
  6.5 90.5 %all-gather.5.cloned.1.call-start = ((), (), s32[]{:S(2)}) async-start(), calls=%async_computation.1 | async-start | bytes 5013504 | tf_op jit(solution)/shard_map/all_gather | solution.py:22
  21.5 17.8 %collective-permute-start = (bf16[21,21,192]{2,1,0:T(8,128)(2,1)S(1)}, bf16[21,21,192]{2,1,0:T(8,128)(2,1)S(1)}, u32[]{:S(2)}, u32[]{:S(2)}) collective-permute-start(bf16[21,21,192]{2,1,0:T(8,128)(2,1)S(1)} %get-tuple-element.14), channel_id=1, source_target_pairs={{0,8},{8,16},{16,24},{24,32},{32,40},{40,48},{48,56},{56,64},{64,7... | collective-permute-start | bytes 508040 | tf_op jit(solution)/shard_map/ppermute | solution.py:37
  25.0 14.2 %collective-permute-start.1 = (bf16[21,21,192]{2,1,0:T(8,128)(2,1)S(1)}, bf16[21,21,192]{2,1,0:T(8,128)(2,1)S(1)}, u32[]{:S(2)}, u32[]{:S(2)}) collective-permute-start(bf16[21,21,192]{2,1,0:T(8,128)(2,1)S(1)} %get-tuple-element.13), channel_id=1, source_target_pairs={{8,0},{16,8},{24,16},{32,24},{40,32},{48,40},{56,48},{64,56},{72,6... | collective-permute-start | bytes 508040 | tf_op jit(solution)/shard_map/ppermute | solution.py:40
  39.2 0.7 copy-start.2
  39.9 0.7 copy-start.3
  48.9 1.0 copy-start
  77.2 1.6 %copy-start.4 = (f16[1536,896]{0,1:T(8,128)(2,1)}, f16[1536,896]{0,1:T(8,128)(2,1)S(1)}, u32[]{:S(2)}) copy-start(f16[1536,896]{0,1:T(8,128)(2,1)S(1)} %copy.19) | copy-start | bytes 8257540
  102.8 13.1 %collective-permute-start.2 = (bf16[4,192,896]{2,1,0:T(8,128)(2,1)S(1)}, bf16[4,192,896]{2,1,0:T(8,128)(2,1)S(1)}, u32[]{:S(2)}, u32[]{:S(2)}) collective-permute-start(bf16[4,192,896]{2,1,0:T(8,128)(2,1)S(1)} %get-tuple-element.11), channel_id=1, source_target_pairs={{0,1},{1,0},{2,3},{3,2},{4,5},{5,4},{6,7},{7,6},{8,9},{9,8},{10,11... | collective-permute-start | bytes 4128776 | tf_op jit(solution)/shard_map/ppermute | solution.py:16
  115.9 5.5 %copy-start.6 = (bf16[192]{0:T(256)(128)(2,1)S(1)}, bf16[192]{0:T(256)(128)(2,1)}, u32[]{:S(2)}) copy-start(bf16[192]{0:T(256)(128)(2,1)} %param.24) | copy-start | bytes 1156
  115.9 5.7 %copy-start.5 = (f32[192]{0:T(256)S(1)}, f32[192]{0:T(256)}, u32[]{:S(2)}) copy-start(f32[192]{0:T(256)} %param.25) | copy-start | bytes 2308
  115.9 5.8 %copy-start.1 = (f32[2,21,21,192]{3,2,1,0:T(8,128)S(1)}, f32[2,21,21,192]{3,2,1,0:T(8,128)}, u32[]{:S(2)}) copy-start(f32[2,21,21,192]{3,2,1,0:T(8,128)} %copy-done) | copy-start | bytes 2032132
  117.3 22.3 %all-to-all-start = ((bf16[4,192,896]{2,1,0:T(8,128)(2,1)}), bf16[4,192,896]{2,1,0:T(8,128)(2,1)S(1)}, u32[]{:S(2)}, u32[]{:S(2)}) async-start(bf16[4,192,896]{2,1,0:T(8,128)(2,1)} %pair.1), calls=%async_computation | async-start | bytes 2752512 | tf_op jit(solution)/shard_map/all_to_all | solution.py:244
Sparse Core Ops, SparseCore 0:
  17.6 79.3 all-gather.4

commit v7 on v5

--- a/solution.py
+++ b/solution.py
@@ -24,11 +24,7 @@
 
 
 def gather_y(own):
-    behind = shift(own, "y", 1, NY)
-    ahead = shift(own, "y", -1, NY)
-    far_up = shift(behind[0], "y", 1, NY)
-    far_down = shift(ahead[1], "y", -1, NY)
-    return own, ahead, behind, far_up, far_down
+    return own, *(shift(own, "y", -d, NY) for d in (1, 2, 3))
 
 
 def exchange(slots, seq_index, first_crop):
@@ -124,31 +120,51 @@
             pltpu.VMEM((KSIDE, PER_DEV, side + 6, columns, width), f32),
             pltpu.VMEM((KSIDE * KSIDE, 8, width), f32),
         ],
-        compiler_params=pltpu.CompilerParams(vmem_limit_bytes=48 * 2**20),
+        compiler_params=vmem(16),
         name="conv",
     )(seq_index.astype(jnp.int32).reshape(1), first_crop, crop_counts, slots, before, after, table)
 
 
+def vmem(mebibytes):
+    return pltpu.CompilerParams(vmem_limit_bytes=mebibytes * 2**20)
+
+
 def whole(space=pltpu.VMEM):
     return pl.BlockSpec(memory_space=space)
 
 
-def split_blocks(blocks):
-    own, ahead, behind, far_up, far_down = blocks
-    ups = (own.at[0], ahead.at[0], far_up, behind.at[0])
-    downs = (own.at[1], ahead.at[1], far_down, behind.at[1])
-    return ups, downs
+def norm_kernel(conv, gain, bias, normed):
+    channels, cells = conv.shape
+    step = 128
+    for c in range(0, cells, step):
+        block = conv[:, c : c + step]
+        mean = jnp.sum(block, axis=0, keepdims=True) * (1.0 / channels)
+        block = block - mean
+        var = jnp.sum(block * block, axis=0, keepdims=True) * (1.0 / channels)
+        block = block * lax.rsqrt(var + 1e-6)
+        normed[c : c + step, :] = (block.T * gain[...] + bias[...]).astype(normed.dtype)
+
+
+def layer_norm(conv, gain, bias):
+    return pl.pallas_call(
+        norm_kernel,
+        out_shape=jax.ShapeDtypeStruct(conv.shape[::-1], jnp.bfloat16),
+        in_specs=[whole()] * 3,
+        out_specs=whole(),
+        compiler_params=vmem(20),
+        name="norm",
+    )(conv, gain.astype(jnp.float32)[None, :], bias.astype(jnp.float32)[None, :])
 
 
 def copy_down_rows(blocks, buffer, sems, y, core):
     width = buffer.shape[0] // NX
     copies = []
-    for d, block in enumerate(split_blocks(blocks)[1]):
+    for d, block in enumerate(blocks):
         source = pl.multiple_of(core * width, width)
         target = pl.multiple_of(lax.rem(y + d, NY) * width, width)
         copies.append(
             pltpu.make_async_copy(
-                block.at[pl.ds(source, width), :], buffer.at[pl.ds(target, width), :], sems.at[d]
+                block.at[1, pl.ds(source, width), :], buffer.at[pl.ds(target, width), :], sems.at[d]
             )
         )
     return copies
@@ -164,13 +180,13 @@
 
 
 def first_kernel(place, normed, b_up, *refs):
-    blocks, (hidden, out, up, down, up_sem, down_sem) = refs[:5], refs[5:]
+    blocks, (hidden, out, up, down, up_sem, down_sem) = refs[:NY], refs[NY:]
     y, core = place[0], place[2]
     ups = []
-    for d, block in enumerate(split_blocks(blocks)[0]):
-        rows = block.shape[0]
+    for d, block in enumerate(blocks):
+        rows = block.shape[1]
         target = pl.multiple_of(lax.rem(y + d, NY) * rows, rows)
-        ups.append(pltpu.make_async_copy(block, up.at[pl.ds(target, rows), :], up_sem.at[d]))
+        ups.append(pltpu.make_async_copy(block.at[0], up.at[pl.ds(target, rows), :], up_sem.at[d]))
     for copy in ups:
         copy.start()
     downs = copy_down_rows(blocks, down, down_sem, y, 1 - core)
@@ -191,7 +207,7 @@
 
 
 def second_kernel(place, hidden, *refs):
-    blocks, (out, down, down_sem) = refs[:5], refs[5:]
+    blocks, (out, down, down_sem) = refs[:NY], refs[NY:]
     downs = copy_down_rows(blocks, down, down_sem, place[0], place[2])
     for copy in downs:
         copy.start()
@@ -223,7 +239,6 @@
     bf16, f32 = jnp.bfloat16, jnp.float32
     cells, units = normed.shape[0], b_up.shape[0]
     place = jnp.stack([lax.axis_index(a).astype(jnp.int32) for a in ("y", "x", "core")])
-    params = pltpu.CompilerParams(vmem_limit_bytes=48 * 2**20)
     half_out = jax.ShapeDtypeStruct((NX, width, cells), bf16)
     down = pltpu.VMEM((NX * width, units), bf16)
     hidden, other = pl.pallas_call(
@@ -237,7 +252,7 @@
             pltpu.SemaphoreType.DMA((4,)),
             pltpu.SemaphoreType.DMA((NX,)),
         ],
-        compiler_params=params,
+        compiler_params=vmem(20),
         name="up_and_down",
     )(place, normed, b_up.astype(f32)[None, :], *blocks)
     other = shift(other, "core", 1, NCORE)
@@ -247,7 +262,7 @@
         in_specs=[whole(pltpu.SMEM), whole()] + [whole(pl.ANY)] * len(blocks),
         out_specs=whole(),
         scratch_shapes=[down, pltpu.SemaphoreType.DMA((NX,))],
-        compiler_params=params,
+        compiler_params=vmem(12),
         name="down_own",
     )(place, hidden, *blocks)
     block = jax.ShapeDtypeStruct((width, cells), bf16)
@@ -256,7 +271,7 @@
         out_shape=(jax.ShapeDtypeStruct((width, cells), f32),) + (block,) * len(DISTANCES),
         in_specs=[whole(pltpu.SMEM), whole(), whole()],
         out_specs=(whole(),) * (1 + len(DISTANCES)),
-        compiler_params=params,
+        compiler_params=vmem(12),
         name="pair",
     )(place, mine, other)
     return own, *(shift(block, "x", d, NX) for d, block in zip(DISTANCES, sent))
@@ -287,19 +302,14 @@
     conv_t = jnp.pad(conv[:, :, :side].reshape(cells, width), ((0, padding), (0, 0))).T
     conv_t = conv_t.astype(jnp.float16)
     conv_all = lax.all_gather(conv_t, TP, axis=0, tiled=True).astype(f32)
-    mean = jnp.mean(conv_all, axis=0, keepdims=True)
-    var = jnp.mean((conv_all - mean) ** 2, axis=0, keepdims=True)
-    normed = (
-        (conv_all - mean) / jnp.sqrt(var + 1e-6) * ln_gain.astype(f32)[:, None]
-        + ln_bias.astype(f32)[:, None]
-    ).astype(jnp.bfloat16).T
+    normed = layer_norm(conv_all, ln_gain, ln_bias)
     sums = mlp_sum(normed, blocks, b_up, width)
     result = pl.pallas_call(
         last_kernel,
         out_shape=jax.ShapeDtypeStruct((cells, width), jnp.bfloat16),
         in_specs=[whole()] * (len(sums) + 3),
         out_specs=whole(),
-        compiler_params=pltpu.CompilerParams(vmem_limit_bytes=48 * 2**20),
+        compiler_params=vmem(12),
         name="result",
     )(*sums, b_down.astype(f32)[:, None], gamma[:, None], block_in.reshape(cells, width))
     return result.reshape(PER_DEV, side, side, width)

time: 173 us -> 146 us (0.84)
  waiting for transfers between devices: 21.1 us -> 11 us
  other arithmetic: 12.4 us -> 3.74 us
  local copies, waits for them, and re-layouts: 19.2 us -> 14.6 us
  starting transfers between devices: 30.6 us -> 28 us
    ppermute x8 -> x7, waiting for transfers between devices: 21.1 us -> 11 us  [shift(): lax.ppermute(block, axis, [(i, (i + distance) % size) for i in range(size)])]
    all_gather x1 -> x0, local copies, waits for them, and re-layouts: 4.96 us -> none  [per_device(): conv_all = lax.all_gather(conv_t, TP, axis=0, tiled=True).astype(f32)]
    transpose x1 -> x0, other arithmetic: 4.38 us -> none  [per_device(): normed = ((conv_all - mean) / jnp.sqrt(var + 1e-06) * ln_gain.astype(f32)...]
    reduce_sum x2 -> x0, other arithmetic: 3.22 us -> none  [the longest x1 2.36 us: per_device(): mean = jnp.mean(conv_all, axis=0, keepdims=True)]
    convert_element_type x2 -> x1, local copies, waits for them, and re-layouts: 3.93 us -> 1.04 us  [per_device(): conv_t = conv_t.astype(jnp.float16)]
    ppermute x8 -> x7, starting transfers between devices: 23.2 us -> 20.6 us  [shift(): lax.ppermute(block, axis, [(i, (i + distance) % size) for i in range(size)])]
    pallas_call x0 -> x1, Pallas kernels: none -> 2.3 us  [layer_norm(): pl.pallas_call(norm_kernel, out_shape=jax.ShapeDtypeStruct(conv.shape[::-...]
    reshape x1 -> x2, local copies, waits for them, and re-layouts: 2.05 us -> 4.07 us  [per_device(): conv[:, :, :side].reshape(cells, width)]
  transfers between devices with their start and end apart: 10 -> 9, of which waited for: 4 -> 2; matrix products, arithmetic and copies ran while one was open for 16% -> 10% of each run, Pallas kernels for 7% -> 10%
where the time goes in v7:
time: 146 us; the launch traced here: 144 us
  blocking collectives  62.4 us (43%)
  starting transfers between devices  28 us (19%)
  Pallas kernels  22.6 us (15%)
  local copies, waits for them, and re-layouts  14.6 us (10%)
  waiting for transfers between devices  11 us (8%)
  other arithmetic  3.74 us (3%)
  between operations  1.68 us (1%)
    all_gather x1, blocking collectives, gather_z(): over_z = lax.all_gather(both.astype(jnp.float16), 'z', axis=1, tiled=True)  36 us
    all_gather x1, blocking collectives, per_device(): conv_all = lax.all_gather(conv_t, TP, axis=0, tiled=True).astype(f32)  26.4 us
    ppermute x7, starting transfers between devices, shift(): lax.ppermute(block, axis, [(i, (i + distance) % size) for i in range(size)])  20.6 us
    ppermute x7, waiting for transfers between devices, shift(): lax.ppermute(block, axis, [(i, (i + distance) % size) for i in range(size)])  11 us
    pallas_call x1, Pallas kernels, depthwise(): pl.pallas_call(conv_kernel, out_shape=(jax.ShapeDtypeStruct((PER_DEV, sid...  8.37 us
    pallas_call x1, Pallas kernels, mlp_sum(): pl.pallas_call(first_kernel, out_shape=(jax.ShapeDtypeStruct((cells, unit...  5.84 us
    ppermute x1, starting transfers between devices, exchange(): lax.ppermute(crop(target - 1), SEQ, [(i + 1, i) for i in range(count - 1)])  5.47 us
    reshape x2, local copies, waits for them, and re-layouts, per_device(): conv[:, :, :side].reshape(cells, width)  4.07 us
  transfers between devices with their start and end apart: 9, of which 2 were waited for; matrix products, arithmetic and copies ran while one was open for 10% of the time, Pallas kernels for 10%

profile of v7, /device:TPU:25, one launch (start us, length us, event | category | flops | bytes accessed | tf_op | source)
XLA Modules:
  0.0 144.0 jit_solution(6967425694285623709)
XLA Ops:
  0.8 36.0 %all-gather.3 = f16[2,384,768]{2,1,0:T(8,128)(2,1)S(1)} all-gather(f16[2,24,768]{2,1,0:T(8,128)(2,1)S(1)} %multiply_convert_fusion.1), channel_id=1, replica_groups=mesh['y'=4,'z'=16,'x'=4,'core'=2] {'z'}, dimensions={1}, use_global_device_ids=true | all-gather | bytes 1253376 | tf_op jit(solution)/shard_map/all_gather | solution.py:22
  37.0 2.4 %collective-permute-start.2 = (bf16[2,384,768]{2,1,0:T(8,128)(2,1)S(1)}, bf16[2,384,768]{2,1,0:T(8,128)(2,1)S(1)}, u32[]{:S(2)}, u32[]{:S(2)}) collective-permute-start(bf16[2,384,768]{2,1,0:T(8,128)(2,1)S(1)} %multiply_convert_fusion.refs_0_), channel_id=1, source_target_pairs={{0,384},{128,0},{256,128},{384,256},{1,385},{129,1},{257,129},{385... | collective-permute-start | bytes 3538952 | tf_op jit(solution)/shard_map/ppermute | solution.py:17
  39.4 2.6 %collective-permute-start.3 = (bf16[2,384,768]{2,1,0:T(8,128)(2,1)S(1)}, bf16[2,384,768]{2,1,0:T(8,128)(2,1)S(1)}, u32[]{:S(2)}, u32[]{:S(2)}) collective-permute-start(bf16[2,384,768]{2,1,0:T(8,128)(2,1)S(1)} %multiply_convert_fusion.refs_0_), channel_id=1, source_target_pairs={{0,256},{128,384},{256,0},{384,128},{1,257},{129,385},{257,1},{385... | collective-permute-start | bytes 3538952 | tf_op jit(solution)/shard_map/ppermute | solution.py:17
  42.0 3.8 %collective-permute-start.4 = (bf16[2,384,768]{2,1,0:T(8,128)(2,1)S(1)}, bf16[2,384,768]{2,1,0:T(8,128)(2,1)}, u32[]{:S(2)}, u32[]{:S(2)}) collective-permute-start(bf16[2,384,768]{2,1,0:T(8,128)(2,1)S(1)} %multiply_convert_fusion.refs_0_), channel_id=1, source_target_pairs={{0,128},{128,256},{256,384},{384,0},{1,129},{129,257},{257,385},{3... | collective-permute-start | bytes 3538952 | tf_op jit(solution)/shard_map/ppermute | solution.py:17
  47.8 1.3 dynamic-slice_bitcast_fusion
  49.1 1.9 %collective-permute-start = (bf16[21,21,192]{2,1,0:T(8,128)(2,1)S(1)}, bf16[21,21,192]{2,1,0:T(8,128)(2,1)S(1)}, u32[]{:S(2)}, u32[]{:S(2)}) collective-permute-start(bf16[21,21,192]{2,1,0:T(8,128)(2,1)S(1)} %get-tuple-element.22), channel_id=1, source_target_pairs={{0,8},{8,16},{16,24},{24,32},{32,40},{40,48},{48,56},{56,64},{64,7... | collective-permute-start | bytes 508040 | tf_op jit(solution)/shard_map/ppermute | solution.py:41
  51.0 5.5 %collective-permute-start.1 = (bf16[21,21,192]{2,1,0:T(8,128)(2,1)S(1)}, bf16[21,21,192]{2,1,0:T(8,128)(2,1)S(1)}, u32[]{:S(2)}, u32[]{:S(2)}) collective-permute-start(bf16[21,21,192]{2,1,0:T(8,128)(2,1)S(1)} %get-tuple-element.21), channel_id=1, source_target_pairs={{8,0},{16,8},{24,16},{32,24},{40,32},{48,40},{56,48},{64,56},{72,6... | collective-permute-start | bytes 508040 | tf_op jit(solution)/shard_map/ppermute | solution.py:44
  60.1 1.3 reshape.19.b_up
  61.4 1.6 %constant_dynamic-slice_fusion.slots = bf16[3,21,21,192]{3,2,1,0:T(8,128)(2,1)S(1)} fusion(bf16[3,21,21,1536]{3,2,1,0:T(8,128)(2,1)} %param.13, s32[]{:T(128)S(6)} %select_n.12), kind=kLoop, calls=%fused_computation.11 | loop fusion | bytes 1016068 | tf_op jit(solution)/shard_map/dynamic_slice | solution.py:292
  63.0 8.4 %conv.1 = (f32[2,21,21,192]{3,2,1,0:T(8,128)S(1)}, f32[2,21,24,192]{3,2,1,0:T(8,128)S(1)}) custom-call(s32[1]{0:T(128)} %bitcast.3.seq, s32[64]{0:T(128)S(1)} %copy-done.5, s32[64]{0:T(128)S(1)} %copy-done.6, bf16[3,21,21,192]{3,2,1,0:T(8,128)(2,1)S(1)} %constant_dynamic-slice_fusion.slots, bf16[21,21,192]{2,1,0:T(8,128)(2,1)S(1)} %collective-permute-done.before, ...), custom_call_target="tpu_custom_call" | custom-call | tf_op jit(solution)/shard_map/conv/pallas_call | solution.py:110
  73.2 2.0 %reshape.14 = f16[882,192]{1,0:T(8,128)(2,1)} reshape(f16[2,21,21,192]{3,2,1,0:T(8,128)(2,1)} %slice_convert_fusion) | data formatting | bytes 677376 | tf_op jit(solution)/shard_map/reshape | solution.py:302
  75.2 2.0 %copy.16 = f16[882,192]{0,1:T(8,128)(2,1)} copy(f16[882,192]{1,0:T(8,128)(2,1)} %reshape.14) | data formatting | bytes 677376 | tf_op jit(solution)/shard_map/reshape | solution.py:302
  78.3 26.4 %all-gather.2 = f16[1536,896]{1,0:T(8,128)(2,1)S(1)} all-gather(f16[192,896]{1,0:T(8,128)(2,1)S(1)} %pad_bitcast_fusion), channel_id=1, replica_groups=mesh['y'=4,'z'=16,'x'=4,'core'=2] {'x','core'}, dimensions={0}, use_global_device_ids=true | all-gather | bytes 3096576 | tf_op jit(solution)/shard_map/all_gather | solution.py:304
  105.1 2.3 %norm.1.normed = bf16[896,1536]{1,0:T(8,128)(2,1)S(1)} custom-call(f32[1536,896]{1,0:T(8,128)S(1)} %convert_element_type.26.conv, f32[1,1536]{1,0:T(1,128)S(1)} %reshape.17.gain, f32[1,1536]{1,0:T(1,128)S(1)} %reshape.18.bias), custom_call_target="tpu_custom_call" | custom-call | tf_op jit(solution)/shard_map/norm/pallas_call | solution.py:149
  107.4 5.8 %up_and_down.1 = (bf16[896,768]{1,0:T(8,128)(2,1)S(1)}, bf16[4,192,896]{2,1,0:T(8,128)(2,1)S(1)}) custom-call(s32[3]{0:T(128)S(1)} %copy-done.3, bf16[896,1536]{1,0:T(8,128)(2,1)S(1)} %norm.1.normed, f32[1,768]{1,0:T(1,128)S(1)} %copy-done.2, bf16[2,384,768]{2,1,0:T(8,128)(2,1)S(1)} %multiply_convert_fusion.refs_0_, ...), custom_call_target="tpu_custom_call" | custom-call | tf_op jit(solution)/shard_map/up_and_down/pallas_call | solution.py:244
  113.3 2.2 %collective-permute-start.5 = (bf16[4,192,896]{2,1,0:T(8,128)(2,1)S(1)}, bf16[4,192,896]{2,1,0:T(8,128)(2,1)S(1)}, u32[]{:S(2)}, u32[]{:S(2)}) collective-permute-start(bf16[4,192,896]{2,1,0:T(8,128)(2,1)S(1)} %get-tuple-element.15), channel_id=1, source_target_pairs={{0,1},{1,0},{2,3},{3,2},{4,5},{5,4},{6,7},{7,6},{8,9},{9,8},{10,11... | collective-permute-start | bytes 4128776 | tf_op jit(solution)/shard_map/ppermute | solution.py:17
  115.5 3.2 %down_own.1.mine = bf16[4,192,896]{2,1,0:T(8,128)(2,1)S(1)} custom-call(s32[3]{0:T(128)S(1)} %copy-done.3, bf16[896,768]{1,0:T(8,128)(2,1)S(1)} %get-tuple-element.14.hidden, bf16[2,384,768]{2,1,0:T(8,128)(2,1)S(1)} %multiply_convert_fusion.refs_0_, bf16[2,384,768]{2,1,0:T(8,128)(2,1)S(1)} %collective-permute-done.2.refs_1_, ...), custom_call_target="tpu_custom_call" | custom-call | tf_op jit(solution)/shard_map/down_own/pallas_call | solution.py:259
  118.7 1.6 %pair.1 = (f32[192,896]{1,0:T(8,128)S(1)}, bf16[192,896]{1,0:T(8,128)(2,1)}, bf16[192,896]{1,0:T(8,128)(2,1)}, bf16[192,896]{1,0:T(8,128)(2,1)}) custom-call(s32[3]{0:T(128)S(1)} %copy-done.3, bf16[4,192,896]{2,1,0:T(8,128)(2,1)S(1)} %down_own.1.mine, bf16[4,192,896]{2,1,0:T(8,128)(2,1)S(1)} %collective-permute-done.5.other), custom_call_target="tpu_custom_call" | custom-call | tf_op jit(solution)/shard_map/pair/pallas_call | solution.py:269
  120.3 3.1 %collective-permute-start.6 = (bf16[192,896]{1,0:T(8,128)(2,1)}, bf16[192,896]{1,0:T(8,128)(2,1)S(1)}, u32[]{:S(2)}, u32[]{:S(2)}) collective-permute-start(bf16[192,896]{1,0:T(8,128)(2,1)} %get-tuple-element.17), channel_id=1, source_target_pairs={{0,4},{2,6},{4,0},{6,2},{1,5},{3,7},{5,1},{7,3},{8,12},{10,14},{12... | collective-permute-start | bytes 1032200 | tf_op jit(solution)/shard_map/ppermute | solution.py:17
  123.4 2.1 %collective-permute-start.7 = (bf16[192,896]{1,0:T(8,128)(2,1)}, bf16[192,896]{1,0:T(8,128)(2,1)S(1)}, u32[]{:S(2)}, u32[]{:S(2)}) collective-permute-start(bf16[192,896]{1,0:T(8,128)(2,1)} %get-tuple-element.18), channel_id=1, source_target_pairs={{0,2},{2,4},{4,6},{6,0},{1,3},{3,5},{5,7},{7,1},{8,10},{10,12},{12... | collective-permute-start | bytes 1032200 | tf_op jit(solution)/shard_map/ppermute | solution.py:17
  125.6 4.3 %collective-permute-start.8 = (bf16[192,896]{1,0:T(8,128)(2,1)}, bf16[192,896]{1,0:T(8,128)(2,1)}, u32[]{:S(2)}, u32[]{:S(2)}) collective-permute-start(bf16[192,896]{1,0:T(8,128)(2,1)} %get-tuple-element.19), channel_id=1, source_target_pairs={{0,6},{2,0},{4,2},{6,4},{1,7},{3,1},{5,3},{7,5},{8,14},{10,8},{12,... | collective-permute-start | bytes 1032200 | tf_op jit(solution)/shard_map/ppermute | solution.py:17
  130.4 2.9 %collective-permute-done.6.first = bf16[192,896]{1,0:T(8,128)(2,1)S(1)} collective-permute-done((bf16[192,896]{1,0:T(8,128)(2,1)}, bf16[192,896]{1,0:T(8,128)(2,1)S(1)}, u32[]{:S(2)}, u32[]{:S(2)}) %collective-permute-start.6) | collective-permute-done | bytes 344096 | tf_op jit(solution)/shard_map/ppermute | solution.py:17
  133.3 8.0 %collective-permute-done.7.second = bf16[192,896]{1,0:T(8,128)(2,1)S(1)} collective-permute-done((bf16[192,896]{1,0:T(8,128)(2,1)}, bf16[192,896]{1,0:T(8,128)(2,1)S(1)}, u32[]{:S(2)}, u32[]{:S(2)}) %collective-permute-start.7) | collective-permute-done | bytes 344096 | tf_op jit(solution)/shard_map/ppermute | solution.py:17
  141.3 1.4 result.1
  (44 shorter events, 10.1 us)
Async XLA Ops:
  36.8 9.0 %copy-start.4 = (s32[64]{0:T(128)S(1)}, s32[64]{0:T(128)}, u32[]{:S(2)}) copy-start(s32[64]{0:T(128)} %first_crop.1) | copy-start | bytes 772
  36.8 20.4 %copy-start.7 = (bf16[3,1536]{1,0:T(4,128)(2,1)S(1)}, bf16[3,1536]{1,0:T(4,128)(2,1)}, u32[]{:S(2)}) copy-start(bf16[3,1536]{1,0:T(4,128)(2,1)} %param.16) | copy-start | bytes 27652
  37.0 70.4 %collective-permute-start.2 = (bf16[2,384,768]{2,1,0:T(8,128)(2,1)S(1)}, bf16[2,384,768]{2,1,0:T(8,128)(2,1)S(1)}, u32[]{:S(2)}, u32[]{:S(2)}) collective-permute-start(bf16[2,384,768]{2,1,0:T(8,128)(2,1)S(1)} %multiply_convert_fusion.refs_0_), channel_id=1, source_target_pairs={{0,384},{128,0},{256,128},{384,256},{1,385},{129,1},{257,129},{385... | collective-permute-start | bytes 3538952 | tf_op jit(solution)/shard_map/ppermute | solution.py:17
  39.4 68.0 %collective-permute-start.3 = (bf16[2,384,768]{2,1,0:T(8,128)(2,1)S(1)}, bf16[2,384,768]{2,1,0:T(8,128)(2,1)S(1)}, u32[]{:S(2)}, u32[]{:S(2)}) collective-permute-start(bf16[2,384,768]{2,1,0:T(8,128)(2,1)S(1)} %multiply_convert_fusion.refs_0_), channel_id=1, source_target_pairs={{0,256},{128,384},{256,0},{384,128},{1,257},{129,385},{257,1},{385... | collective-permute-start | bytes 3538952 | tf_op jit(solution)/shard_map/ppermute | solution.py:17
  42.0 65.4 %collective-permute-start.4 = (bf16[2,384,768]{2,1,0:T(8,128)(2,1)S(1)}, bf16[2,384,768]{2,1,0:T(8,128)(2,1)}, u32[]{:S(2)}, u32[]{:S(2)}) collective-permute-start(bf16[2,384,768]{2,1,0:T(8,128)(2,1)S(1)} %multiply_convert_fusion.refs_0_), channel_id=1, source_target_pairs={{0,128},{128,256},{256,384},{384,0},{1,129},{129,257},{257,385},{3... | collective-permute-start | bytes 3538952 | tf_op jit(solution)/shard_map/ppermute | solution.py:17
  47.7 15.2 %copy-start.5 = (s32[64]{0:T(128)S(1)}, s32[64]{0:T(128)}, u32[]{:S(2)}) copy-start(s32[64]{0:T(128)} %first_crop.1) | copy-start | bytes 772
  47.7 15.2 %copy-start.6 = (s32[64]{0:T(128)S(1)}, s32[64]{0:T(128)}, u32[]{:S(2)}) copy-start(s32[64]{0:T(128)} %crop_counts.1) | copy-start | bytes 772
  49.1 13.8 %collective-permute-start = (bf16[21,21,192]{2,1,0:T(8,128)(2,1)S(1)}, bf16[21,21,192]{2,1,0:T(8,128)(2,1)S(1)}, u32[]{:S(2)}, u32[]{:S(2)}) collective-permute-start(bf16[21,21,192]{2,1,0:T(8,128)(2,1)S(1)} %get-tuple-element.22), channel_id=1, source_target_pairs={{0,8},{8,16},{16,24},{24,32},{32,40},{40,48},{48,56},{56,64},{64,7... | collective-permute-start | bytes 508040 | tf_op jit(solution)/shard_map/ppermute | solution.py:41
  51.0 11.9 %collective-permute-start.1 = (bf16[21,21,192]{2,1,0:T(8,128)(2,1)S(1)}, bf16[21,21,192]{2,1,0:T(8,128)(2,1)S(1)}, u32[]{:S(2)}, u32[]{:S(2)}) collective-permute-start(bf16[21,21,192]{2,1,0:T(8,128)(2,1)S(1)} %get-tuple-element.21), channel_id=1, source_target_pairs={{8,0},{16,8},{24,16},{32,24},{40,32},{48,40},{56,48},{64,56},{72,6... | collective-permute-start | bytes 508040 | tf_op jit(solution)/shard_map/ppermute | solution.py:44
  71.4 0.9 copy-start
  105.1 2.4 %copy-start.2 = (f32[1,768]{1,0:T(1,128)S(1)}, f32[1,768]{1,0:T(1,128)}, u32[]{:S(2)}) copy-start(f32[1,768]{1,0:T(1,128)} %reshape.19.b_up) | copy-start | bytes 9220
  105.1 2.4 %copy-start.3 = (s32[3]{0:T(128)S(1)}, s32[3]{0:T(128)}, u32[]{:S(2)}) copy-start(s32[3]{0:T(128)} %pad_add_fusion.place) | copy-start | bytes 40
  113.3 5.5 %collective-permute-start.5 = (bf16[4,192,896]{2,1,0:T(8,128)(2,1)S(1)}, bf16[4,192,896]{2,1,0:T(8,128)(2,1)S(1)}, u32[]{:S(2)}, u32[]{:S(2)}) collective-permute-start(bf16[4,192,896]{2,1,0:T(8,128)(2,1)S(1)} %get-tuple-element.15), channel_id=1, source_target_pairs={{0,1},{1,0},{2,3},{3,2},{4,5},{5,4},{6,7},{7,6},{8,9},{9,8},{10,11... | collective-permute-start | bytes 4128776 | tf_op jit(solution)/shard_map/ppermute | solution.py:17
  118.7 11.2 %copy-start.9 = (bf16[192]{0:T(256)(128)(2,1)S(1)}, bf16[192]{0:T(256)(128)(2,1)}, u32[]{:S(2)}) copy-start(bf16[192]{0:T(256)(128)(2,1)} %param.24) | copy-start | bytes 1156
  118.7 11.4 %copy-start.8 = (f32[192]{0:T(256)S(1)}, f32[192]{0:T(256)}, u32[]{:S(2)}) copy-start(f32[192]{0:T(256)} %param.25) | copy-start | bytes 2308
  118.7 11.5 %copy-start.1 = (f32[2,21,21,192]{3,2,1,0:T(8,128)S(1)}, f32[2,21,21,192]{3,2,1,0:T(8,128)}, u32[]{:S(2)}) copy-start(f32[2,21,21,192]{3,2,1,0:T(8,128)} %copy-done) | copy-start | bytes 2032132
  120.3 12.9 %collective-permute-start.6 = (bf16[192,896]{1,0:T(8,128)(2,1)}, bf16[192,896]{1,0:T(8,128)(2,1)S(1)}, u32[]{:S(2)}, u32[]{:S(2)}) collective-permute-start(bf16[192,896]{1,0:T(8,128)(2,1)} %get-tuple-element.17), channel_id=1, source_target_pairs={{0,4},{2,6},{4,0},{6,2},{1,5},{3,7},{5,1},{7,3},{8,12},{10,14},{12... | collective-permute-start | bytes 1032200 | tf_op jit(solution)/shard_map/ppermute | solution.py:17
  123.4 17.9 %collective-permute-start.7 = (bf16[192,896]{1,0:T(8,128)(2,1)}, bf16[192,896]{1,0:T(8,128)(2,1)S(1)}, u32[]{:S(2)}, u32[]{:S(2)}) collective-permute-start(bf16[192,896]{1,0:T(8,128)(2,1)} %get-tuple-element.18), channel_id=1, source_target_pairs={{0,2},{2,4},{4,6},{6,0},{1,3},{3,5},{5,7},{7,1},{8,10},{10,12},{12... | collective-permute-start | bytes 1032200 | tf_op jit(solution)/shard_map/ppermute | solution.py:17
  125.6 15.7 %collective-permute-start.8 = (bf16[192,896]{1,0:T(8,128)(2,1)}, bf16[192,896]{1,0:T(8,128)(2,1)}, u32[]{:S(2)}, u32[]{:S(2)}) collective-permute-start(bf16[192,896]{1,0:T(8,128)(2,1)} %get-tuple-element.19), channel_id=1, source_target_pairs={{0,6},{2,0},{4,2},{6,4},{1,7},{3,1},{5,3},{7,5},{8,14},{10,8},{12,... | collective-permute-start | bytes 1032200 | tf_op jit(solution)/shard_map/ppermute | solution.py:17

commit v8 on v7

--- a/solution.py
+++ b/solution.py
@@ -46,10 +46,12 @@
 
 
 def conv_kernel(
-    seq, first_crop, crop_counts, slots, before, after, table, block_in, conv, padded, shifted, taps
+    seq, first_crop, crop_counts, slots, before, after, table,
+    block_in, conv, padded, shifted, taps, rows, flat,
 ):
     f32 = jnp.float32
-    side = block_in.shape[1]
+    side = rows.shape[1]
+    cells = side * side
     shards = first_crop.shape[0]
     margin = KSIDE // 2
     here = seq[0]
@@ -80,7 +82,9 @@
         received = (before if n == 0 else after)[...].astype(f32)
         held = (first <= target) & (target < limit)
         crop = jnp.where(held, mine, received) + tile
-        block_in[n] = crop
+        for i in range(side):
+            at = n * cells + i * side
+            block_in[at : at + side, :] = crop[i]
         padded[:, margin : margin + side, :] = crop
         for b in range(KSIDE):
             shifted[b, n, margin : margin + side] = padded[:, b : b + shifted.shape[3], :]
@@ -97,21 +101,30 @@
                     if 0 <= r - o < KSIDE:
                         sums[o] = sums[o] + row * taps[(r - o) * KSIDE + b][None]
         for o in range(3):
-            conv[n, top + o] = sums[o].reshape(columns, width) + bias
+            rows[n, top + o] = sums[o].reshape(columns, width) + bias
         return 0
 
     lax.fori_loop(0, PER_DEV * groups, three_rows, 0)
+    last = PER_DEV * cells // 8 * 8
+    flat[last:, :] = jnp.zeros((flat.shape[0] - last, width), f32)
+    for n in range(PER_DEV):
+        for i in range(side):
+            at = n * cells + i * side
+            flat[at : at + side, :] = rows[n, i][:side]
+    conv[...] = flat[...].T
 
 
 def depthwise(seq_index, first_crop, crop_counts, slots, before, after, table):
     f32 = jnp.float32
     side, width = slots.shape[1], slots.shape[3]
     columns = 24
+    cells = PER_DEV * side * side
+    padded_cells = cells + -cells % 128
     return pl.pallas_call(
         conv_kernel,
         out_shape=(
-            jax.ShapeDtypeStruct((PER_DEV, side, side, width), f32),
-            jax.ShapeDtypeStruct((PER_DEV, side, columns, width), f32),
+            jax.ShapeDtypeStruct((cells, width), f32),
+            jax.ShapeDtypeStruct((width, padded_cells), f32),
         ),
         in_specs=[whole(pltpu.SMEM)] * 3 + [whole()] * 4,
         out_specs=(whole(), whole()),
@@ -119,8 +132,10 @@
             pltpu.VMEM((side, columns + 8, width), f32),
             pltpu.VMEM((KSIDE, PER_DEV, side + 6, columns, width), f32),
             pltpu.VMEM((KSIDE * KSIDE, 8, width), f32),
+            pltpu.VMEM((PER_DEV, side, columns, width), f32),
+            pltpu.VMEM((padded_cells, width), f32),
         ],
-        compiler_params=vmem(16),
+        compiler_params=vmem(18),
         name="conv",
     )(seq_index.astype(jnp.int32).reshape(1), first_crop, crop_counts, slots, before, after, table)
 
@@ -133,8 +148,10 @@
     return pl.BlockSpec(memory_space=space)
 
 
-def norm_kernel(conv, gain, bias, normed):
+def norm_kernel(conv, gain_ref, bias_ref, normed):
     channels, cells = conv.shape
+    gain = gain_ref[...].astype(jnp.float32)[None, :]
+    bias = bias_ref[...].astype(jnp.float32)[None, :]
     step = 128
     for c in range(0, cells, step):
         block = conv[:, c : c + step]
@@ -142,7 +159,7 @@
         block = block - mean
         var = jnp.sum(block * block, axis=0, keepdims=True) * (1.0 / channels)
         block = block * lax.rsqrt(var + 1e-6)
-        normed[c : c + step, :] = (block.T * gain[...] + bias[...]).astype(normed.dtype)
+        normed[c : c + step, :] = (block.T * gain + bias).astype(normed.dtype)
 
 
 def layer_norm(conv, gain, bias):
@@ -153,7 +170,7 @@
         out_specs=whole(),
         compiler_params=vmem(20),
         name="norm",
-    )(conv, gain.astype(jnp.float32)[None, :], bias.astype(jnp.float32)[None, :])
+    )(conv, gain, bias)
 
 
 def copy_down_rows(blocks, buffer, sems, y, core):
@@ -179,9 +196,10 @@
         out[x] = product[x * width : (x + 1) * width].astype(out.dtype)
 
 
-def first_kernel(place, normed, b_up, *refs):
+def first_kernel(y_ref, core_ref, normed, b_up, *refs):
     blocks, (hidden, out, up, down, up_sem, down_sem) = refs[:NY], refs[NY:]
-    y, core = place[0], place[2]
+    y, core = y_ref[0], core_ref[0]
+    bias = b_up[...].astype(jnp.float32)[None, :]
     ups = []
     for d, block in enumerate(blocks):
         rows = block.shape[1]
@@ -194,11 +212,11 @@
         copy.start()
     for copy in ups:
         copy.wait()
-    cells = normed.shape[0]
+    cells, units = normed.shape[0], b_up.shape[0]
     rows = cells // 4
     for r in range(0, cells, rows):
         pre = jnp.dot(normed[r : r + rows], up[...], preferred_element_type=jnp.float32)
-        pre = pre + b_up[...]
+        pre = pre + bias
         act = 0.5 * pre * (1.0 + lax.erf(pre * 0.5**0.5))
         hidden[r : r + rows] = act.astype(hidden.dtype)
     for copy in downs:
@@ -206,9 +224,9 @@
     down_product(down, hidden[...], out)
 
 
-def second_kernel(place, hidden, *refs):
+def second_kernel(y, core, hidden, *refs):
     blocks, (out, down, down_sem) = refs[:NY], refs[NY:]
-    downs = copy_down_rows(blocks, down, down_sem, place[0], place[2])
+    downs = copy_down_rows(blocks, down, down_sem, y[0], core[0])
     for copy in downs:
         copy.start()
     for copy in downs:
@@ -216,9 +234,9 @@
     down_product(down, hidden[...], out)
 
 
-def pair_kernel(place, mine, other, own, *sent):
+def pair_kernel(x, mine, other, own, *sent):
     def pair(distance):
-        i = lax.rem(place[1] + distance, NX)
+        i = lax.rem(x[0] + distance, NX)
         return mine[i].astype(jnp.float32) + other[i].astype(jnp.float32)
 
     own[...] = pair(0)
@@ -238,13 +256,13 @@
 def mlp_sum(normed, blocks, b_up, width):
     bf16, f32 = jnp.bfloat16, jnp.float32
     cells, units = normed.shape[0], b_up.shape[0]
-    place = jnp.stack([lax.axis_index(a).astype(jnp.int32) for a in ("y", "x", "core")])
+    y, x, core = (lax.axis_index(a).astype(jnp.int32).reshape(1) for a in ("y", "x", "core"))
     half_out = jax.ShapeDtypeStruct((NX, width, cells), bf16)
     down = pltpu.VMEM((NX * width, units), bf16)
     hidden, other = pl.pallas_call(
         first_kernel,
         out_shape=(jax.ShapeDtypeStruct((cells, units), bf16), half_out),
-        in_specs=[whole(pltpu.SMEM), whole(), whole()] + [whole(pl.ANY)] * len(blocks),
+        in_specs=[whole(pltpu.SMEM)] * 2 + [whole()] * 2 + [whole(pl.ANY)] * len(blocks),
         out_specs=(whole(), whole()),
         scratch_shapes=[
             pltpu.VMEM((normed.shape[1], units), bf16),
@@ -254,17 +272,17 @@
         ],
         compiler_params=vmem(20),
         name="up_and_down",
-    )(place, normed, b_up.astype(f32)[None, :], *blocks)
+    )(y, core, normed, b_up, *blocks)
     other = shift(other, "core", 1, NCORE)
     mine = pl.pallas_call(
         second_kernel,
         out_shape=half_out,
-        in_specs=[whole(pltpu.SMEM), whole()] + [whole(pl.ANY)] * len(blocks),
+        in_specs=[whole(pltpu.SMEM)] * 2 + [whole()] + [whole(pl.ANY)] * len(blocks),
         out_specs=whole(),
         scratch_shapes=[down, pltpu.SemaphoreType.DMA((NX,))],
         compiler_params=vmem(12),
         name="down_own",
-    )(place, hidden, *blocks)
+    )(y, core, hidden, *blocks)
     block = jax.ShapeDtypeStruct((width, cells), bf16)
     own, *sent = pl.pallas_call(
         pair_kernel,
@@ -273,8 +291,9 @@
         out_specs=(whole(),) * (1 + len(DISTANCES)),
         compiler_params=vmem(12),
         name="pair",
-    )(place, mine, other)
-    return own, *(shift(block, "x", d, NX) for d, block in zip(DISTANCES, sent))
+    )(x, mine, other)
+    received = (shift(block, "x", d, NX) for d, block in zip(DISTANCES, sent))
+    return own, *(pltpu.with_memory_space_constraint(r, pltpu.VMEM) for r in received)
 
 
 def per_device(
@@ -298,9 +317,7 @@
         seq_index, first_crop, crop_counts, slots, before, after, table
     )
     cells = PER_DEV * side * side
-    padding = -cells % 128
-    conv_t = jnp.pad(conv[:, :, :side].reshape(cells, width), ((0, padding), (0, 0))).T
-    conv_t = conv_t.astype(jnp.float16)
+    conv_t = conv.astype(jnp.float16)
     conv_all = lax.all_gather(conv_t, TP, axis=0, tiled=True).astype(f32)
     normed = layer_norm(conv_all, ln_gain, ln_bias)
     sums = mlp_sum(normed, blocks, b_up, width)
@@ -311,7 +328,7 @@
         out_specs=whole(),
         compiler_params=vmem(12),
         name="result",
-    )(*sums, b_down.astype(f32)[:, None], gamma[:, None], block_in.reshape(cells, width))
+    )(*sums, b_down.astype(f32)[:, None], gamma[:, None], block_in)
     return result.reshape(PER_DEV, side, side, width)
 
 

time: 146 us -> 137 us (0.938)
  local copies, waits for them, and re-layouts: 14.6 us -> 7.05 us
  starting transfers between devices: 28 us -> 31.8 us
  Pallas kernels: 22.6 us -> 20.6 us
    reshape x3 -> x0, local copies, waits for them, and re-layouts: 4.19 us -> none  [the longest x2 4.07 us: per_device(): conv[:, :, :side].reshape(cells, width)]
    ppermute x7, starting transfers between devices: 20.6 us -> 24.4 us  [shift(): lax.ppermute(block, axis, [(i, (i + distance) % size) for i in range(size)])]
    broadcast_in_dim x3 -> x0, local copies, waits for them, and re-layouts: 2.65 us -> none  [the longest x1 1.27 us: mlp_sum(): b_up.astype(f32)[None, :]]
    another operation x2 -> x0, other arithmetic: 1.49 us -> none
  transfers between devices with their start and end apart: 9 -> 9, of which waited for: 2 -> 3; matrix products, arithmetic and copies ran while one was open for 10% -> 4% of each run, Pallas kernels for 10% -> 10%
where the time goes in v8:
time: 137 us; the launch traced here: 136 us
  blocking collectives  62.9 us (46%)
  starting transfers between devices  31.8 us (23%)
  Pallas kernels  20.6 us (15%)
  waiting for transfers between devices  9.64 us (7%)
  local copies, waits for them, and re-layouts  7.05 us (5%)
  other arithmetic  2.29 us (2%)
  between operations  1.53 us (1%)
    all_gather x1, blocking collectives, gather_z(): over_z = lax.all_gather(both.astype(jnp.float16), 'z', axis=1, tiled=True)  36 us
    all_gather x1, blocking collectives, per_device(): conv_all = lax.all_gather(conv_t, TP, axis=0, tiled=True).astype(f32)  26.9 us
    ppermute x7, starting transfers between devices, shift(): lax.ppermute(block, axis, [(i, (i + distance) % size) for i in range(size)])  24.4 us
    ppermute x7, waiting for transfers between devices, shift(): lax.ppermute(block, axis, [(i, (i + distance) % size) for i in range(size)])  9.53 us
    pallas_call x1, Pallas kernels, depthwise(): pl.pallas_call(conv_kernel, out_shape=(jax.ShapeDtypeStruct((cells, width...  8.87 us
    ppermute x1, starting transfers between devices, exchange(): lax.ppermute(crop(target - 1), SEQ, [(i + 1, i) for i in range(count - 1)])  5.47 us
    pallas_call x1, Pallas kernels, mlp_sum(): pl.pallas_call(first_kernel, out_shape=(jax.ShapeDtypeStruct((cells, unit...  5.29 us
  transfers between devices with their start and end apart: 9, of which 3 were waited for; matrix products, arithmetic and copies ran while one was open for 4% of the time, Pallas kernels for 10%

profile of v8, /device:TPU:25, one launch (start us, length us, event | category | flops | bytes accessed | tf_op | source)
XLA Modules:
  0.0 135.9 jit_solution(9172812252800183857)
XLA Ops:
  0.0 0.8 multiply_convert_fusion.1
  0.8 36.0 %all-gather.3 = f16[2,384,768]{2,1,0:T(8,128)(2,1)S(1)} all-gather(f16[2,24,768]{2,1,0:T(8,128)(2,1)S(1)} %multiply_convert_fusion.1), channel_id=1, replica_groups=mesh['y'=4,'z'=16,'x'=4,'core'=2] {'z'}, dimensions={1}, use_global_device_ids=true | all-gather | bytes 1253376 | tf_op jit(solution)/shard_map/all_gather | solution.py:22
  37.0 2.4 %collective-permute-start.2 = (bf16[2,384,768]{2,1,0:T(8,128)(2,1)S(1)}, bf16[2,384,768]{2,1,0:T(8,128)(2,1)S(1)}, u32[]{:S(2)}, u32[]{:S(2)}) collective-permute-start(bf16[2,384,768]{2,1,0:T(8,128)(2,1)S(1)} %multiply_convert_fusion.refs_0_), channel_id=1, source_target_pairs={{0,384},{128,0},{256,128},{384,256},{1,385},{129,1},{257,129},{385... | collective-permute-start | bytes 3538952 | tf_op jit(solution)/shard_map/ppermute | solution.py:17
  39.4 2.6 %collective-permute-start.3 = (bf16[2,384,768]{2,1,0:T(8,128)(2,1)S(1)}, bf16[2,384,768]{2,1,0:T(8,128)(2,1)S(1)}, u32[]{:S(2)}, u32[]{:S(2)}) collective-permute-start(bf16[2,384,768]{2,1,0:T(8,128)(2,1)S(1)} %multiply_convert_fusion.refs_0_), channel_id=1, source_target_pairs={{0,256},{128,384},{256,0},{384,128},{1,257},{129,385},{257,1},{385... | collective-permute-start | bytes 3538952 | tf_op jit(solution)/shard_map/ppermute | solution.py:17
  42.0 3.8 %collective-permute-start.4 = (bf16[2,384,768]{2,1,0:T(8,128)(2,1)S(1)}, bf16[2,384,768]{2,1,0:T(8,128)(2,1)}, u32[]{:S(2)}, u32[]{:S(2)}) collective-permute-start(bf16[2,384,768]{2,1,0:T(8,128)(2,1)S(1)} %multiply_convert_fusion.refs_0_), channel_id=1, source_target_pairs={{0,128},{128,256},{256,384},{384,0},{1,129},{129,257},{257,385},{3... | collective-permute-start | bytes 3538952 | tf_op jit(solution)/shard_map/ppermute | solution.py:17
  47.7 1.3 dynamic-slice_bitcast_fusion
  49.0 1.9 %collective-permute-start = (bf16[21,21,192]{2,1,0:T(8,128)(2,1)S(1)}, bf16[21,21,192]{2,1,0:T(8,128)(2,1)S(1)}, u32[]{:S(2)}, u32[]{:S(2)}) collective-permute-start(bf16[21,21,192]{2,1,0:T(8,128)(2,1)S(1)} %get-tuple-element.22), channel_id=1, source_target_pairs={{0,8},{8,16},{16,24},{24,32},{32,40},{40,48},{48,56},{56,64},{64,7... | collective-permute-start | bytes 508040 | tf_op jit(solution)/shard_map/ppermute | solution.py:41
  51.0 5.5 %collective-permute-start.1 = (bf16[21,21,192]{2,1,0:T(8,128)(2,1)S(1)}, bf16[21,21,192]{2,1,0:T(8,128)(2,1)S(1)}, u32[]{:S(2)}, u32[]{:S(2)}) collective-permute-start(bf16[21,21,192]{2,1,0:T(8,128)(2,1)S(1)} %get-tuple-element.21), channel_id=1, source_target_pairs={{8,0},{16,8},{24,16},{32,24},{40,32},{48,40},{56,48},{64,56},{72,6... | collective-permute-start | bytes 508040 | tf_op jit(solution)/shard_map/ppermute | solution.py:44
  57.2 0.9 fusion.1.table
  58.0 1.6 %constant_dynamic-slice_fusion.slots = bf16[3,21,21,192]{3,2,1,0:T(8,128)(2,1)S(1)} fusion(bf16[3,21,21,1536]{3,2,1,0:T(8,128)(2,1)} %param.13, s32[]{:T(128)S(6)} %select_n.12), kind=kLoop, calls=%fused_computation.9 | loop fusion | bytes 1016068 | tf_op jit(solution)/shard_map/dynamic_slice | solution.py:311
  59.8 8.9 %conv.1 = (f32[882,192]{1,0:T(8,128)S(1)}, f32[192,896]{1,0:T(8,128)S(1)}) custom-call(s32[1]{0:T(128)} %bitcast.3.seq, s32[64]{0:T(128)S(1)} %copy-done.5, s32[64]{0:T(128)S(1)} %copy-done.6, bf16[3,21,21,192]{3,2,1,0:T(8,128)(2,1)S(1)} %constant_dynamic-slice_fusion.slots, bf16[21,21,192]{2,1,0:T(8,128)(2,1)S(1)} %collective-permute-done.before, ...), custom_call_target="tpu_custom_call" | custom-call | tf_op jit(solution)/shard_map/conv/pallas_call | solution.py:123
  68.7 0.9 copy-done
  69.6 26.9 %all-gather.2 = f16[1536,896]{1,0:T(8,128)(2,1)S(1)} all-gather(f16[192,896]{1,0:T(8,128)(2,1)S(1)} %convert_element_type.19), channel_id=1, replica_groups=mesh['y'=4,'z'=16,'x'=4,'core'=2] {'x','core'}, dimensions={0}, use_global_device_ids=true | all-gather | bytes 3096576 | tf_op jit(solution)/shard_map/all_gather | solution.py:321
  97.2 2.4 %norm.1.normed = bf16[896,1536]{1,0:T(8,128)(2,1)S(1)} custom-call(f32[1536,896]{1,0:T(8,128)S(1)} %convert_element_type.20.conv, bf16[1536]{0:T(1024)(128)(2,1)S(1)} %copy-done.2, bf16[1536]{0:T(1024)(128)(2,1)S(1)} %copy-done.3), custom_call_target="tpu_custom_call" | custom-call | tf_op jit(solution)/shard_map/norm/pallas_call | solution.py:166
  99.6 5.3 %up_and_down.1 = (bf16[896,768]{1,0:T(8,128)(2,1)S(1)}, bf16[4,192,896]{2,1,0:T(8,128)(2,1)S(1)}) custom-call(s32[1]{0:T(128)} %bitcast.1.y_ref.y, s32[1]{0:T(128)} %bitcast.2.core_ref.core, bf16[896,1536]{1,0:T(8,128)(2,1)S(1)} %norm.1.normed, bf16[768]{0:T(1024)(128)(2,1)S(1)} %copy-done.4, bf16[2,384,768]{2,1,0:T(8,128)(2,1)S(1)} %multiply_convert_fusion.refs_0_, ...), custom_call_target="tpu_custom_call" | custom-call | tf_op jit(solution)/shard_map/up_and_down/pallas_call | solution.py:262
  104.9 4.5 %collective-permute-start.5 = (bf16[4,192,896]{2,1,0:T(8,128)(2,1)S(1)}, bf16[4,192,896]{2,1,0:T(8,128)(2,1)S(1)}, u32[]{:S(2)}, u32[]{:S(2)}) collective-permute-start(bf16[4,192,896]{2,1,0:T(8,128)(2,1)S(1)} %get-tuple-element.15), channel_id=1, source_target_pairs={{0,1},{1,0},{2,3},{3,2},{4,5},{5,4},{6,7},{7,6},{8,9},{9,8},{10,11... | collective-permute-start | bytes 4128776 | tf_op jit(solution)/shard_map/ppermute | solution.py:17
  109.4 2.6 %down_own.1.mine = bf16[4,192,896]{2,1,0:T(8,128)(2,1)S(1)} custom-call(s32[1]{0:T(128)} %bitcast.1.y_ref.y, s32[1]{0:T(128)} %bitcast.2.core_ref.core, bf16[896,768]{1,0:T(8,128)(2,1)S(1)} %get-tuple-element.14.hidden, bf16[2,384,768]{2,1,0:T(8,128)(2,1)S(1)} %multiply_convert_fusion.refs_0_, bf16[2,384,768]{2,1,0:T(8,128)(2,1)S(1)} %collective-permute-done.2.refs_1_, ...), custom_call_target="tpu_custom_call" | custom-call | tf_op jit(solution)/shard_map/down_own/pallas_call | solution.py:277
  112.1 1.1 pair.1
  113.2 4.6 %collective-permute-start.6 = (bf16[192,896]{1,0:T(8,128)(2,1)}, bf16[192,896]{1,0:T(8,128)(2,1)S(1)}, u32[]{:S(2)}, u32[]{:S(2)}) collective-permute-start(bf16[192,896]{1,0:T(8,128)(2,1)} %get-tuple-element.17), channel_id=1, source_target_pairs={{0,4},{2,6},{4,0},{6,2},{1,5},{3,7},{5,1},{7,3},{8,12},{10,14},{12... | collective-permute-start | bytes 1032200 | tf_op jit(solution)/shard_map/ppermute | solution.py:17
  117.8 2.2 %collective-permute-start.7 = (bf16[192,896]{1,0:T(8,128)(2,1)}, bf16[192,896]{1,0:T(8,128)(2,1)S(1)}, u32[]{:S(2)}, u32[]{:S(2)}) collective-permute-start(bf16[192,896]{1,0:T(8,128)(2,1)} %get-tuple-element.18), channel_id=1, source_target_pairs={{0,2},{2,4},{4,6},{6,0},{1,3},{3,5},{5,7},{7,1},{8,10},{10,12},{12... | collective-permute-start | bytes 1032200 | tf_op jit(solution)/shard_map/ppermute | solution.py:17
  120.1 4.3 %collective-permute-start.8 = (bf16[192,896]{1,0:T(8,128)(2,1)S(1)}, bf16[192,896]{1,0:T(8,128)(2,1)S(1)}, u32[]{:S(2)}, u32[]{:S(2)}) collective-permute-start(bf16[192,896]{1,0:T(8,128)(2,1)S(1)} %get-tuple-element.19), channel_id=1, source_target_pairs={{0,6},{2,0},{4,2},{6,4},{1,7},{3,1},{5,3},{7,5},{8,14},{10,8},{12,... | collective-permute-start | bytes 1032200 | tf_op jit(solution)/shard_map/ppermute | solution.py:17
  124.6 1.6 %collective-permute-done.6.first = bf16[192,896]{1,0:T(8,128)(2,1)S(1)} collective-permute-done((bf16[192,896]{1,0:T(8,128)(2,1)}, bf16[192,896]{1,0:T(8,128)(2,1)S(1)}, u32[]{:S(2)}, u32[]{:S(2)}) %collective-permute-start.6) | collective-permute-done | bytes 344096 | tf_op jit(solution)/shard_map/ppermute | solution.py:17
  126.2 7.9 %collective-permute-done.7.second = bf16[192,896]{1,0:T(8,128)(2,1)S(1)} collective-permute-done((bf16[192,896]{1,0:T(8,128)(2,1)}, bf16[192,896]{1,0:T(8,128)(2,1)S(1)}, u32[]{:S(2)}, u32[]{:S(2)}) %collective-permute-start.7) | collective-permute-done | bytes 344096 | tf_op jit(solution)/shard_map/ppermute | solution.py:17
  134.8 1.1 copy.17
  (36 shorter events, 3.3 us)
Async XLA Ops:
  36.8 9.0 %copy-start.5 = (s32[64]{0:T(128)S(1)}, s32[64]{0:T(128)}, u32[]{:S(2)}) copy-start(s32[64]{0:T(128)} %first_crop.1) | copy-start | bytes 772
  36.8 20.3 %copy-start.7 = (bf16[3,1536]{1,0:T(4,128)(2,1)S(1)}, bf16[3,1536]{1,0:T(4,128)(2,1)}, u32[]{:S(2)}) copy-start(bf16[3,1536]{1,0:T(4,128)(2,1)} %param.16) | copy-start | bytes 27652
  37.0 62.6 %collective-permute-start.2 = (bf16[2,384,768]{2,1,0:T(8,128)(2,1)S(1)}, bf16[2,384,768]{2,1,0:T(8,128)(2,1)S(1)}, u32[]{:S(2)}, u32[]{:S(2)}) collective-permute-start(bf16[2,384,768]{2,1,0:T(8,128)(2,1)S(1)} %multiply_convert_fusion.refs_0_), channel_id=1, source_target_pairs={{0,384},{128,0},{256,128},{384,256},{1,385},{129,1},{257,129},{385... | collective-permute-start | bytes 3538952 | tf_op jit(solution)/shard_map/ppermute | solution.py:17
  39.4 60.2 %collective-permute-start.3 = (bf16[2,384,768]{2,1,0:T(8,128)(2,1)S(1)}, bf16[2,384,768]{2,1,0:T(8,128)(2,1)S(1)}, u32[]{:S(2)}, u32[]{:S(2)}) collective-permute-start(bf16[2,384,768]{2,1,0:T(8,128)(2,1)S(1)} %multiply_convert_fusion.refs_0_), channel_id=1, source_target_pairs={{0,256},{128,384},{256,0},{384,128},{1,257},{129,385},{257,1},{385... | collective-permute-start | bytes 3538952 | tf_op jit(solution)/shard_map/ppermute | solution.py:17
  42.0 57.6 %collective-permute-start.4 = (bf16[2,384,768]{2,1,0:T(8,128)(2,1)S(1)}, bf16[2,384,768]{2,1,0:T(8,128)(2,1)}, u32[]{:S(2)}, u32[]{:S(2)}) collective-permute-start(bf16[2,384,768]{2,1,0:T(8,128)(2,1)S(1)} %multiply_convert_fusion.refs_0_), channel_id=1, source_target_pairs={{0,128},{128,256},{256,384},{384,0},{1,129},{129,257},{257,385},{3... | collective-permute-start | bytes 3538952 | tf_op jit(solution)/shard_map/ppermute | solution.py:17
  47.7 12.1 %copy-start.6 = (s32[64]{0:T(128)S(1)}, s32[64]{0:T(128)}, u32[]{:S(2)}) copy-start(s32[64]{0:T(128)} %crop_counts.1) | copy-start | bytes 772
  49.0 10.6 %collective-permute-start = (bf16[21,21,192]{2,1,0:T(8,128)(2,1)S(1)}, bf16[21,21,192]{2,1,0:T(8,128)(2,1)S(1)}, u32[]{:S(2)}, u32[]{:S(2)}) collective-permute-start(bf16[21,21,192]{2,1,0:T(8,128)(2,1)S(1)} %get-tuple-element.22), channel_id=1, source_target_pairs={{0,8},{8,16},{16,24},{24,32},{32,40},{40,48},{48,56},{56,64},{64,7... | collective-permute-start | bytes 508040 | tf_op jit(solution)/shard_map/ppermute | solution.py:41
  51.0 8.8 %collective-permute-start.1 = (bf16[21,21,192]{2,1,0:T(8,128)(2,1)S(1)}, bf16[21,21,192]{2,1,0:T(8,128)(2,1)S(1)}, u32[]{:S(2)}, u32[]{:S(2)}) collective-permute-start(bf16[21,21,192]{2,1,0:T(8,128)(2,1)S(1)} %get-tuple-element.21), channel_id=1, source_target_pairs={{8,0},{16,8},{24,16},{32,24},{40,32},{48,40},{56,48},{64,56},{72,6... | collective-permute-start | bytes 508040 | tf_op jit(solution)/shard_map/ppermute | solution.py:44
  68.6 0.9 copy-start
  96.5 0.7 copy-start.2
  96.5 0.7 copy-start.3
  97.2 2.4 %copy-start.4 = (bf16[768]{0:T(1024)(128)(2,1)S(1)}, bf16[768]{0:T(1024)(128)(2,1)}, u32[]{:S(2)}) copy-start(bf16[768]{0:T(1024)(128)(2,1)} %b_up.1) | copy-start | bytes 4612
  104.9 7.1 %collective-permute-start.5 = (bf16[4,192,896]{2,1,0:T(8,128)(2,1)S(1)}, bf16[4,192,896]{2,1,0:T(8,128)(2,1)S(1)}, u32[]{:S(2)}, u32[]{:S(2)}) collective-permute-start(bf16[4,192,896]{2,1,0:T(8,128)(2,1)S(1)} %get-tuple-element.15), channel_id=1, source_target_pairs={{0,1},{1,0},{2,3},{3,2},{4,5},{5,4},{6,7},{7,6},{8,9},{9,8},{10,11... | collective-permute-start | bytes 4128776 | tf_op jit(solution)/shard_map/ppermute | solution.py:17
  112.1 12.3 %copy-start.9 = (bf16[192]{0:T(256)(128)(2,1)S(1)}, bf16[192]{0:T(256)(128)(2,1)}, u32[]{:S(2)}) copy-start(bf16[192]{0:T(256)(128)(2,1)} %param.24) | copy-start | bytes 1156
  112.1 12.4 %copy-start.8 = (f32[192]{0:T(256)S(1)}, f32[192]{0:T(256)}, u32[]{:S(2)}) copy-start(f32[192]{0:T(256)} %param.25) | copy-start | bytes 2308
  112.1 22.0 %copy-start.1 = (f32[882,192]{1,0:T(8,128)S(1)}, f32[882,192]{1,0:T(8,128)}, u32[]{:S(2)}) copy-start(f32[882,192]{1,0:T(8,128)} %copy-done) | copy-start | bytes 2032132
  113.2 13.0 %collective-permute-start.6 = (bf16[192,896]{1,0:T(8,128)(2,1)}, bf16[192,896]{1,0:T(8,128)(2,1)S(1)}, u32[]{:S(2)}, u32[]{:S(2)}) collective-permute-start(bf16[192,896]{1,0:T(8,128)(2,1)} %get-tuple-element.17), channel_id=1, source_target_pairs={{0,4},{2,6},{4,0},{6,2},{1,5},{3,7},{5,1},{7,3},{8,12},{10,14},{12... | collective-permute-start | bytes 1032200 | tf_op jit(solution)/shard_map/ppermute | solution.py:17
  117.8 16.3 %collective-permute-start.7 = (bf16[192,896]{1,0:T(8,128)(2,1)}, bf16[192,896]{1,0:T(8,128)(2,1)S(1)}, u32[]{:S(2)}, u32[]{:S(2)}) collective-permute-start(bf16[192,896]{1,0:T(8,128)(2,1)} %get-tuple-element.18), channel_id=1, source_target_pairs={{0,2},{2,4},{4,6},{6,0},{1,3},{3,5},{5,7},{7,1},{8,10},{10,12},{12... | collective-permute-start | bytes 1032200 | tf_op jit(solution)/shard_map/ppermute | solution.py:17
  120.1 14.1 %collective-permute-start.8 = (bf16[192,896]{1,0:T(8,128)(2,1)S(1)}, bf16[192,896]{1,0:T(8,128)(2,1)S(1)}, u32[]{:S(2)}, u32[]{:S(2)}) collective-permute-start(bf16[192,896]{1,0:T(8,128)(2,1)S(1)} %get-tuple-element.19), channel_id=1, source_target_pairs={{0,6},{2,0},{4,2},{6,4},{1,7},{3,1},{5,3},{7,5},{8,14},{10,8},{12,... | collective-permute-start | bytes 1032200 | tf_op jit(solution)/shard_map/ppermute | solution.py:17

commit v9 on v8

--- a/solution.py
+++ b/solution.py
@@ -6,7 +6,9 @@
 from jax.sharding import Mesh, PartitionSpec as P
 
 NY, NZ, NX, NCORE = 4, 16, 4, 2
-SEQ = ("y", "z")
+PARITIES = 2
+Z = ("z_half", "parity")
+SEQ = ("y",) + Z
 TP = ("x", "core")
 PER_DEV = 2
 KSIDE = 7
@@ -17,14 +19,11 @@
     return lax.ppermute(block, axis, [(i, (i + distance) % size) for i in range(size)])
 
 
-def gather_z(w_up, w_down):
-    both = jnp.stack([w_up, w_down.T]).astype(jnp.float32) * 2.0**18
-    over_z = lax.all_gather(both.astype(jnp.float16), "z", axis=1, tiled=True)
-    return (over_z.astype(jnp.float32) * 2.0**-18).astype(jnp.bfloat16)
-
-
-def gather_y(own):
-    return own, *(shift(own, "y", -d, NY) for d in (1, 2, 3))
+def gather_own(w_up, w_down):
+    both = jnp.stack([w_up, w_down.T])
+    own = lax.all_gather(both, "z_half", axis=1, tiled=True)
+    blocks = [own] + [shift(own, "y", -d, NY) for d in (1, 2, 3)]
+    return jnp.stack([b[0] for b in blocks]), jnp.stack([b[1] for b in blocks])
 
 
 def exchange(slots, seq_index, first_crop):
@@ -150,16 +149,25 @@
 
 def norm_kernel(conv, gain_ref, bias_ref, normed):
     channels, cells = conv.shape
-    gain = gain_ref[...].astype(jnp.float32)[None, :]
-    bias = bias_ref[...].astype(jnp.float32)[None, :]
     step = 128
+    rows = channels // (NY * NZ)
+
+    def columns(ref):
+        line = ref[...].astype(jnp.float32)[None, :]
+        return jnp.broadcast_to(line, (step, channels)).T
+
+    gain, bias = columns(gain_ref), columns(bias_ref)
+    order = [
+        (y * NZ + z) * rows for p in range(PARITIES) for y in range(NY) for z in range(p, NZ, PARITIES)
+    ]
     for c in range(0, cells, step):
         block = conv[:, c : c + step]
         mean = jnp.sum(block, axis=0, keepdims=True) * (1.0 / channels)
         block = block - mean
         var = jnp.sum(block * block, axis=0, keepdims=True) * (1.0 / channels)
-        block = block * lax.rsqrt(var + 1e-6)
-        normed[c : c + step, :] = (block.T * gain + bias).astype(normed.dtype)
+        block = block * lax.rsqrt(var + 1e-6) * gain + bias
+        block = jnp.concatenate([block[r : r + rows] for r in order])
+        normed[c : c + step, :] = block.T.astype(normed.dtype)
 
 
 def layer_norm(conv, gain, bias):
@@ -173,17 +181,22 @@
     )(conv, gain, bias)
 
 
-def copy_down_rows(blocks, buffer, sems, y, core):
+def copy_down_rows(near, far, buffer, sems, y, parity, core):
     width = buffer.shape[0] // NX
+    half = width // PARITIES
+    source = pl.multiple_of(core * half, half)
     copies = []
-    for d, block in enumerate(blocks):
-        source = pl.multiple_of(core * width, width)
-        target = pl.multiple_of(lax.rem(y + d, NY) * width, width)
-        copies.append(
-            pltpu.make_async_copy(
-                block.at[1, pl.ds(source, width), :], buffer.at[pl.ds(target, width), :], sems.at[d]
+    for d in range(NY):
+        start = lax.rem(y + d, NY) * width
+        for blocks, of in ((near, parity), (far, 1 - parity)):
+            target = pl.multiple_of(start + of * half, half)
+            copies.append(
+                pltpu.make_async_copy(
+                    blocks.at[d, pl.ds(source, half), :],
+                    buffer.at[pl.ds(target, half), :],
+                    sems.at[len(copies)],
+                )
             )
-        )
     return copies
 
 
@@ -196,18 +209,26 @@
         out[x] = product[x * width : (x + 1) * width].astype(out.dtype)
 
 
-def first_kernel(y_ref, core_ref, normed, b_up, *refs):
-    blocks, (hidden, out, up, down, up_sem, down_sem) = refs[:NY], refs[NY:]
-    y, core = y_ref[0], core_ref[0]
+def first_kernel(
+    place, normed, b_up, near_up, far_up, near_down, far_down,
+    hidden, out, up, down, up_sem, down_sem,
+):
+    y, parity, core = place[0], place[1], place[2]
     bias = b_up[...].astype(jnp.float32)[None, :]
+    rows = near_up.shape[1]
     ups = []
-    for d, block in enumerate(blocks):
-        rows = block.shape[1]
-        target = pl.multiple_of(lax.rem(y + d, NY) * rows, rows)
-        ups.append(pltpu.make_async_copy(block.at[0], up.at[pl.ds(target, rows), :], up_sem.at[d]))
+    for d in range(NY):
+        start = lax.rem(y + d, NY) * rows
+        for blocks, of in ((near_up, parity), (far_up, 1 - parity)):
+            target = pl.multiple_of(start + of * NY * rows, rows)
+            ups.append(
+                pltpu.make_async_copy(
+                    blocks.at[d], up.at[pl.ds(target, rows), :], up_sem.at[len(ups)]
+                )
+            )
     for copy in ups:
         copy.start()
-    downs = copy_down_rows(blocks, down, down_sem, y, 1 - core)
+    downs = copy_down_rows(near_down, far_down, down, down_sem, y, parity, 1 - core)
     for copy in downs:
         copy.start()
     for copy in ups:
@@ -224,9 +245,8 @@
     down_product(down, hidden[...], out)
 
 
-def second_kernel(y, core, hidden, *refs):
-    blocks, (out, down, down_sem) = refs[:NY], refs[NY:]
-    downs = copy_down_rows(blocks, down, down_sem, y[0], core[0])
+def second_kernel(place, hidden, near_down, far_down, out, down, down_sem):
+    downs = copy_down_rows(near_down, far_down, down, down_sem, place[0], place[1], place[2])
     for copy in downs:
         copy.start()
     for copy in downs:
@@ -248,6 +268,11 @@
     total = own[...]
     for block in (first, second, third):
         total = total + block[...].astype(jnp.float32)
+    half = total.shape[0] // PARITIES
+    step = half // (NZ // PARITIES // NCORE)
+    total = jnp.concatenate(
+        [total[p * half + m : p * half + m + step] for m in range(0, half, step) for p in range(PARITIES)]
+    )
     scaled = gamma[...] * (total + b_down[...])
     rows = residual.shape[0]
     out[...] = (residual[...] + scaled.T[:rows]).astype(out.dtype)
@@ -256,33 +281,36 @@
 def mlp_sum(normed, blocks, b_up, width):
     bf16, f32 = jnp.bfloat16, jnp.float32
     cells, units = normed.shape[0], b_up.shape[0]
-    y, x, core = (lax.axis_index(a).astype(jnp.int32).reshape(1) for a in ("y", "x", "core"))
+    axes = ("y", "parity", "core")
+    place = jnp.stack([lax.axis_index(a).astype(jnp.int32) for a in axes])
+    x = lax.axis_index("x").astype(jnp.int32).reshape(1)
+    near_up, far_up, near_down, far_down = blocks
     half_out = jax.ShapeDtypeStruct((NX, width, cells), bf16)
     down = pltpu.VMEM((NX * width, units), bf16)
     hidden, other = pl.pallas_call(
         first_kernel,
         out_shape=(jax.ShapeDtypeStruct((cells, units), bf16), half_out),
-        in_specs=[whole(pltpu.SMEM)] * 2 + [whole()] * 2 + [whole(pl.ANY)] * len(blocks),
+        in_specs=[whole(pltpu.SMEM)] + [whole()] * 2 + [whole(pl.ANY)] * 4,
         out_specs=(whole(), whole()),
         scratch_shapes=[
             pltpu.VMEM((normed.shape[1], units), bf16),
             down,
-            pltpu.SemaphoreType.DMA((4,)),
-            pltpu.SemaphoreType.DMA((NX,)),
+            pltpu.SemaphoreType.DMA((NY * PARITIES,)),
+            pltpu.SemaphoreType.DMA((NY * PARITIES,)),
         ],
         compiler_params=vmem(20),
         name="up_and_down",
-    )(y, core, normed, b_up, *blocks)
+    )(place, normed, b_up, *blocks)
     other = shift(other, "core", 1, NCORE)
     mine = pl.pallas_call(
         second_kernel,
         out_shape=half_out,
-        in_specs=[whole(pltpu.SMEM)] * 2 + [whole()] + [whole(pl.ANY)] * len(blocks),
+        in_specs=[whole(pltpu.SMEM), whole()] + [whole(pl.ANY)] * 2,
         out_specs=whole(),
-        scratch_shapes=[down, pltpu.SemaphoreType.DMA((NX,))],
+        scratch_shapes=[down, pltpu.SemaphoreType.DMA((NY * PARITIES,))],
         compiler_params=vmem(12),
         name="down_own",
-    )(y, core, hidden, *blocks)
+    )(place, hidden, near_down, far_down)
     block = jax.ShapeDtypeStruct((width, cells), bf16)
     own, *sent = pl.pallas_call(
         pair_kernel,
@@ -305,7 +333,7 @@
     side = crop_features.shape[1]
     seq_index = lax.axis_index(SEQ)
     start = lax.axis_index(TP) * width
-    blocks = gather_y(gather_z(w_up, w_down))
+    near_up, near_down = gather_own(w_up, w_down)
 
     def channels(array):
         return lax.dynamic_slice_in_dim(array, start, width, array.ndim - 1)
@@ -317,7 +345,10 @@
         seq_index, first_crop, crop_counts, slots, before, after, table
     )
     cells = PER_DEV * side * side
-    conv_t = conv.astype(jnp.float16)
+    conv_t, near_up, near_down = lax.optimization_barrier(
+        (conv.astype(jnp.float16), near_up, near_down)
+    )
+    blocks = (near_up, shift(near_up, Z, -1, NZ), near_down, shift(near_down, Z, 1, NZ))
     conv_all = lax.all_gather(conv_t, TP, axis=0, tiled=True).astype(f32)
     normed = layer_norm(conv_all, ln_gain, ln_bias)
     sums = mlp_sum(normed, blocks, b_up, width)
@@ -333,7 +364,7 @@
 
 
 def solution(mesh):
-    fine = Mesh(mesh.devices.reshape(NY, NZ, NX, NCORE), SEQ + TP)
+    fine = Mesh(mesh.devices.reshape(NY, NZ // PARITIES, PARITIES, NX, NCORE), SEQ + TP)
     placed = (
         P(SEQ, None, None, None), P(), P(), P(), P(), P(), P(), P(),
         P(SEQ, TP), P(TP), P(TP, SEQ), P(TP), P(TP),

time: 137 us -> 146 us (1.066)
  the two profiles are of different devices: /device:TPU:25 before, /device:TPU:13 now
where the time goes in v9:
time: 146 us; the launch traced here: 145 us
  blocking collectives  52.1 us (36%)
  starting transfers between devices  42.4 us (29%)
  Pallas kernels  23.2 us (16%)
  waiting for transfers between devices  16.9 us (12%)
  local copies, waits for them, and re-layouts  7.43 us (5%)
  other arithmetic  1.68 us (1%)
  between operations  1.64 us (1%)
    ppermute x9, starting transfers between devices, shift(): lax.ppermute(block, axis, [(i, (i + distance) % size) for i in range(size)])  35 us
    all_gather x1, blocking collectives, gather_own(): own = lax.all_gather(both, 'z_half', axis=1, tiled=True)  32.6 us
    all_gather x1, blocking collectives, per_device(): conv_all = lax.all_gather(conv_t, TP, axis=0, tiled=True).astype(f32)  19.5 us
    ppermute x9, waiting for transfers between devices, shift(): lax.ppermute(block, axis, [(i, (i + distance) % size) for i in range(size)])  15.5 us
    pallas_call x1, Pallas kernels, depthwise(): pl.pallas_call(conv_kernel, out_shape=(jax.ShapeDtypeStruct((cells, width...  8.87 us
    pallas_call x1, Pallas kernels, mlp_sum(): pl.pallas_call(first_kernel, out_shape=(jax.ShapeDtypeStruct((cells, unit...  6.52 us
    ppermute x1, starting transfers between devices, exchange(): lax.ppermute(crop(target - 1), SEQ, [(i + 1, i) for i in range(count - 1)])  4.64 us
    pallas_call x1, Pallas kernels, mlp_sum(): pl.pallas_call(second_kernel, out_shape=half_out, in_specs=[whole(pltpu.S...  3.59 us
  transfers between devices with their start and end apart: 11, of which 4 were waited for; matrix products, arithmetic and copies ran while one was open for 4% of the time, Pallas kernels for 10%

profile of v9, /device:TPU:13, one launch (start us, length us, event | category | flops | bytes accessed | tf_op | source)
XLA Modules:
  0.0 145.4 jit_solution(17794529107278807085)
XLA Ops:
  0.8 32.6 %all_gather.6 = bf16[2,192,768]{2,1,0:T(8,128)(2,1)S(1)} all-gather(bf16[2,24,768]{2,1,0:T(8,128)(2,1)S(1)} %pad_maximum_fusion.2), channel_id=1, replica_groups=mesh['y'=4,'z_half'=8,'parity'=2,'x'=4,'core'=2] {'z_half'}, dimensions={1}, use_global_device_ids=true | all-gather | bytes 663552 | tf_op jit(solution)/shard_map/all_gather | solution.py:24
  33.4 3.2 %collective-permute-start.4 = (bf16[2,192,768]{2,1,0:T(8,128)(2,1)S(1)}, bf16[2,192,768]{2,1,0:T(8,128)(2,1)}, u32[]{:S(2)}, u32[]{:S(2)}) collective-permute-start(bf16[2,192,768]{2,1,0:T(8,128)(2,1)S(1)} %all_gather.6), channel_id=1, source_target_pairs={{0,128},{128,256},{256,384},{384,0},{1,129},{129,257},{257,385},{3... | collective-permute-start | bytes 1769480 | tf_op jit(solution)/shard_map/ppermute | solution.py:19
  36.6 2.6 %collective-permute-start.3 = (bf16[2,192,768]{2,1,0:T(8,128)(2,1)S(1)}, bf16[2,192,768]{2,1,0:T(8,128)(2,1)S(1)}, u32[]{:S(2)}, u32[]{:S(2)}) collective-permute-start(bf16[2,192,768]{2,1,0:T(8,128)(2,1)S(1)} %all_gather.6), channel_id=1, source_target_pairs={{0,256},{128,384},{256,0},{384,128},{1,257},{129,385},{257,1},{385... | collective-permute-start | bytes 1769480 | tf_op jit(solution)/shard_map/ppermute | solution.py:19
  39.3 4.0 %collective-permute-start.2 = (bf16[2,192,768]{2,1,0:T(8,128)(2,1)S(1)}, bf16[2,192,768]{2,1,0:T(8,128)(2,1)S(1)}, u32[]{:S(2)}, u32[]{:S(2)}) collective-permute-start(bf16[2,192,768]{2,1,0:T(8,128)(2,1)S(1)} %all_gather.6), channel_id=1, source_target_pairs={{0,384},{128,0},{256,128},{384,256},{1,385},{129,1},{257,129},{385... | collective-permute-start | bytes 1769480 | tf_op jit(solution)/shard_map/ppermute | solution.py:19
  43.3 1.3 dynamic_slice.19
  45.8 1.3 dynamic-slice_bitcast_fusion
  47.2 2.8 %collective-permute-start = (bf16[21,21,192]{2,1,0:T(8,128)(2,1)S(1)}, bf16[21,21,192]{2,1,0:T(8,128)(2,1)S(1)}, u32[]{:S(2)}, u32[]{:S(2)}) collective-permute-start(bf16[21,21,192]{2,1,0:T(8,128)(2,1)S(1)} %get-tuple-element.28), channel_id=1, source_target_pairs={{0,8},{8,16},{16,24},{24,32},{32,40},{40,48},{48,56},{56,64},{64,7... | collective-permute-start | bytes 508040 | tf_op jit(solution)/shard_map/ppermute | solution.py:40
  49.9 4.6 %collective-permute-start.1 = (bf16[21,21,192]{2,1,0:T(8,128)(2,1)S(1)}, bf16[21,21,192]{2,1,0:T(8,128)(2,1)S(1)}, u32[]{:S(2)}, u32[]{:S(2)}) collective-permute-start(bf16[21,21,192]{2,1,0:T(8,128)(2,1)S(1)} %get-tuple-element.27), channel_id=1, source_target_pairs={{8,0},{16,8},{24,16},{32,24},{40,32},{48,40},{56,48},{64,56},{72,6... | collective-permute-start | bytes 508040 | tf_op jit(solution)/shard_map/ppermute | solution.py:43
  54.7 1.6 %constant_dynamic-slice_fusion.slots = bf16[3,21,21,192]{3,2,1,0:T(8,128)(2,1)S(1)} fusion(bf16[3,21,21,1536]{3,2,1,0:T(8,128)(2,1)} %param.13, s32[]{:T(128)S(6)} %select_n.12), kind=kLoop, calls=%fused_computation.10 | loop fusion | bytes 1016068 | tf_op jit(solution)/shard_map/dynamic_slice | solution.py:339
  56.5 1.3 collective-permute-done.1.after
  57.9 8.9 %conv.1 = (f32[882,192]{1,0:T(8,128)S(1)}, f32[192,896]{1,0:T(8,128)S(1)}) custom-call(s32[1]{0:T(128)} %bitcast.4.seq, s32[64]{0:T(128)S(1)} %copy-done.3, s32[64]{0:T(128)S(1)} %copy-done.4, bf16[3,21,21,192]{3,2,1,0:T(8,128)(2,1)S(1)} %constant_dynamic-slice_fusion.slots, bf16[21,21,192]{2,1,0:T(8,128)(2,1)S(1)} %collective-permute-done.before, ...), custom_call_target="tpu_custom_call" | custom-call | tf_op jit(solution)/shard_map/conv/pallas_call | solution.py:122
  68.3 9.6 %collective-permute-start.5 = (bf16[4,192,768]{2,1,0:T(8,128)(2,1)S(1)}, bf16[4,192,768]{2,1,0:T(8,128)(2,1)S(1)}, u32[]{:S(2)}, u32[]{:S(2)}) collective-permute-start(bf16[4,192,768]{2,1,0:T(8,128)(2,1)S(1)} %get-tuple-element.18.near_up), channel_id=1, source_target_pairs={{0,120},{8,0},{16,8},{24,16},{32,24},{40,32},{48,40},{56,48},{64,5... | collective-permute-start | bytes 3538952 | tf_op jit(solution)/shard_map/ppermute | solution.py:19
  78.0 1.9 %collective-permute-start.6 = (bf16[4,192,768]{2,1,0:T(8,128)(2,1)S(1)}, bf16[4,192,768]{2,1,0:T(8,128)(2,1)S(1)}, u32[]{:S(2)}, u32[]{:S(2)}) collective-permute-start(bf16[4,192,768]{2,1,0:T(8,128)(2,1)S(1)} %get-tuple-element.19.near_down), channel_id=1, source_target_pairs={{0,8},{8,16},{16,24},{24,32},{32,40},{40,48},{48,56},{56,64},{64,7... | collective-permute-start | bytes 3538952 | tf_op jit(solution)/shard_map/ppermute | solution.py:19
  79.9 19.5 %all-gather.1 = f16[1536,896]{1,0:T(8,128)(2,1)S(1)} all-gather(f16[192,896]{1,0:T(8,128)(2,1)S(1)} %convert_element_type.7), channel_id=1, replica_groups=mesh['y'=4,'z_half'=8,'parity'=2,'x'=4,'core'=2] {'x','core'}, dimensions={0}, use_global_device_ids=true | all-gather | bytes 3096576 | tf_op jit(solution)/shard_map/all_gather | solution.py:352
  100.1 2.7 %norm.1.normed = bf16[896,1536]{1,0:T(8,128)(2,1)S(1)} custom-call(f32[1536,896]{1,0:T(8,128)S(1)} %convert_element_type.8.conv, bf16[1536]{0:T(1024)(128)(2,1)S(1)} %copy-done, bf16[1536]{0:T(1024)(128)(2,1)S(1)} %copy-done.1), custom_call_target="tpu_custom_call" | custom-call | tf_op jit(solution)/shard_map/norm/pallas_call | solution.py:174
  102.9 2.6 %collective-permute-done.6.far_down = bf16[4,192,768]{2,1,0:T(8,128)(2,1)S(1)} collective-permute-done((bf16[4,192,768]{2,1,0:T(8,128)(2,1)S(1)}, bf16[4,192,768]{2,1,0:T(8,128)(2,1)S(1)}, u32[]{:S(2)}, u32[]{:S(2)}) %collective-permute-start.6) | collective-permute-done | bytes 1179680 | tf_op jit(solution)/shard_map/ppermute | solution.py:19
  105.5 6.5 %up_and_down.1 = (bf16[896,768]{1,0:T(8,128)(2,1)S(1)}, bf16[4,192,896]{2,1,0:T(8,128)(2,1)S(1)}) custom-call(s32[3]{0:T(128)S(1)} %pad_add_fusion.place, bf16[896,1536]{1,0:T(8,128)(2,1)S(1)} %norm.1.normed, bf16[768]{0:T(1024)(128)(2,1)S(1)} %copy-done.2, bf16[4,192,768]{2,1,0:T(8,128)(2,1)S(1)} %get-tuple-element.18.near_up, ...), custom_call_target="tpu_custom_call" | custom-call | tf_op jit(solution)/shard_map/up_and_down/pallas_call | solution.py:290
  112.0 5.9 %collective-permute-start.7 = (bf16[4,192,896]{2,1,0:T(8,128)(2,1)S(1)}, bf16[4,192,896]{2,1,0:T(8,128)(2,1)S(1)}, u32[]{:S(2)}, u32[]{:S(2)}) collective-permute-start(bf16[4,192,896]{2,1,0:T(8,128)(2,1)S(1)} %get-tuple-element.21), channel_id=1, source_target_pairs={{0,1},{1,0},{2,3},{3,2},{4,5},{5,4},{6,7},{7,6},{8,9},{9,8},{10,11... | collective-permute-start | bytes 4128776 | tf_op jit(solution)/shard_map/ppermute | solution.py:19
  117.9 3.6 %down_own.1.mine = bf16[4,192,896]{2,1,0:T(8,128)(2,1)S(1)} custom-call(s32[3]{0:T(128)S(1)} %pad_add_fusion.place, bf16[896,768]{1,0:T(8,128)(2,1)S(1)} %get-tuple-element.20.hidden, bf16[4,192,768]{2,1,0:T(8,128)(2,1)S(1)} %get-tuple-element.19.near_down, bf16[4,192,768]{2,1,0:T(8,128)(2,1)S(1)} %collective-permute-done.6.far_down), custom_call_target="tpu_custom_call" | custom-call | tf_op jit(solution)/shard_map/down_own/pallas_call | solution.py:305
  122.6 2.1 %collective-permute-start.8 = (bf16[192,896]{1,0:T(8,128)(2,1)}, bf16[192,896]{1,0:T(8,128)(2,1)S(1)}, u32[]{:S(2)}, u32[]{:S(2)}) collective-permute-start(bf16[192,896]{1,0:T(8,128)(2,1)} %get-tuple-element.23), channel_id=1, source_target_pairs={{0,4},{2,6},{4,0},{6,2},{1,5},{3,7},{5,1},{7,3},{8,12},{10,14},{12... | collective-permute-start | bytes 1032200 | tf_op jit(solution)/shard_map/ppermute | solution.py:19
  124.7 3.7 %collective-permute-start.9 = (bf16[192,896]{1,0:T(8,128)(2,1)}, bf16[192,896]{1,0:T(8,128)(2,1)S(1)}, u32[]{:S(2)}, u32[]{:S(2)}) collective-permute-start(bf16[192,896]{1,0:T(8,128)(2,1)} %get-tuple-element.24), channel_id=1, source_target_pairs={{0,2},{2,4},{4,6},{6,0},{1,3},{3,5},{5,7},{7,1},{8,10},{10,12},{12... | collective-permute-start | bytes 1032200 | tf_op jit(solution)/shard_map/ppermute | solution.py:19
  128.5 2.0 %collective-permute-start.10 = (bf16[192,896]{1,0:T(8,128)(2,1)S(1)}, bf16[192,896]{1,0:T(8,128)(2,1)S(1)}, u32[]{:S(2)}, u32[]{:S(2)}) collective-permute-start(bf16[192,896]{1,0:T(8,128)(2,1)S(1)} %get-tuple-element.25), channel_id=1, source_target_pairs={{0,6},{2,0},{4,2},{6,4},{1,7},{3,1},{5,3},{7,5},{8,14},{10,8},{12,... | collective-permute-start | bytes 1032200 | tf_op jit(solution)/shard_map/ppermute | solution.py:19
  130.7 5.2 %collective-permute-done.8.first = bf16[192,896]{1,0:T(8,128)(2,1)S(1)} collective-permute-done((bf16[192,896]{1,0:T(8,128)(2,1)}, bf16[192,896]{1,0:T(8,128)(2,1)S(1)}, u32[]{:S(2)}, u32[]{:S(2)}) %collective-permute-start.8) | collective-permute-done | bytes 344096 | tf_op jit(solution)/shard_map/ppermute | solution.py:19
  135.9 7.7 %collective-permute-done.9.second = bf16[192,896]{1,0:T(8,128)(2,1)S(1)} collective-permute-done((bf16[192,896]{1,0:T(8,128)(2,1)}, bf16[192,896]{1,0:T(8,128)(2,1)S(1)}, u32[]{:S(2)}, u32[]{:S(2)}) %collective-permute-start.9) | collective-permute-done | bytes 344096 | tf_op jit(solution)/shard_map/ppermute | solution.py:19
  (45 shorter events, 6.4 us)
Async XLA Ops:
  0.0 54.6 %copy-start.7 = (bf16[1536]{0:T(1024)(128)(2,1)S(1)}, bf16[1536]{0:T(1024)(128)(2,1)}, u32[]{:S(2)}) copy-start(bf16[1536]{0:T(1024)(128)(2,1)} %param.18) | copy-start | bytes 9220
  33.4 33.4 %collective-permute-start.4 = (bf16[2,192,768]{2,1,0:T(8,128)(2,1)S(1)}, bf16[2,192,768]{2,1,0:T(8,128)(2,1)}, u32[]{:S(2)}, u32[]{:S(2)}) collective-permute-start(bf16[2,192,768]{2,1,0:T(8,128)(2,1)S(1)} %all_gather.6), channel_id=1, source_target_pairs={{0,128},{128,256},{256,384},{384,0},{1,129},{129,257},{257,385},{3... | collective-permute-start | bytes 1769480 | tf_op jit(solution)/shard_map/ppermute | solution.py:19
  36.6 31.3 %collective-permute-start.3 = (bf16[2,192,768]{2,1,0:T(8,128)(2,1)S(1)}, bf16[2,192,768]{2,1,0:T(8,128)(2,1)S(1)}, u32[]{:S(2)}, u32[]{:S(2)}) collective-permute-start(bf16[2,192,768]{2,1,0:T(8,128)(2,1)S(1)} %all_gather.6), channel_id=1, source_target_pairs={{0,256},{128,384},{256,0},{384,128},{1,257},{129,385},{257,1},{385... | collective-permute-start | bytes 1769480 | tf_op jit(solution)/shard_map/ppermute | solution.py:19
  39.3 28.7 %collective-permute-start.2 = (bf16[2,192,768]{2,1,0:T(8,128)(2,1)S(1)}, bf16[2,192,768]{2,1,0:T(8,128)(2,1)S(1)}, u32[]{:S(2)}, u32[]{:S(2)}) collective-permute-start(bf16[2,192,768]{2,1,0:T(8,128)(2,1)S(1)} %all_gather.6), channel_id=1, source_target_pairs={{0,384},{128,0},{256,128},{384,256},{1,385},{129,1},{257,129},{385... | collective-permute-start | bytes 1769480 | tf_op jit(solution)/shard_map/ppermute | solution.py:19
  47.2 9.4 %collective-permute-start = (bf16[21,21,192]{2,1,0:T(8,128)(2,1)S(1)}, bf16[21,21,192]{2,1,0:T(8,128)(2,1)S(1)}, u32[]{:S(2)}, u32[]{:S(2)}) collective-permute-start(bf16[21,21,192]{2,1,0:T(8,128)(2,1)S(1)} %get-tuple-element.28), channel_id=1, source_target_pairs={{0,8},{8,16},{16,24},{24,32},{32,40},{40,48},{48,56},{56,64},{64,7... | collective-permute-start | bytes 508040 | tf_op jit(solution)/shard_map/ppermute | solution.py:40
  49.9 7.9 %collective-permute-start.1 = (bf16[21,21,192]{2,1,0:T(8,128)(2,1)S(1)}, bf16[21,21,192]{2,1,0:T(8,128)(2,1)S(1)}, u32[]{:S(2)}, u32[]{:S(2)}) collective-permute-start(bf16[21,21,192]{2,1,0:T(8,128)(2,1)S(1)} %get-tuple-element.27), channel_id=1, source_target_pairs={{8,0},{16,8},{24,16},{32,24},{40,32},{48,40},{56,48},{64,56},{72,6... | collective-permute-start | bytes 508040 | tf_op jit(solution)/shard_map/ppermute | solution.py:43
  54.6 1.7 %copy-start.5 = (bf16[49,1536]{1,0:T(8,128)(2,1)S(1)}, bf16[49,1536]{1,0:T(8,128)(2,1)}, u32[]{:S(2)}) copy-start(bf16[49,1536]{1,0:T(8,128)(2,1)} %param.17) | copy-start | bytes 451588
  54.6 1.7 %copy-start.6 = (bf16[3,1536]{1,0:T(4,128)(2,1)S(1)}, bf16[3,1536]{1,0:T(4,128)(2,1)}, u32[]{:S(2)}) copy-start(bf16[3,1536]{1,0:T(4,128)(2,1)} %param.16) | copy-start | bytes 27652
  54.7 3.2 %copy-start.3 = (s32[64]{0:T(128)S(1)}, s32[64]{0:T(128)}, u32[]{:S(2)}) copy-start(s32[64]{0:T(128)} %first_crop.1) | copy-start | bytes 772
  54.7 3.2 %copy-start.4 = (s32[64]{0:T(128)S(1)}, s32[64]{0:T(128)}, u32[]{:S(2)}) copy-start(s32[64]{0:T(128)} %crop_counts.1) | copy-start | bytes 772
  68.3 34.5 %collective-permute-start.5 = (bf16[4,192,768]{2,1,0:T(8,128)(2,1)S(1)}, bf16[4,192,768]{2,1,0:T(8,128)(2,1)S(1)}, u32[]{:S(2)}, u32[]{:S(2)}) collective-permute-start(bf16[4,192,768]{2,1,0:T(8,128)(2,1)S(1)} %get-tuple-element.18.near_up), channel_id=1, source_target_pairs={{0,120},{8,0},{16,8},{24,16},{32,24},{40,32},{48,40},{56,48},{64,5... | collective-permute-start | bytes 3538952 | tf_op jit(solution)/shard_map/ppermute | solution.py:19
  78.0 27.5 %collective-permute-start.6 = (bf16[4,192,768]{2,1,0:T(8,128)(2,1)S(1)}, bf16[4,192,768]{2,1,0:T(8,128)(2,1)S(1)}, u32[]{:S(2)}, u32[]{:S(2)}) collective-permute-start(bf16[4,192,768]{2,1,0:T(8,128)(2,1)S(1)} %get-tuple-element.19.near_down), channel_id=1, source_target_pairs={{0,8},{8,16},{16,24},{24,32},{32,40},{40,48},{48,56},{56,64},{64,7... | collective-permute-start | bytes 3538952 | tf_op jit(solution)/shard_map/ppermute | solution.py:19
  99.4 0.7 copy-start
  99.4 0.7 copy-start.1
  100.1 5.4 %copy-start.2 = (bf16[768]{0:T(1024)(128)(2,1)S(1)}, bf16[768]{0:T(1024)(128)(2,1)}, u32[]{:S(2)}) copy-start(bf16[768]{0:T(1024)(128)(2,1)} %b_up.1) | copy-start | bytes 4612
  112.0 9.5 %collective-permute-start.7 = (bf16[4,192,896]{2,1,0:T(8,128)(2,1)S(1)}, bf16[4,192,896]{2,1,0:T(8,128)(2,1)S(1)}, u32[]{:S(2)}, u32[]{:S(2)}) collective-permute-start(bf16[4,192,896]{2,1,0:T(8,128)(2,1)S(1)} %get-tuple-element.21), channel_id=1, source_target_pairs={{0,1},{1,0},{2,3},{3,2},{4,5},{5,4},{6,7},{7,6},{8,9},{9,8},{10,11... | collective-permute-start | bytes 4128776 | tf_op jit(solution)/shard_map/ppermute | solution.py:19
  121.5 9.0 %copy-start.9 = (bf16[192]{0:T(256)(128)(2,1)S(1)}, bf16[192]{0:T(256)(128)(2,1)}, u32[]{:S(2)}) copy-start(bf16[192]{0:T(256)(128)(2,1)} %param.24) | copy-start | bytes 1156
  121.5 9.1 %copy-start.8 = (f32[192]{0:T(256)S(1)}, f32[192]{0:T(256)}, u32[]{:S(2)}) copy-start(f32[192]{0:T(256)} %param.25) | copy-start | bytes 2308
  122.6 13.3 %collective-permute-start.8 = (bf16[192,896]{1,0:T(8,128)(2,1)}, bf16[192,896]{1,0:T(8,128)(2,1)S(1)}, u32[]{:S(2)}, u32[]{:S(2)}) collective-permute-start(bf16[192,896]{1,0:T(8,128)(2,1)} %get-tuple-element.23), channel_id=1, source_target_pairs={{0,4},{2,6},{4,0},{6,2},{1,5},{3,7},{5,1},{7,3},{8,12},{10,14},{12... | collective-permute-start | bytes 1032200 | tf_op jit(solution)/shard_map/ppermute | solution.py:19
  124.7 18.9 %collective-permute-start.9 = (bf16[192,896]{1,0:T(8,128)(2,1)}, bf16[192,896]{1,0:T(8,128)(2,1)S(1)}, u32[]{:S(2)}, u32[]{:S(2)}) collective-permute-start(bf16[192,896]{1,0:T(8,128)(2,1)} %get-tuple-element.24), channel_id=1, source_target_pairs={{0,2},{2,4},{4,6},{6,0},{1,3},{3,5},{5,7},{7,1},{8,10},{10,12},{12... | collective-permute-start | bytes 1032200 | tf_op jit(solution)/shard_map/ppermute | solution.py:19
  128.5 15.2 %collective-permute-start.10 = (bf16[192,896]{1,0:T(8,128)(2,1)S(1)}, bf16[192,896]{1,0:T(8,128)(2,1)S(1)}, u32[]{:S(2)}, u32[]{:S(2)}) collective-permute-start(bf16[192,896]{1,0:T(8,128)(2,1)S(1)} %get-tuple-element.25), channel_id=1, source_target_pairs={{0,6},{2,0},{4,2},{6,4},{1,7},{3,1},{5,3},{7,5},{8,14},{10,8},{12,... | collective-permute-start | bytes 1032200 | tf_op jit(solution)/shard_map/ppermute | solution.py:19

commit v10 on v8

--- a/solution.py
+++ b/solution.py
@@ -24,7 +24,8 @@
 
 
 def gather_y(own):
-    return own, *(shift(own, "y", -d, NY) for d in (1, 2, 3))
+    copies = jnp.broadcast_to(own[None], (NY,) + own.shape)
+    return lax.all_to_all(copies, "y", split_axis=0, concat_axis=0, tiled=True)
 
 
 def exchange(slots, seq_index, first_crop):
@@ -173,18 +174,17 @@
     )(conv, gain, bias)
 
 
-def copy_down_rows(blocks, buffer, sems, y, core):
+def copy_down_rows(blocks, buffer, sems, core):
     width = buffer.shape[0] // NX
-    copies = []
-    for d, block in enumerate(blocks):
-        source = pl.multiple_of(core * width, width)
-        target = pl.multiple_of(lax.rem(y + d, NY) * width, width)
-        copies.append(
-            pltpu.make_async_copy(
-                block.at[1, pl.ds(source, width), :], buffer.at[pl.ds(target, width), :], sems.at[d]
-            )
+    source = pl.multiple_of(core * width, width)
+    return [
+        pltpu.make_async_copy(
+            blocks.at[d, 1, pl.ds(source, width), :],
+            buffer.at[pl.ds(d * width, width), :],
+            sems.at[d],
         )
-    return copies
+        for d in range(NY)
+    ]
 
 
 def down_product(buffer, hidden, out):
@@ -196,18 +196,16 @@
         out[x] = product[x * width : (x + 1) * width].astype(out.dtype)
 
 
-def first_kernel(y_ref, core_ref, normed, b_up, *refs):
-    blocks, (hidden, out, up, down, up_sem, down_sem) = refs[:NY], refs[NY:]
-    y, core = y_ref[0], core_ref[0]
+def first_kernel(core, normed, b_up, blocks, hidden, out, up, down, up_sem, down_sem):
     bias = b_up[...].astype(jnp.float32)[None, :]
-    ups = []
-    for d, block in enumerate(blocks):
-        rows = block.shape[1]
-        target = pl.multiple_of(lax.rem(y + d, NY) * rows, rows)
-        ups.append(pltpu.make_async_copy(block.at[0], up.at[pl.ds(target, rows), :], up_sem.at[d]))
+    rows = blocks.shape[2]
+    ups = [
+        pltpu.make_async_copy(blocks.at[d, 0], up.at[pl.ds(d * rows, rows), :], up_sem.at[d])
+        for d in range(NY)
+    ]
     for copy in ups:
         copy.start()
-    downs = copy_down_rows(blocks, down, down_sem, y, 1 - core)
+    downs = copy_down_rows(blocks, down, down_sem, 1 - core[0])
     for copy in downs:
         copy.start()
     for copy in ups:
@@ -224,9 +222,8 @@
     down_product(down, hidden[...], out)
 
 
-def second_kernel(y, core, hidden, *refs):
-    blocks, (out, down, down_sem) = refs[:NY], refs[NY:]
-    downs = copy_down_rows(blocks, down, down_sem, y[0], core[0])
+def second_kernel(core, hidden, blocks, out, down, down_sem):
+    downs = copy_down_rows(blocks, down, down_sem, core[0])
     for copy in downs:
         copy.start()
     for copy in downs:
@@ -256,13 +253,13 @@
 def mlp_sum(normed, blocks, b_up, width):
     bf16, f32 = jnp.bfloat16, jnp.float32
     cells, units = normed.shape[0], b_up.shape[0]
-    y, x, core = (lax.axis_index(a).astype(jnp.int32).reshape(1) for a in ("y", "x", "core"))
+    x, core = (lax.axis_index(a).astype(jnp.int32).reshape(1) for a in TP)
     half_out = jax.ShapeDtypeStruct((NX, width, cells), bf16)
     down = pltpu.VMEM((NX * width, units), bf16)
     hidden, other = pl.pallas_call(
         first_kernel,
         out_shape=(jax.ShapeDtypeStruct((cells, units), bf16), half_out),
-        in_specs=[whole(pltpu.SMEM)] * 2 + [whole()] * 2 + [whole(pl.ANY)] * len(blocks),
+        in_specs=[whole(pltpu.SMEM), whole(), whole(), whole(pl.ANY)],
         out_specs=(whole(), whole()),
         scratch_shapes=[
             pltpu.VMEM((normed.shape[1], units), bf16),
@@ -272,17 +269,17 @@
         ],
         compiler_params=vmem(20),
         name="up_and_down",
-    )(y, core, normed, b_up, *blocks)
+    )(core, normed, b_up, blocks)
     other = shift(other, "core", 1, NCORE)
     mine = pl.pallas_call(
         second_kernel,
         out_shape=half_out,
-        in_specs=[whole(pltpu.SMEM)] * 2 + [whole()] + [whole(pl.ANY)] * len(blocks),
+        in_specs=[whole(pltpu.SMEM), whole(), whole(pl.ANY)],
         out_specs=whole(),
         scratch_shapes=[down, pltpu.SemaphoreType.DMA((NX,))],
         compiler_params=vmem(12),
         name="down_own",
-    )(y, core, hidden, *blocks)
+    )(core, hidden, blocks)
     block = jax.ShapeDtypeStruct((width, cells), bf16)
     own, *sent = pl.pallas_call(
         pair_kernel,

time: 137 us -> 141 us (1.029)
  the two profiles are of different devices: /device:TPU:25 before, /device:TPU:1 now
where the time goes in v10:
time: 141 us
  blocking collectives  63.1 us (45%)
  starting transfers between devices  28.7 us (20%)
  Pallas kernels  21.1 us (15%)
  waiting for transfers between devices  15.6 us (11%)
  local copies, waits for them, and re-layouts  8.81 us (6%)
  between operations  1.59 us (1%)
  other arithmetic  1.53 us (1%)
    all_gather x1, blocking collectives, gather_z(): over_z = lax.all_gather(both.astype(jnp.float16), 'z', axis=1, tiled=True)  36.8 us
    all_gather x1, blocking collectives, per_device(): conv_all = lax.all_gather(conv_t, TP, axis=0, tiled=True).astype(f32)  26.3 us
    ppermute x4, starting transfers between devices, shift(): lax.ppermute(block, axis, [(i, (i + distance) % size) for i in range(size)])  21.1 us
    ppermute x4, waiting for transfers between devices, shift(): lax.ppermute(block, axis, [(i, (i + distance) % size) for i in range(size)])  9.52 us
    pallas_call x1, Pallas kernels, depthwise(): pl.pallas_call(conv_kernel, out_shape=(jax.ShapeDtypeStruct((cells, width...  8.87 us
    pallas_call x1, Pallas kernels, mlp_sum(): pl.pallas_call(first_kernel, out_shape=(jax.ShapeDtypeStruct((cells, unit...  5.71 us
    all_to_all x1, starting transfers between devices, gather_y(): return lax.all_to_all(copies, 'y', split_axis=0, concat_axis=0, tiled=True)  5.1 us
    ppermute x1, waiting for transfers between devices, exchange(): lax.ppermute(crop(target - 1), SEQ, [(i + 1, i) for i in range(count - 1)])  4.23 us
  transfers between devices with their start and end apart: 7, of which 5 were waited for; matrix products, arithmetic and copies ran while one was open for 3% of the time, Pallas kernels for 10%

profile of v10, /device:TPU:1, one launch (start us, length us, event | category | flops | bytes accessed | tf_op | source)
XLA Modules:
  0.0 140.6 jit_solution(15585546659060965979)
XLA Ops:
  0.0 0.8 multiply_convert_fusion.1
  0.8 36.8 %all-gather.3 = f16[2,384,768]{2,1,0:T(8,128)(2,1)S(1)} all-gather(f16[2,24,768]{2,1,0:T(8,128)(2,1)S(1)} %multiply_convert_fusion.1), channel_id=1, replica_groups=mesh['y'=4,'z'=16,'x'=4,'core'=2] {'z'}, dimensions={1}, use_global_device_ids=true | all-gather | bytes 1253376 | tf_op jit(solution)/shard_map/all_gather | solution.py:22
  37.9 2.5 %broadcast_in_dim.18 = bf16[4,2,384,768]{3,2,1,0:T(8,128)(2,1)} broadcast(bf16[2,384,768]{2,1,0:T(8,128)(2,1)S(1)} %multiply_convert_fusion), dimensions={1,2,3} | broadcast | bytes 5898240 | tf_op jit(solution)/shard_map/broadcast_in_dim | solution.py:27
  40.4 5.1 %all-to-all-start = ((bf16[4,2,384,768]{3,2,1,0:T(8,128)(2,1)}), bf16[4,2,384,768]{3,2,1,0:T(8,128)(2,1)}, u32[]{:S(2)}, u32[]{:S(2)}) async-start(bf16[4,2,384,768]{3,2,1,0:T(8,128)(2,1)} %broadcast_in_dim.18), calls=%async_computation | async-start | bytes 9437184 | tf_op jit(solution)/shard_map/all_to_all | solution.py:28
  47.4 1.3 dynamic-slice_bitcast_fusion
  48.8 1.3 collective-permute-start
  50.1 1.3 collective-permute-start.1
  51.5 1.6 %constant_dynamic-slice_fusion.slots = bf16[3,21,21,192]{3,2,1,0:T(8,128)(2,1)S(1)} fusion(bf16[3,21,21,1536]{3,2,1,0:T(8,128)(2,1)} %param.13, s32[]{:T(128)S(6)} %select_n.12), kind=kLoop, calls=%fused_computation.9 | loop fusion | bytes 1016068 | tf_op jit(solution)/shard_map/dynamic_slice | solution.py:308
  53.3 4.2 %collective-permute-done.1.after = bf16[21,21,192]{2,1,0:T(8,128)(2,1)S(1)} collective-permute-done((bf16[21,21,192]{2,1,0:T(8,128)(2,1)S(1)}, bf16[21,21,192]{2,1,0:T(8,128)(2,1)S(1)}, u32[]{:S(2)}, u32[]{:S(2)}) %collective-permute-start.1) | collective-permute-done | bytes 169376 | tf_op jit(solution)/shard_map/ppermute | solution.py:45
  57.6 8.9 %conv.1 = (f32[882,192]{1,0:T(8,128)S(1)}, f32[192,896]{1,0:T(8,128)S(1)}) custom-call(s32[1]{0:T(128)} %bitcast.2.seq, s32[64]{0:T(128)S(1)} %copy-done.5, s32[64]{0:T(128)S(1)} %copy-done.6, bf16[3,21,21,192]{3,2,1,0:T(8,128)(2,1)S(1)} %constant_dynamic-slice_fusion.slots, bf16[21,21,192]{2,1,0:T(8,128)(2,1)S(1)} %collective-permute-done.before, ...), custom_call_target="tpu_custom_call" | custom-call | tf_op jit(solution)/shard_map/conv/pallas_call | solution.py:124
  66.5 0.9 copy-done
  67.3 26.3 %all-gather.2 = f16[1536,896]{1,0:T(8,128)(2,1)S(1)} all-gather(f16[192,896]{1,0:T(8,128)(2,1)S(1)} %convert_element_type.19), channel_id=1, replica_groups=mesh['y'=4,'z'=16,'x'=4,'core'=2] {'x','core'}, dimensions={0}, use_global_device_ids=true | all-gather | bytes 3096576 | tf_op jit(solution)/shard_map/all_gather | solution.py:318
  94.4 2.4 %norm.1.normed = bf16[896,1536]{1,0:T(8,128)(2,1)S(1)} custom-call(f32[1536,896]{1,0:T(8,128)S(1)} %convert_element_type.20.conv, bf16[1536]{0:T(1024)(128)(2,1)S(1)} %copy-done.2, bf16[1536]{0:T(1024)(128)(2,1)S(1)} %copy-done.3), custom_call_target="tpu_custom_call" | custom-call | tf_op jit(solution)/shard_map/norm/pallas_call | solution.py:167
  96.7 1.7 %all-to-all-done.blocks = bf16[4,2,384,768]{3,2,1,0:T(8,128)(2,1)} async-done(((bf16[4,2,384,768]{3,2,1,0:T(8,128)(2,1)}), bf16[4,2,384,768]{3,2,1,0:T(8,128)(2,1)}, u32[]{:S(2)}, u32[]{:S(2)}) %all-to-all-start) | async-done | bytes 4718624 | tf_op jit(solution)/shard_map/all_to_all | solution.py:28
  98.4 5.7 %up_and_down.1 = (bf16[896,768]{1,0:T(8,128)(2,1)S(1)}, bf16[4,192,896]{2,1,0:T(8,128)(2,1)S(1)}) custom-call(s32[1]{0:T(128)} %bitcast.1.core, bf16[896,1536]{1,0:T(8,128)(2,1)S(1)} %norm.1.normed, bf16[768]{0:T(1024)(128)(2,1)S(1)} %copy-done.4, bf16[4,2,384,768]{3,2,1,0:T(8,128)(2,1)} %all-to-all-done.blocks), custom_call_target="tpu_custom_call" | custom-call | tf_op jit(solution)/shard_map/up_and_down/pallas_call | solution.py:259
  104.1 9.9 %collective-permute-start.2 = (bf16[4,192,896]{2,1,0:T(8,128)(2,1)S(1)}, bf16[4,192,896]{2,1,0:T(8,128)(2,1)S(1)}, u32[]{:S(2)}, u32[]{:S(2)}) collective-permute-start(bf16[4,192,896]{2,1,0:T(8,128)(2,1)S(1)} %get-tuple-element.15), channel_id=1, source_target_pairs={{0,1},{1,0},{2,3},{3,2},{4,5},{5,4},{6,7},{7,6},{8,9},{9,8},{10,11... | collective-permute-start | bytes 4128776 | tf_op jit(solution)/shard_map/ppermute | solution.py:17
  114.1 2.7 %down_own.1.mine = bf16[4,192,896]{2,1,0:T(8,128)(2,1)S(1)} custom-call(s32[1]{0:T(128)} %bitcast.1.core, bf16[896,768]{1,0:T(8,128)(2,1)S(1)} %get-tuple-element.14.hidden, bf16[4,2,384,768]{3,2,1,0:T(8,128)(2,1)} %all-to-all-done.blocks), custom_call_target="tpu_custom_call" | custom-call | tf_op jit(solution)/shard_map/down_own/pallas_call | solution.py:274
  116.8 1.1 pair.1
  117.9 4.6 %collective-permute-start.3 = (bf16[192,896]{1,0:T(8,128)(2,1)}, bf16[192,896]{1,0:T(8,128)(2,1)S(1)}, u32[]{:S(2)}, u32[]{:S(2)}) collective-permute-start(bf16[192,896]{1,0:T(8,128)(2,1)} %get-tuple-element.17), channel_id=1, source_target_pairs={{0,4},{2,6},{4,0},{6,2},{1,5},{3,7},{5,1},{7,3},{8,12},{10,14},{12... | collective-permute-start | bytes 1032200 | tf_op jit(solution)/shard_map/ppermute | solution.py:17
  122.5 2.2 %collective-permute-start.4 = (bf16[192,896]{1,0:T(8,128)(2,1)}, bf16[192,896]{1,0:T(8,128)(2,1)S(1)}, u32[]{:S(2)}, u32[]{:S(2)}) collective-permute-start(bf16[192,896]{1,0:T(8,128)(2,1)} %get-tuple-element.18), channel_id=1, source_target_pairs={{0,2},{2,4},{4,6},{6,0},{1,3},{3,5},{5,7},{7,1},{8,10},{10,12},{12... | collective-permute-start | bytes 1032200 | tf_op jit(solution)/shard_map/ppermute | solution.py:17
  124.8 4.3 %collective-permute-start.5 = (bf16[192,896]{1,0:T(8,128)(2,1)S(1)}, bf16[192,896]{1,0:T(8,128)(2,1)S(1)}, u32[]{:S(2)}, u32[]{:S(2)}) collective-permute-start(bf16[192,896]{1,0:T(8,128)(2,1)S(1)} %get-tuple-element.19), channel_id=1, source_target_pairs={{0,6},{2,0},{4,2},{6,4},{1,7},{3,1},{5,3},{7,5},{8,14},{10,8},{12,... | collective-permute-start | bytes 1032200 | tf_op jit(solution)/shard_map/ppermute | solution.py:17
  129.3 1.5 %collective-permute-done.3.first = bf16[192,896]{1,0:T(8,128)(2,1)S(1)} collective-permute-done((bf16[192,896]{1,0:T(8,128)(2,1)}, bf16[192,896]{1,0:T(8,128)(2,1)S(1)}, u32[]{:S(2)}, u32[]{:S(2)}) %collective-permute-start.3) | collective-permute-done | bytes 344096 | tf_op jit(solution)/shard_map/ppermute | solution.py:17
  130.8 8.0 %collective-permute-done.4.second = bf16[192,896]{1,0:T(8,128)(2,1)S(1)} collective-permute-done((bf16[192,896]{1,0:T(8,128)(2,1)}, bf16[192,896]{1,0:T(8,128)(2,1)S(1)}, u32[]{:S(2)}, u32[]{:S(2)}) %collective-permute-start.4) | collective-permute-done | bytes 344096 | tf_op jit(solution)/shard_map/ppermute | solution.py:17
  139.5 1.1 copy.17
  (37 shorter events, 2.8 us)
Async XLA Ops:
  40.3 5.1 %copy-start.5 = (s32[64]{0:T(128)S(1)}, s32[64]{0:T(128)}, u32[]{:S(2)}) copy-start(s32[64]{0:T(128)} %first_crop.1) | copy-start | bytes 772
  40.4 11.0 %copy-start.9 = (bf16[1536]{0:T(1024)(128)(2,1)S(1)}, bf16[1536]{0:T(1024)(128)(2,1)}, u32[]{:S(2)}) copy-start(bf16[1536]{0:T(1024)(128)(2,1)} %param.18) | copy-start | bytes 9220
  40.4 11.1 %copy-start.7 = (bf16[49,1536]{1,0:T(8,128)(2,1)S(1)}, bf16[49,1536]{1,0:T(8,128)(2,1)}, u32[]{:S(2)}) copy-start(bf16[49,1536]{1,0:T(8,128)(2,1)} %param.17) | copy-start | bytes 451588
  40.4 11.1 %copy-start.8 = (bf16[3,1536]{1,0:T(4,128)(2,1)S(1)}, bf16[3,1536]{1,0:T(4,128)(2,1)}, u32[]{:S(2)}) copy-start(bf16[3,1536]{1,0:T(4,128)(2,1)} %param.16) | copy-start | bytes 27652
  40.4 58.1 %all-to-all-start = ((bf16[4,2,384,768]{3,2,1,0:T(8,128)(2,1)}), bf16[4,2,384,768]{3,2,1,0:T(8,128)(2,1)}, u32[]{:S(2)}, u32[]{:S(2)}) async-start(bf16[4,2,384,768]{3,2,1,0:T(8,128)(2,1)} %broadcast_in_dim.18), calls=%async_computation | async-start | bytes 9437184 | tf_op jit(solution)/shard_map/all_to_all | solution.py:28
  45.5 12.1 %copy-start.6 = (s32[64]{0:T(128)S(1)}, s32[64]{0:T(128)}, u32[]{:S(2)}) copy-start(s32[64]{0:T(128)} %crop_counts.1) | copy-start | bytes 772
  48.8 4.6 %collective-permute-start = (bf16[21,21,192]{2,1,0:T(8,128)(2,1)S(1)}, bf16[21,21,192]{2,1,0:T(8,128)(2,1)S(1)}, u32[]{:S(2)}, u32[]{:S(2)}) collective-permute-start(bf16[21,21,192]{2,1,0:T(8,128)(2,1)S(1)} %get-tuple-element.22), channel_id=1, source_target_pairs={{0,8},{8,16},{16,24},{24,32},{32,40},{40,48},{48,56},{56,64},{64,7... | collective-permute-start | bytes 508040 | tf_op jit(solution)/shard_map/ppermute | solution.py:42
  50.1 7.5 %collective-permute-start.1 = (bf16[21,21,192]{2,1,0:T(8,128)(2,1)S(1)}, bf16[21,21,192]{2,1,0:T(8,128)(2,1)S(1)}, u32[]{:S(2)}, u32[]{:S(2)}) collective-permute-start(bf16[21,21,192]{2,1,0:T(8,128)(2,1)S(1)} %get-tuple-element.21), channel_id=1, source_target_pairs={{8,0},{16,8},{24,16},{32,24},{40,32},{48,40},{56,48},{64,56},{72,6... | collective-permute-start | bytes 508040 | tf_op jit(solution)/shard_map/ppermute | solution.py:45
  66.4 0.9 copy-start
  93.6 0.7 copy-start.2
  93.6 0.7 copy-start.3
  94.3 4.1 %copy-start.4 = (bf16[768]{0:T(1024)(128)(2,1)S(1)}, bf16[768]{0:T(1024)(128)(2,1)}, u32[]{:S(2)}) copy-start(bf16[768]{0:T(1024)(128)(2,1)} %b_up.1) | copy-start | bytes 4612
  104.1 12.7 %collective-permute-start.2 = (bf16[4,192,896]{2,1,0:T(8,128)(2,1)S(1)}, bf16[4,192,896]{2,1,0:T(8,128)(2,1)S(1)}, u32[]{:S(2)}, u32[]{:S(2)}) collective-permute-start(bf16[4,192,896]{2,1,0:T(8,128)(2,1)S(1)} %get-tuple-element.15), channel_id=1, source_target_pairs={{0,1},{1,0},{2,3},{3,2},{4,5},{5,4},{6,7},{7,6},{8,9},{9,8},{10,11... | collective-permute-start | bytes 4128776 | tf_op jit(solution)/shard_map/ppermute | solution.py:17
  116.8 12.3 %copy-start.11 = (bf16[192]{0:T(256)(128)(2,1)S(1)}, bf16[192]{0:T(256)(128)(2,1)}, u32[]{:S(2)}) copy-start(bf16[192]{0:T(256)(128)(2,1)} %param.24) | copy-start | bytes 1156
  116.8 12.4 %copy-start.10 = (f32[192]{0:T(256)S(1)}, f32[192]{0:T(256)}, u32[]{:S(2)}) copy-start(f32[192]{0:T(256)} %param.25) | copy-start | bytes 2308
  116.8 22.1 %copy-start.1 = (f32[882,192]{1,0:T(8,128)S(1)}, f32[882,192]{1,0:T(8,128)}, u32[]{:S(2)}) copy-start(f32[882,192]{1,0:T(8,128)} %copy-done) | copy-start | bytes 2032132
  117.9 12.9 %collective-permute-start.3 = (bf16[192,896]{1,0:T(8,128)(2,1)}, bf16[192,896]{1,0:T(8,128)(2,1)S(1)}, u32[]{:S(2)}, u32[]{:S(2)}) collective-permute-start(bf16[192,896]{1,0:T(8,128)(2,1)} %get-tuple-element.17), channel_id=1, source_target_pairs={{0,4},{2,6},{4,0},{6,2},{1,5},{3,7},{5,1},{7,3},{8,12},{10,14},{12... | collective-permute-start | bytes 1032200 | tf_op jit(solution)/shard_map/ppermute | solution.py:17
  122.5 16.3 %collective-permute-start.4 = (bf16[192,896]{1,0:T(8,128)(2,1)}, bf16[192,896]{1,0:T(8,128)(2,1)S(1)}, u32[]{:S(2)}, u32[]{:S(2)}) collective-permute-start(bf16[192,896]{1,0:T(8,128)(2,1)} %get-tuple-element.18), channel_id=1, source_target_pairs={{0,2},{2,4},{4,6},{6,0},{1,3},{3,5},{5,7},{7,1},{8,10},{10,12},{12... | collective-permute-start | bytes 1032200 | tf_op jit(solution)/shard_map/ppermute | solution.py:17
  124.8 14.1 %collective-permute-start.5 = (bf16[192,896]{1,0:T(8,128)(2,1)S(1)}, bf16[192,896]{1,0:T(8,128)(2,1)S(1)}, u32[]{:S(2)}, u32[]{:S(2)}) collective-permute-start(bf16[192,896]{1,0:T(8,128)(2,1)S(1)} %get-tuple-element.19), channel_id=1, source_target_pairs={{0,6},{2,0},{4,2},{6,4},{1,7},{3,1},{5,3},{7,5},{8,14},{10,8},{12,... | collective-permute-start | bytes 1032200 | tf_op jit(solution)/shard_map/ppermute | solution.py:17

commit v11 on v8

--- a/solution.py
+++ b/solution.py
@@ -11,6 +11,7 @@
 PER_DEV = 2
 KSIDE = 7
 DISTANCES = (2, 1, 3)
+Y_STEPS = (0, 2, 1, 3)
 
 
 def shift(block, axis, distance, size):
@@ -24,7 +25,7 @@
 
 
 def gather_y(own):
-    return own, *(shift(own, "y", -d, NY) for d in (1, 2, 3))
+    return own, *(shift(own, "y", -d, NY) for d in Y_STEPS[1:])
 
 
 def exchange(slots, seq_index, first_crop):
@@ -64,7 +65,9 @@
     for t in range(KSIDE * KSIDE):
         taps[t] = jnp.broadcast_to(table[t : t + 1, :].astype(f32), taps.shape[1:])
     padded[...] = jnp.zeros_like(padded)
-    shifted[...] = jnp.zeros_like(shifted)
+    edge = jnp.zeros((KSIDE, PER_DEV, margin) + shifted.shape[3:], f32)
+    shifted[:, :, :margin] = edge
+    shifted[:, :, margin + side :] = edge
     for n in range(PER_DEV):
         target = PER_DEV * here + n
 
@@ -176,7 +179,7 @@
 def copy_down_rows(blocks, buffer, sems, y, core):
     width = buffer.shape[0] // NX
     copies = []
-    for d, block in enumerate(blocks):
+    for d, block in zip(Y_STEPS, blocks):
         source = pl.multiple_of(core * width, width)
         target = pl.multiple_of(lax.rem(y + d, NY) * width, width)
         copies.append(
@@ -201,7 +204,7 @@
     y, core = y_ref[0], core_ref[0]
     bias = b_up[...].astype(jnp.float32)[None, :]
     ups = []
-    for d, block in enumerate(blocks):
+    for d, block in zip(Y_STEPS, blocks):
         rows = block.shape[1]
         target = pl.multiple_of(lax.rem(y + d, NY) * rows, rows)
         ups.append(pltpu.make_async_copy(block.at[0], up.at[pl.ds(target, rows), :], up_sem.at[d]))

time: 137 us -> 135 us (0.985)
  starting transfers between devices: 31.8 us -> 28.4 us
  waiting for transfers between devices: 9.64 us -> 11.5 us
    ppermute x7, starting transfers between devices: 24.4 us -> 21 us  [shift(): lax.ppermute(block, axis, [(i, (i + distance) % size) for i in range(size)])]
    ppermute x7, waiting for transfers between devices: 9.53 us -> 11.4 us  [shift(): lax.ppermute(block, axis, [(i, (i + distance) % size) for i in range(size)])]
  transfers between devices with their start and end apart: 9 -> 9, of which waited for: 3 -> 4; matrix products, arithmetic and copies ran while one was open for 4% -> 4% of each run, Pallas kernels for 10% -> 10%
where the time goes in v11:
time: 135 us; the launch traced here: 134 us
  blocking collectives  62.9 us (47%)
  starting transfers between devices  28.4 us (21%)
  Pallas kernels  20.2 us (15%)
  waiting for transfers between devices  11.5 us (9%)
  local copies, waits for them, and re-layouts  7.05 us (5%)
  other arithmetic  2.29 us (2%)
  between operations  1.5 us (1%)
    all_gather x1, blocking collectives, gather_z(): over_z = lax.all_gather(both.astype(jnp.float16), 'z', axis=1, tiled=True)  36 us
    all_gather x1, blocking collectives, per_device(): conv_all = lax.all_gather(conv_t, TP, axis=0, tiled=True).astype(f32)  26.9 us
    ppermute x7, starting transfers between devices, shift(): lax.ppermute(block, axis, [(i, (i + distance) % size) for i in range(size)])  21 us
    ppermute x7, waiting for transfers between devices, shift(): lax.ppermute(block, axis, [(i, (i + distance) % size) for i in range(size)])  11.4 us
    pallas_call x1, Pallas kernels, depthwise(): pl.pallas_call(conv_kernel, out_shape=(jax.ShapeDtypeStruct((cells, width...  8.41 us
    ppermute x1, starting transfers between devices, exchange(): lax.ppermute(crop(target - 1), SEQ, [(i + 1, i) for i in range(count - 1)])  5.47 us
    pallas_call x1, Pallas kernels, mlp_sum(): pl.pallas_call(first_kernel, out_shape=(jax.ShapeDtypeStruct((cells, unit...  5.29 us
  transfers between devices with their start and end apart: 9, of which 4 were waited for; matrix products, arithmetic and copies ran while one was open for 4% of the time, Pallas kernels for 10%

profile of v11, /device:TPU:25, one launch (start us, length us, event | category | flops | bytes accessed | tf_op | source)
XLA Modules:
  0.0 133.9 jit_solution(8269077247153284357)
XLA Ops:
  0.0 0.8 multiply_convert_fusion.1
  0.8 36.0 %all-gather.3 = f16[2,384,768]{2,1,0:T(8,128)(2,1)S(1)} all-gather(f16[2,24,768]{2,1,0:T(8,128)(2,1)S(1)} %multiply_convert_fusion.1), channel_id=1, replica_groups=mesh['y'=4,'z'=16,'x'=4,'core'=2] {'z'}, dimensions={1}, use_global_device_ids=true | all-gather | bytes 1253376 | tf_op jit(solution)/shard_map/all_gather | solution.py:23
  37.0 2.9 %collective-permute-start.2 = (bf16[2,384,768]{2,1,0:T(8,128)(2,1)S(1)}, bf16[2,384,768]{2,1,0:T(8,128)(2,1)S(1)}, u32[]{:S(2)}, u32[]{:S(2)}) collective-permute-start(bf16[2,384,768]{2,1,0:T(8,128)(2,1)S(1)} %multiply_convert_fusion.refs_0_), channel_id=1, source_target_pairs={{0,256},{128,384},{256,0},{384,128},{1,257},{129,385},{257,1},{385... | collective-permute-start | bytes 3538952 | tf_op jit(solution)/shard_map/ppermute | solution.py:18
  39.9 1.9 %collective-permute-start.3 = (bf16[2,384,768]{2,1,0:T(8,128)(2,1)S(1)}, bf16[2,384,768]{2,1,0:T(8,128)(2,1)S(1)}, u32[]{:S(2)}, u32[]{:S(2)}) collective-permute-start(bf16[2,384,768]{2,1,0:T(8,128)(2,1)S(1)} %multiply_convert_fusion.refs_0_), channel_id=1, source_target_pairs={{0,384},{128,0},{256,128},{384,256},{1,385},{129,1},{257,129},{385... | collective-permute-start | bytes 3538952 | tf_op jit(solution)/shard_map/ppermute | solution.py:18
  41.8 4.6 %collective-permute-start.4 = (bf16[2,384,768]{2,1,0:T(8,128)(2,1)S(1)}, bf16[2,384,768]{2,1,0:T(8,128)(2,1)}, u32[]{:S(2)}, u32[]{:S(2)}) collective-permute-start(bf16[2,384,768]{2,1,0:T(8,128)(2,1)S(1)} %multiply_convert_fusion.refs_0_), channel_id=1, source_target_pairs={{0,128},{128,256},{256,384},{384,0},{1,129},{129,257},{257,385},{3... | collective-permute-start | bytes 3538952 | tf_op jit(solution)/shard_map/ppermute | solution.py:18
  48.3 1.3 %dynamic-slice_bitcast_fusion = (bf16[21,21,192]{2,1,0:T(8,128)(2,1)S(1)}, bf16[21,21,192]{2,1,0:T(8,128)(2,1)S(1)}) fusion(bf16[3,21,21,1536]{3,2,1,0:T(8,128)(2,1)} %param.13, s32[]{:T(128)S(6)} %min.14, s32[]{:T(128)S(6)} %select_n.14, s32[]{:T(128)S(6)} %min.12), kind=kLoop, calls=%fused_computation.1 | loop fusion | bytes 677388 | tf_op jit(solution)/shard_map/jit(dynamic_index_in_dim)/squeeze | solution.py:37
  49.7 1.9 %collective-permute-start = (bf16[21,21,192]{2,1,0:T(8,128)(2,1)S(1)}, bf16[21,21,192]{2,1,0:T(8,128)(2,1)S(1)}, u32[]{:S(2)}, u32[]{:S(2)}) collective-permute-start(bf16[21,21,192]{2,1,0:T(8,128)(2,1)S(1)} %get-tuple-element.22), channel_id=1, source_target_pairs={{0,8},{8,16},{16,24},{24,32},{32,40},{40,48},{48,56},{56,64},{64,7... | collective-permute-start | bytes 508040 | tf_op jit(solution)/shard_map/ppermute | solution.py:42
  51.6 5.5 %collective-permute-start.1 = (bf16[21,21,192]{2,1,0:T(8,128)(2,1)S(1)}, bf16[21,21,192]{2,1,0:T(8,128)(2,1)S(1)}, u32[]{:S(2)}, u32[]{:S(2)}) collective-permute-start(bf16[21,21,192]{2,1,0:T(8,128)(2,1)S(1)} %get-tuple-element.21), channel_id=1, source_target_pairs={{8,0},{16,8},{24,16},{32,24},{40,32},{48,40},{56,48},{64,56},{72,6... | collective-permute-start | bytes 508040 | tf_op jit(solution)/shard_map/ppermute | solution.py:45
  57.8 0.9 fusion.1.table
  58.6 1.6 %constant_dynamic-slice_fusion.slots = bf16[3,21,21,192]{3,2,1,0:T(8,128)(2,1)S(1)} fusion(bf16[3,21,21,1536]{3,2,1,0:T(8,128)(2,1)} %param.13, s32[]{:T(128)S(6)} %select_n.12), kind=kLoop, calls=%fused_computation.9 | loop fusion | bytes 1016068 | tf_op jit(solution)/shard_map/dynamic_slice | solution.py:314
  60.4 8.4 %conv.1 = (f32[882,192]{1,0:T(8,128)S(1)}, f32[192,896]{1,0:T(8,128)S(1)}) custom-call(s32[1]{0:T(128)} %bitcast.3.seq, s32[64]{0:T(128)S(1)} %copy-done.5, s32[64]{0:T(128)S(1)} %copy-done.6, bf16[3,21,21,192]{3,2,1,0:T(8,128)(2,1)S(1)} %constant_dynamic-slice_fusion.slots, bf16[21,21,192]{2,1,0:T(8,128)(2,1)S(1)} %collective-permute-done.before, ...), custom_call_target="tpu_custom_call" | custom-call | tf_op jit(solution)/shard_map/conv/pallas_call | solution.py:126
  68.8 0.9 copy-done
  69.7 26.9 %all-gather.2 = f16[1536,896]{1,0:T(8,128)(2,1)S(1)} all-gather(f16[192,896]{1,0:T(8,128)(2,1)S(1)} %convert_element_type.19), channel_id=1, replica_groups=mesh['y'=4,'z'=16,'x'=4,'core'=2] {'x','core'}, dimensions={0}, use_global_device_ids=true | all-gather | bytes 3096576 | tf_op jit(solution)/shard_map/all_gather | solution.py:324
  97.3 2.4 %norm.1.normed = bf16[896,1536]{1,0:T(8,128)(2,1)S(1)} custom-call(f32[1536,896]{1,0:T(8,128)S(1)} %convert_element_type.20.conv, bf16[1536]{0:T(1024)(128)(2,1)S(1)} %copy-done.2, bf16[1536]{0:T(1024)(128)(2,1)S(1)} %copy-done.3), custom_call_target="tpu_custom_call" | custom-call | tf_op jit(solution)/shard_map/norm/pallas_call | solution.py:169
  99.8 5.3 %up_and_down.1 = (bf16[896,768]{1,0:T(8,128)(2,1)S(1)}, bf16[4,192,896]{2,1,0:T(8,128)(2,1)S(1)}) custom-call(s32[1]{0:T(128)} %bitcast.1.y_ref.y, s32[1]{0:T(128)} %bitcast.2.core_ref.core, bf16[896,1536]{1,0:T(8,128)(2,1)S(1)} %norm.1.normed, bf16[768]{0:T(1024)(128)(2,1)S(1)} %copy-done.4, bf16[2,384,768]{2,1,0:T(8,128)(2,1)S(1)} %multiply_convert_fusion.refs_0_, ...), custom_call_target="tpu_custom_call" | custom-call | tf_op jit(solution)/shard_map/up_and_down/pallas_call | solution.py:265
  105.1 2.1 %collective-permute-start.5 = (bf16[4,192,896]{2,1,0:T(8,128)(2,1)S(1)}, bf16[4,192,896]{2,1,0:T(8,128)(2,1)S(1)}, u32[]{:S(2)}, u32[]{:S(2)}) collective-permute-start(bf16[4,192,896]{2,1,0:T(8,128)(2,1)S(1)} %get-tuple-element.15), channel_id=1, source_target_pairs={{0,1},{1,0},{2,3},{3,2},{4,5},{5,4},{6,7},{7,6},{8,9},{9,8},{10,11... | collective-permute-start | bytes 4128776 | tf_op jit(solution)/shard_map/ppermute | solution.py:18
  107.1 2.6 %down_own.1.mine = bf16[4,192,896]{2,1,0:T(8,128)(2,1)S(1)} custom-call(s32[1]{0:T(128)} %bitcast.1.y_ref.y, s32[1]{0:T(128)} %bitcast.2.core_ref.core, bf16[896,768]{1,0:T(8,128)(2,1)S(1)} %get-tuple-element.14.hidden, bf16[2,384,768]{2,1,0:T(8,128)(2,1)S(1)} %multiply_convert_fusion.refs_0_, bf16[2,384,768]{2,1,0:T(8,128)(2,1)S(1)} %collective-permute-done.2.refs_1_, ...), custom_call_target="tpu_custom_call" | custom-call | tf_op jit(solution)/shard_map/down_own/pallas_call | solution.py:280
  110.1 1.1 pair.1
  111.2 3.1 %collective-permute-start.6 = (bf16[192,896]{1,0:T(8,128)(2,1)}, bf16[192,896]{1,0:T(8,128)(2,1)S(1)}, u32[]{:S(2)}, u32[]{:S(2)}) collective-permute-start(bf16[192,896]{1,0:T(8,128)(2,1)} %get-tuple-element.17), channel_id=1, source_target_pairs={{0,4},{2,6},{4,0},{6,2},{1,5},{3,7},{5,1},{7,3},{8,12},{10,14},{12... | collective-permute-start | bytes 1032200 | tf_op jit(solution)/shard_map/ppermute | solution.py:18
  114.2 2.2 %collective-permute-start.7 = (bf16[192,896]{1,0:T(8,128)(2,1)}, bf16[192,896]{1,0:T(8,128)(2,1)S(1)}, u32[]{:S(2)}, u32[]{:S(2)}) collective-permute-start(bf16[192,896]{1,0:T(8,128)(2,1)} %get-tuple-element.18), channel_id=1, source_target_pairs={{0,2},{2,4},{4,6},{6,0},{1,3},{3,5},{5,7},{7,1},{8,10},{10,12},{12... | collective-permute-start | bytes 1032200 | tf_op jit(solution)/shard_map/ppermute | solution.py:18
  116.4 4.3 %collective-permute-start.8 = (bf16[192,896]{1,0:T(8,128)(2,1)S(1)}, bf16[192,896]{1,0:T(8,128)(2,1)S(1)}, u32[]{:S(2)}, u32[]{:S(2)}) collective-permute-start(bf16[192,896]{1,0:T(8,128)(2,1)S(1)} %get-tuple-element.19), channel_id=1, source_target_pairs={{0,6},{2,0},{4,2},{6,4},{1,7},{3,1},{5,3},{7,5},{8,14},{10,8},{12,... | collective-permute-start | bytes 1032200 | tf_op jit(solution)/shard_map/ppermute | solution.py:18
  121.0 3.3 %collective-permute-done.6.first = bf16[192,896]{1,0:T(8,128)(2,1)S(1)} collective-permute-done((bf16[192,896]{1,0:T(8,128)(2,1)}, bf16[192,896]{1,0:T(8,128)(2,1)S(1)}, u32[]{:S(2)}, u32[]{:S(2)}) %collective-permute-start.6) | collective-permute-done | bytes 344096 | tf_op jit(solution)/shard_map/ppermute | solution.py:18
  124.3 7.8 %collective-permute-done.7.second = bf16[192,896]{1,0:T(8,128)(2,1)S(1)} collective-permute-done((bf16[192,896]{1,0:T(8,128)(2,1)}, bf16[192,896]{1,0:T(8,128)(2,1)S(1)}, u32[]{:S(2)}, u32[]{:S(2)}) %collective-permute-start.7) | collective-permute-done | bytes 344096 | tf_op jit(solution)/shard_map/ppermute | solution.py:18
  132.8 1.1 copy.17
  (36 shorter events, 3.6 us)
Async XLA Ops:
  36.8 9.6 %copy-start.5 = (s32[64]{0:T(128)S(1)}, s32[64]{0:T(128)}, u32[]{:S(2)}) copy-start(s32[64]{0:T(128)} %first_crop.1) | copy-start | bytes 772
  36.8 21.0 %copy-start.7 = (bf16[3,1536]{1,0:T(4,128)(2,1)S(1)}, bf16[3,1536]{1,0:T(4,128)(2,1)}, u32[]{:S(2)}) copy-start(bf16[3,1536]{1,0:T(4,128)(2,1)} %param.16) | copy-start | bytes 27652
  37.0 62.7 %collective-permute-start.2 = (bf16[2,384,768]{2,1,0:T(8,128)(2,1)S(1)}, bf16[2,384,768]{2,1,0:T(8,128)(2,1)S(1)}, u32[]{:S(2)}, u32[]{:S(2)}) collective-permute-start(bf16[2,384,768]{2,1,0:T(8,128)(2,1)S(1)} %multiply_convert_fusion.refs_0_), channel_id=1, source_target_pairs={{0,256},{128,384},{256,0},{384,128},{1,257},{129,385},{257,1},{385... | collective-permute-start | bytes 3538952 | tf_op jit(solution)/shard_map/ppermute | solution.py:18
  39.9 59.8 %collective-permute-start.3 = (bf16[2,384,768]{2,1,0:T(8,128)(2,1)S(1)}, bf16[2,384,768]{2,1,0:T(8,128)(2,1)S(1)}, u32[]{:S(2)}, u32[]{:S(2)}) collective-permute-start(bf16[2,384,768]{2,1,0:T(8,128)(2,1)S(1)} %multiply_convert_fusion.refs_0_), channel_id=1, source_target_pairs={{0,384},{128,0},{256,128},{384,256},{1,385},{129,1},{257,129},{385... | collective-permute-start | bytes 3538952 | tf_op jit(solution)/shard_map/ppermute | solution.py:18
  41.8 57.9 %collective-permute-start.4 = (bf16[2,384,768]{2,1,0:T(8,128)(2,1)S(1)}, bf16[2,384,768]{2,1,0:T(8,128)(2,1)}, u32[]{:S(2)}, u32[]{:S(2)}) collective-permute-start(bf16[2,384,768]{2,1,0:T(8,128)(2,1)S(1)} %multiply_convert_fusion.refs_0_), channel_id=1, source_target_pairs={{0,128},{128,256},{256,384},{384,0},{1,129},{129,257},{257,385},{3... | collective-permute-start | bytes 3538952 | tf_op jit(solution)/shard_map/ppermute | solution.py:18
  48.3 12.1 %copy-start.6 = (s32[64]{0:T(128)S(1)}, s32[64]{0:T(128)}, u32[]{:S(2)}) copy-start(s32[64]{0:T(128)} %crop_counts.1) | copy-start | bytes 772
  49.7 10.6 %collective-permute-start = (bf16[21,21,192]{2,1,0:T(8,128)(2,1)S(1)}, bf16[21,21,192]{2,1,0:T(8,128)(2,1)S(1)}, u32[]{:S(2)}, u32[]{:S(2)}) collective-permute-start(bf16[21,21,192]{2,1,0:T(8,128)(2,1)S(1)} %get-tuple-element.22), channel_id=1, source_target_pairs={{0,8},{8,16},{16,24},{24,32},{32,40},{40,48},{48,56},{56,64},{64,7... | collective-permute-start | bytes 508040 | tf_op jit(solution)/shard_map/ppermute | solution.py:42
  51.6 8.8 %collective-permute-start.1 = (bf16[21,21,192]{2,1,0:T(8,128)(2,1)S(1)}, bf16[21,21,192]{2,1,0:T(8,128)(2,1)S(1)}, u32[]{:S(2)}, u32[]{:S(2)}) collective-permute-start(bf16[21,21,192]{2,1,0:T(8,128)(2,1)S(1)} %get-tuple-element.21), channel_id=1, source_target_pairs={{8,0},{16,8},{24,16},{32,24},{40,32},{48,40},{56,48},{64,56},{72,6... | collective-permute-start | bytes 508040 | tf_op jit(solution)/shard_map/ppermute | solution.py:45
  68.8 0.9 copy-start
  96.6 0.7 copy-start.2
  96.6 0.7 copy-start.3
  97.3 2.4 %copy-start.4 = (bf16[768]{0:T(1024)(128)(2,1)S(1)}, bf16[768]{0:T(1024)(128)(2,1)}, u32[]{:S(2)}) copy-start(bf16[768]{0:T(1024)(128)(2,1)} %b_up.1) | copy-start | bytes 4612
  105.1 5.0 %collective-permute-start.5 = (bf16[4,192,896]{2,1,0:T(8,128)(2,1)S(1)}, bf16[4,192,896]{2,1,0:T(8,128)(2,1)S(1)}, u32[]{:S(2)}, u32[]{:S(2)}) collective-permute-start(bf16[4,192,896]{2,1,0:T(8,128)(2,1)S(1)} %get-tuple-element.15), channel_id=1, source_target_pairs={{0,1},{1,0},{2,3},{3,2},{4,5},{5,4},{6,7},{7,6},{8,9},{9,8},{10,11... | collective-permute-start | bytes 4128776 | tf_op jit(solution)/shard_map/ppermute | solution.py:18
  110.1 10.7 %copy-start.9 = (bf16[192]{0:T(256)(128)(2,1)S(1)}, bf16[192]{0:T(256)(128)(2,1)}, u32[]{:S(2)}) copy-start(bf16[192]{0:T(256)(128)(2,1)} %param.24) | copy-start | bytes 1156
  110.1 10.8 %copy-start.8 = (f32[192]{0:T(256)S(1)}, f32[192]{0:T(256)}, u32[]{:S(2)}) copy-start(f32[192]{0:T(256)} %param.25) | copy-start | bytes 2308
  110.1 22.0 %copy-start.1 = (f32[882,192]{1,0:T(8,128)S(1)}, f32[882,192]{1,0:T(8,128)}, u32[]{:S(2)}) copy-start(f32[882,192]{1,0:T(8,128)} %copy-done) | copy-start | bytes 2032132
  111.2 13.1 %collective-permute-start.6 = (bf16[192,896]{1,0:T(8,128)(2,1)}, bf16[192,896]{1,0:T(8,128)(2,1)S(1)}, u32[]{:S(2)}, u32[]{:S(2)}) collective-permute-start(bf16[192,896]{1,0:T(8,128)(2,1)} %get-tuple-element.17), channel_id=1, source_target_pairs={{0,4},{2,6},{4,0},{6,2},{1,5},{3,7},{5,1},{7,3},{8,12},{10,14},{12... | collective-permute-start | bytes 1032200 | tf_op jit(solution)/shard_map/ppermute | solution.py:18
  114.2 17.9 %collective-permute-start.7 = (bf16[192,896]{1,0:T(8,128)(2,1)}, bf16[192,896]{1,0:T(8,128)(2,1)S(1)}, u32[]{:S(2)}, u32[]{:S(2)}) collective-permute-start(bf16[192,896]{1,0:T(8,128)(2,1)} %get-tuple-element.18), channel_id=1, source_target_pairs={{0,2},{2,4},{4,6},{6,0},{1,3},{3,5},{5,7},{7,1},{8,10},{10,12},{12... | collective-permute-start | bytes 1032200 | tf_op jit(solution)/shard_map/ppermute | solution.py:18
  116.4 15.7 %collective-permute-start.8 = (bf16[192,896]{1,0:T(8,128)(2,1)S(1)}, bf16[192,896]{1,0:T(8,128)(2,1)S(1)}, u32[]{:S(2)}, u32[]{:S(2)}) collective-permute-start(bf16[192,896]{1,0:T(8,128)(2,1)S(1)} %get-tuple-element.19), channel_id=1, source_target_pairs={{0,6},{2,0},{4,2},{6,4},{1,7},{3,1},{5,3},{7,5},{8,14},{10,8},{12,... | collective-permute-start | bytes 1032200 | tf_op jit(solution)/shard_map/ppermute | solution.py:18

commit v12 on v11

--- a/solution.py
+++ b/solution.py
@@ -48,7 +48,7 @@
 
 def conv_kernel(
     seq, first_crop, crop_counts, slots, before, after, table,
-    block_in, conv, padded, shifted, taps, rows, flat,
+    block_out, conv, padded, shifted, taps, rows, flat, block_in, sem,
 ):
     f32 = jnp.float32
     side = rows.shape[1]
@@ -91,6 +91,8 @@
         padded[:, margin : margin + side, :] = crop
         for b in range(KSIDE):
             shifted[b, n, margin : margin + side] = padded[:, b : b + shifted.shape[3], :]
+    keep = pltpu.make_async_copy(block_in, block_out, sem)
+    keep.start()
     columns, width = shifted.shape[3:]
     groups = side // 3
 
@@ -115,6 +117,7 @@
             at = n * cells + i * side
             flat[at : at + side, :] = rows[n, i][:side]
     conv[...] = flat[...].T
+    keep.wait()
 
 
 def depthwise(seq_index, first_crop, crop_counts, slots, before, after, table):
@@ -126,17 +129,19 @@
     return pl.pallas_call(
         conv_kernel,
         out_shape=(
-            jax.ShapeDtypeStruct((cells, width), f32),
+            pltpu.HBM((cells, width), f32),
             jax.ShapeDtypeStruct((width, padded_cells), f32),
         ),
         in_specs=[whole(pltpu.SMEM)] * 3 + [whole()] * 4,
-        out_specs=(whole(), whole()),
+        out_specs=(whole(pltpu.HBM), whole()),
         scratch_shapes=[
             pltpu.VMEM((side, columns + 8, width), f32),
             pltpu.VMEM((KSIDE, PER_DEV, side + 6, columns, width), f32),
             pltpu.VMEM((KSIDE * KSIDE, 8, width), f32),
             pltpu.VMEM((PER_DEV, side, columns, width), f32),
             pltpu.VMEM((padded_cells, width), f32),
+            pltpu.VMEM((cells, width), f32),
+            pltpu.SemaphoreType.DMA,
         ],
         compiler_params=vmem(18),
         name="conv",

time: 135 us -> 134 us (level)
  no operation moved by 1% of the time
where the time goes in v12:
time: 134 us; the launch traced here: 133 us
  blocking collectives  63 us (47%)
  starting transfers between devices  28.4 us (21%)
  Pallas kernels  20.2 us (15%)
  waiting for transfers between devices  11.5 us (9%)
  local copies, waits for them, and re-layouts  6.14 us (5%)
  other arithmetic  2.29 us (2%)
  between operations  1.41 us (1%)
    all_gather x1, blocking collectives, gather_z(): over_z = lax.all_gather(both.astype(jnp.float16), 'z', axis=1, tiled=True)  36 us
    all_gather x1, blocking collectives, per_device(): conv_all = lax.all_gather(conv_t, TP, axis=0, tiled=True).astype(f32)  27 us
    ppermute x7, starting transfers between devices, shift(): lax.ppermute(block, axis, [(i, (i + distance) % size) for i in range(size)])  21 us
    ppermute x7, waiting for transfers between devices, shift(): lax.ppermute(block, axis, [(i, (i + distance) % size) for i in range(size)])  11.4 us
    pallas_call x1, Pallas kernels, depthwise(): pl.pallas_call(conv_kernel, out_shape=(pltpu.HBM((cells, width), f32), ja...  8.41 us
    ppermute x1, starting transfers between devices, exchange(): lax.ppermute(crop(target - 1), SEQ, [(i + 1, i) for i in range(count - 1)])  5.47 us
    pallas_call x1, Pallas kernels, mlp_sum(): pl.pallas_call(first_kernel, out_shape=(jax.ShapeDtypeStruct((cells, unit...  5.29 us
  transfers between devices with their start and end apart: 9, of which 4 were waited for; matrix products, arithmetic and copies ran while one was open for 4% of the time, Pallas kernels for 10%

profile of v12, /device:TPU:25, one launch (start us, length us, event | category | flops | bytes accessed | tf_op | source)
XLA Modules:
  0.0 132.9 jit_solution(17527773913211909295)
XLA Ops:
  0.0 0.8 multiply_convert_fusion.1
  0.8 36.0 %all-gather.3 = f16[2,384,768]{2,1,0:T(8,128)(2,1)S(1)} all-gather(f16[2,24,768]{2,1,0:T(8,128)(2,1)S(1)} %multiply_convert_fusion.1), channel_id=1, replica_groups=mesh['y'=4,'z'=16,'x'=4,'core'=2] {'z'}, dimensions={1}, use_global_device_ids=true | all-gather | bytes 1253376 | tf_op jit(solution)/shard_map/all_gather | solution.py:23
  37.0 2.9 %collective-permute-start.2 = (bf16[2,384,768]{2,1,0:T(8,128)(2,1)S(1)}, bf16[2,384,768]{2,1,0:T(8,128)(2,1)S(1)}, u32[]{:S(2)}, u32[]{:S(2)}) collective-permute-start(bf16[2,384,768]{2,1,0:T(8,128)(2,1)S(1)} %multiply_convert_fusion.refs_0_), channel_id=1, source_target_pairs={{0,256},{128,384},{256,0},{384,128},{1,257},{129,385},{257,1},{385... | collective-permute-start | bytes 3538952 | tf_op jit(solution)/shard_map/ppermute | solution.py:18
  39.9 1.9 %collective-permute-start.3 = (bf16[2,384,768]{2,1,0:T(8,128)(2,1)S(1)}, bf16[2,384,768]{2,1,0:T(8,128)(2,1)S(1)}, u32[]{:S(2)}, u32[]{:S(2)}) collective-permute-start(bf16[2,384,768]{2,1,0:T(8,128)(2,1)S(1)} %multiply_convert_fusion.refs_0_), channel_id=1, source_target_pairs={{0,384},{128,0},{256,128},{384,256},{1,385},{129,1},{257,129},{385... | collective-permute-start | bytes 3538952 | tf_op jit(solution)/shard_map/ppermute | solution.py:18
  41.8 4.6 %collective-permute-start.4 = (bf16[2,384,768]{2,1,0:T(8,128)(2,1)S(1)}, bf16[2,384,768]{2,1,0:T(8,128)(2,1)}, u32[]{:S(2)}, u32[]{:S(2)}) collective-permute-start(bf16[2,384,768]{2,1,0:T(8,128)(2,1)S(1)} %multiply_convert_fusion.refs_0_), channel_id=1, source_target_pairs={{0,128},{128,256},{256,384},{384,0},{1,129},{129,257},{257,385},{3... | collective-permute-start | bytes 3538952 | tf_op jit(solution)/shard_map/ppermute | solution.py:18
  48.2 1.3 %dynamic-slice_bitcast_fusion = (bf16[21,21,192]{2,1,0:T(8,128)(2,1)S(1)}, bf16[21,21,192]{2,1,0:T(8,128)(2,1)S(1)}) fusion(bf16[3,21,21,1536]{3,2,1,0:T(8,128)(2,1)} %param.13, s32[]{:T(128)S(6)} %min.14, s32[]{:T(128)S(6)} %select_n.14, s32[]{:T(128)S(6)} %min.12), kind=kLoop, calls=%fused_computation.1 | loop fusion | bytes 677388 | tf_op jit(solution)/shard_map/jit(dynamic_index_in_dim)/squeeze | solution.py:37
  49.5 1.9 %collective-permute-start = (bf16[21,21,192]{2,1,0:T(8,128)(2,1)S(1)}, bf16[21,21,192]{2,1,0:T(8,128)(2,1)S(1)}, u32[]{:S(2)}, u32[]{:S(2)}) collective-permute-start(bf16[21,21,192]{2,1,0:T(8,128)(2,1)S(1)} %get-tuple-element.22), channel_id=1, source_target_pairs={{0,8},{8,16},{16,24},{24,32},{32,40},{40,48},{48,56},{56,64},{64,7... | collective-permute-start | bytes 508040 | tf_op jit(solution)/shard_map/ppermute | solution.py:42
  51.5 5.5 %collective-permute-start.1 = (bf16[21,21,192]{2,1,0:T(8,128)(2,1)S(1)}, bf16[21,21,192]{2,1,0:T(8,128)(2,1)S(1)}, u32[]{:S(2)}, u32[]{:S(2)}) collective-permute-start(bf16[21,21,192]{2,1,0:T(8,128)(2,1)S(1)} %get-tuple-element.21), channel_id=1, source_target_pairs={{8,0},{16,8},{24,16},{32,24},{40,32},{48,40},{56,48},{64,56},{72,6... | collective-permute-start | bytes 508040 | tf_op jit(solution)/shard_map/ppermute | solution.py:45
  56.9 0.7 broadcast_in_dim.11
  57.6 0.9 fusion.1.table
  58.5 1.6 %constant_dynamic-slice_fusion.slots = bf16[3,21,21,192]{3,2,1,0:T(8,128)(2,1)S(1)} fusion(bf16[3,21,21,1536]{3,2,1,0:T(8,128)(2,1)} %param.13, s32[]{:T(128)S(6)} %select_n.12), kind=kLoop, calls=%fused_computation.9 | loop fusion | bytes 1016068 | tf_op jit(solution)/shard_map/dynamic_slice | solution.py:319
  60.2 8.4 %conv.1 = (f32[882,192]{1,0:T(8,128)}, f32[192,896]{1,0:T(8,128)S(1)}) custom-call(s32[1]{0:T(128)} %bitcast.3.seq, s32[64]{0:T(128)S(1)} %copy-done.4, s32[64]{0:T(128)S(1)} %copy-done.5, bf16[3,21,21,192]{3,2,1,0:T(8,128)(2,1)S(1)} %constant_dynamic-slice_fusion.slots, bf16[21,21,192]{2,1,0:T(8,128)(2,1)S(1)} %collective-permute-done.before, ...), custom_call_target="tpu_custom_call" | custom-call | tf_op jit(solution)/shard_map/conv/pallas_call | solution.py:129
  68.7 27.0 %all-gather.2 = f16[1536,896]{1,0:T(8,128)(2,1)S(1)} all-gather(f16[192,896]{1,0:T(8,128)(2,1)S(1)} %convert_element_type.19), channel_id=1, replica_groups=mesh['y'=4,'z'=16,'x'=4,'core'=2] {'x','core'}, dimensions={0}, use_global_device_ids=true | all-gather | bytes 3096576 | tf_op jit(solution)/shard_map/all_gather | solution.py:329
  96.4 2.4 %norm.1.normed = bf16[896,1536]{1,0:T(8,128)(2,1)S(1)} custom-call(f32[1536,896]{1,0:T(8,128)S(1)} %convert_element_type.20.conv, bf16[1536]{0:T(1024)(128)(2,1)S(1)} %copy-done.1, bf16[1536]{0:T(1024)(128)(2,1)S(1)} %copy-done.2), custom_call_target="tpu_custom_call" | custom-call | tf_op jit(solution)/shard_map/norm/pallas_call | solution.py:174
  98.8 5.3 %up_and_down.1 = (bf16[896,768]{1,0:T(8,128)(2,1)S(1)}, bf16[4,192,896]{2,1,0:T(8,128)(2,1)S(1)}) custom-call(s32[1]{0:T(128)} %bitcast.1.y_ref.y, s32[1]{0:T(128)} %bitcast.2.core_ref.core, bf16[896,1536]{1,0:T(8,128)(2,1)S(1)} %norm.1.normed, bf16[768]{0:T(1024)(128)(2,1)S(1)} %copy-done.3, bf16[2,384,768]{2,1,0:T(8,128)(2,1)S(1)} %multiply_convert_fusion.refs_0_, ...), custom_call_target="tpu_custom_call" | custom-call | tf_op jit(solution)/shard_map/up_and_down/pallas_call | solution.py:270
  104.1 2.1 %collective-permute-start.5 = (bf16[4,192,896]{2,1,0:T(8,128)(2,1)S(1)}, bf16[4,192,896]{2,1,0:T(8,128)(2,1)S(1)}, u32[]{:S(2)}, u32[]{:S(2)}) collective-permute-start(bf16[4,192,896]{2,1,0:T(8,128)(2,1)S(1)} %get-tuple-element.15), channel_id=1, source_target_pairs={{0,1},{1,0},{2,3},{3,2},{4,5},{5,4},{6,7},{7,6},{8,9},{9,8},{10,11... | collective-permute-start | bytes 4128776 | tf_op jit(solution)/shard_map/ppermute | solution.py:18
  106.1 2.6 %down_own.1.mine = bf16[4,192,896]{2,1,0:T(8,128)(2,1)S(1)} custom-call(s32[1]{0:T(128)} %bitcast.1.y_ref.y, s32[1]{0:T(128)} %bitcast.2.core_ref.core, bf16[896,768]{1,0:T(8,128)(2,1)S(1)} %get-tuple-element.14.hidden, bf16[2,384,768]{2,1,0:T(8,128)(2,1)S(1)} %multiply_convert_fusion.refs_0_, bf16[2,384,768]{2,1,0:T(8,128)(2,1)S(1)} %collective-permute-done.2.refs_1_, ...), custom_call_target="tpu_custom_call" | custom-call | tf_op jit(solution)/shard_map/down_own/pallas_call | solution.py:285
  109.1 1.1 pair.1
  110.2 3.1 %collective-permute-start.6 = (bf16[192,896]{1,0:T(8,128)(2,1)}, bf16[192,896]{1,0:T(8,128)(2,1)S(1)}, u32[]{:S(2)}, u32[]{:S(2)}) collective-permute-start(bf16[192,896]{1,0:T(8,128)(2,1)} %get-tuple-element.17), channel_id=1, source_target_pairs={{0,4},{2,6},{4,0},{6,2},{1,5},{3,7},{5,1},{7,3},{8,12},{10,14},{12... | collective-permute-start | bytes 1032200 | tf_op jit(solution)/shard_map/ppermute | solution.py:18
  113.3 2.1 %collective-permute-start.7 = (bf16[192,896]{1,0:T(8,128)(2,1)}, bf16[192,896]{1,0:T(8,128)(2,1)S(1)}, u32[]{:S(2)}, u32[]{:S(2)}) collective-permute-start(bf16[192,896]{1,0:T(8,128)(2,1)} %get-tuple-element.18), channel_id=1, source_target_pairs={{0,2},{2,4},{4,6},{6,0},{1,3},{3,5},{5,7},{7,1},{8,10},{10,12},{12... | collective-permute-start | bytes 1032200 | tf_op jit(solution)/shard_map/ppermute | solution.py:18
  115.4 4.3 %collective-permute-start.8 = (bf16[192,896]{1,0:T(8,128)(2,1)S(1)}, bf16[192,896]{1,0:T(8,128)(2,1)S(1)}, u32[]{:S(2)}, u32[]{:S(2)}) collective-permute-start(bf16[192,896]{1,0:T(8,128)(2,1)S(1)} %get-tuple-element.19), channel_id=1, source_target_pairs={{0,6},{2,0},{4,2},{6,4},{1,7},{3,1},{5,3},{7,5},{8,14},{10,8},{12,... | collective-permute-start | bytes 1032200 | tf_op jit(solution)/shard_map/ppermute | solution.py:18
  120.1 3.3 %collective-permute-done.6.first = bf16[192,896]{1,0:T(8,128)(2,1)S(1)} collective-permute-done((bf16[192,896]{1,0:T(8,128)(2,1)}, bf16[192,896]{1,0:T(8,128)(2,1)S(1)}, u32[]{:S(2)}, u32[]{:S(2)}) %collective-permute-start.6) | collective-permute-done | bytes 344096 | tf_op jit(solution)/shard_map/ppermute | solution.py:18
  123.3 7.8 %collective-permute-done.7.second = bf16[192,896]{1,0:T(8,128)(2,1)S(1)} collective-permute-done((bf16[192,896]{1,0:T(8,128)(2,1)}, bf16[192,896]{1,0:T(8,128)(2,1)S(1)}, u32[]{:S(2)}, u32[]{:S(2)}) %collective-permute-start.7) | collective-permute-done | bytes 344096 | tf_op jit(solution)/shard_map/ppermute | solution.py:18
  131.8 1.1 copy.17
  (34 shorter events, 2.9 us)
Async XLA Ops:
  36.8 9.6 %copy-start.4 = (s32[64]{0:T(128)S(1)}, s32[64]{0:T(128)}, u32[]{:S(2)}) copy-start(s32[64]{0:T(128)} %first_crop.1) | copy-start | bytes 772
  36.8 20.8 %copy-start.6 = (bf16[3,1536]{1,0:T(4,128)(2,1)S(1)}, bf16[3,1536]{1,0:T(4,128)(2,1)}, u32[]{:S(2)}) copy-start(bf16[3,1536]{1,0:T(4,128)(2,1)} %param.16) | copy-start | bytes 27652
  37.0 61.7 %collective-permute-start.2 = (bf16[2,384,768]{2,1,0:T(8,128)(2,1)S(1)}, bf16[2,384,768]{2,1,0:T(8,128)(2,1)S(1)}, u32[]{:S(2)}, u32[]{:S(2)}) collective-permute-start(bf16[2,384,768]{2,1,0:T(8,128)(2,1)S(1)} %multiply_convert_fusion.refs_0_), channel_id=1, source_target_pairs={{0,256},{128,384},{256,0},{384,128},{1,257},{129,385},{257,1},{385... | collective-permute-start | bytes 3538952 | tf_op jit(solution)/shard_map/ppermute | solution.py:18
  39.9 58.8 %collective-permute-start.3 = (bf16[2,384,768]{2,1,0:T(8,128)(2,1)S(1)}, bf16[2,384,768]{2,1,0:T(8,128)(2,1)S(1)}, u32[]{:S(2)}, u32[]{:S(2)}) collective-permute-start(bf16[2,384,768]{2,1,0:T(8,128)(2,1)S(1)} %multiply_convert_fusion.refs_0_), channel_id=1, source_target_pairs={{0,384},{128,0},{256,128},{384,256},{1,385},{129,1},{257,129},{385... | collective-permute-start | bytes 3538952 | tf_op jit(solution)/shard_map/ppermute | solution.py:18
  41.8 56.9 %collective-permute-start.4 = (bf16[2,384,768]{2,1,0:T(8,128)(2,1)S(1)}, bf16[2,384,768]{2,1,0:T(8,128)(2,1)}, u32[]{:S(2)}, u32[]{:S(2)}) collective-permute-start(bf16[2,384,768]{2,1,0:T(8,128)(2,1)S(1)} %multiply_convert_fusion.refs_0_), channel_id=1, source_target_pairs={{0,128},{128,256},{256,384},{384,0},{1,129},{129,257},{257,385},{3... | collective-permute-start | bytes 3538952 | tf_op jit(solution)/shard_map/ppermute | solution.py:18
  48.2 12.1 %copy-start.5 = (s32[64]{0:T(128)S(1)}, s32[64]{0:T(128)}, u32[]{:S(2)}) copy-start(s32[64]{0:T(128)} %crop_counts.1) | copy-start | bytes 772
  49.5 10.6 %collective-permute-start = (bf16[21,21,192]{2,1,0:T(8,128)(2,1)S(1)}, bf16[21,21,192]{2,1,0:T(8,128)(2,1)S(1)}, u32[]{:S(2)}, u32[]{:S(2)}) collective-permute-start(bf16[21,21,192]{2,1,0:T(8,128)(2,1)S(1)} %get-tuple-element.22), channel_id=1, source_target_pairs={{0,8},{8,16},{16,24},{24,32},{32,40},{40,48},{48,56},{56,64},{64,7... | collective-permute-start | bytes 508040 | tf_op jit(solution)/shard_map/ppermute | solution.py:42
  51.5 8.8 %collective-permute-start.1 = (bf16[21,21,192]{2,1,0:T(8,128)(2,1)S(1)}, bf16[21,21,192]{2,1,0:T(8,128)(2,1)S(1)}, u32[]{:S(2)}, u32[]{:S(2)}) collective-permute-start(bf16[21,21,192]{2,1,0:T(8,128)(2,1)S(1)} %get-tuple-element.21), channel_id=1, source_target_pairs={{8,0},{16,8},{24,16},{32,24},{40,32},{48,40},{56,48},{64,56},{72,6... | collective-permute-start | bytes 508040 | tf_op jit(solution)/shard_map/ppermute | solution.py:45
  95.7 0.7 copy-start.1
  95.7 0.7 copy-start.2
  96.4 2.4 %copy-start.3 = (bf16[768]{0:T(1024)(128)(2,1)S(1)}, bf16[768]{0:T(1024)(128)(2,1)}, u32[]{:S(2)}) copy-start(bf16[768]{0:T(1024)(128)(2,1)} %b_up.1) | copy-start | bytes 4612
  104.1 5.0 %collective-permute-start.5 = (bf16[4,192,896]{2,1,0:T(8,128)(2,1)S(1)}, bf16[4,192,896]{2,1,0:T(8,128)(2,1)S(1)}, u32[]{:S(2)}, u32[]{:S(2)}) collective-permute-start(bf16[4,192,896]{2,1,0:T(8,128)(2,1)S(1)} %get-tuple-element.15), channel_id=1, source_target_pairs={{0,1},{1,0},{2,3},{3,2},{4,5},{5,4},{6,7},{7,6},{8,9},{9,8},{10,11... | collective-permute-start | bytes 4128776 | tf_op jit(solution)/shard_map/ppermute | solution.py:18
  109.1 10.7 %copy-start.8 = (bf16[192]{0:T(256)(128)(2,1)S(1)}, bf16[192]{0:T(256)(128)(2,1)}, u32[]{:S(2)}) copy-start(bf16[192]{0:T(256)(128)(2,1)} %param.24) | copy-start | bytes 1156
  109.1 10.8 %copy-start.7 = (f32[192]{0:T(256)S(1)}, f32[192]{0:T(256)}, u32[]{:S(2)}) copy-start(f32[192]{0:T(256)} %param.25) | copy-start | bytes 2308
  109.1 22.0 %copy-start = (f32[882,192]{1,0:T(8,128)S(1)}, f32[882,192]{1,0:T(8,128)}, u32[]{:S(2)}) copy-start(f32[882,192]{1,0:T(8,128)} %get-tuple-element.20.residual) | copy-start | bytes 2032132
  110.2 13.1 %collective-permute-start.6 = (bf16[192,896]{1,0:T(8,128)(2,1)}, bf16[192,896]{1,0:T(8,128)(2,1)S(1)}, u32[]{:S(2)}, u32[]{:S(2)}) collective-permute-start(bf16[192,896]{1,0:T(8,128)(2,1)} %get-tuple-element.17), channel_id=1, source_target_pairs={{0,4},{2,6},{4,0},{6,2},{1,5},{3,7},{5,1},{7,3},{8,12},{10,14},{12... | collective-permute-start | bytes 1032200 | tf_op jit(solution)/shard_map/ppermute | solution.py:18
  113.3 17.9 %collective-permute-start.7 = (bf16[192,896]{1,0:T(8,128)(2,1)}, bf16[192,896]{1,0:T(8,128)(2,1)S(1)}, u32[]{:S(2)}, u32[]{:S(2)}) collective-permute-start(bf16[192,896]{1,0:T(8,128)(2,1)} %get-tuple-element.18), channel_id=1, source_target_pairs={{0,2},{2,4},{4,6},{6,0},{1,3},{3,5},{5,7},{7,1},{8,10},{10,12},{12... | collective-permute-start | bytes 1032200 | tf_op jit(solution)/shard_map/ppermute | solution.py:18
  115.4 15.7 %collective-permute-start.8 = (bf16[192,896]{1,0:T(8,128)(2,1)S(1)}, bf16[192,896]{1,0:T(8,128)(2,1)S(1)}, u32[]{:S(2)}, u32[]{:S(2)}) collective-permute-start(bf16[192,896]{1,0:T(8,128)(2,1)S(1)} %get-tuple-element.19), channel_id=1, source_target_pairs={{0,6},{2,0},{4,2},{6,4},{1,7},{3,1},{5,3},{7,5},{8,14},{10,8},{12,... | collective-permute-start | bytes 1032200 | tf_op jit(solution)/shard_map/ppermute | solution.py:18
